TPU v7x, 32 devices: a whole 2x2x4 slice. The times are simulated.
32 devices in a mesh: groups: 2 (over x), tm: 8 (over z, y), tensor: 2 (over core).
Axes of the slice: x: 2, y: 2, z: 4, core: 2. Of those that a mesh axis runs over, the one named last changes fastest.
Arguments:
- frames_in: bfloat16 [4096, 6144], P(('groups', 'tm', 'tensor')), parts along dimension 0, may hold values from -6 to 6
- cotangent: bfloat16 [4096, 6144], P(('groups', 'tm', 'tensor')), parts along dimension 0, may hold values from -6 to 6
- down_weight: bfloat16 [6144, 384], P('tensor'), may hold values from -0.078125 to 0.078125
- down_bias: float32 [384], replicated, may hold values from -4 to 4
- conv_kernel: float32 [3, 384], replicated, may hold values from -3 to 3
- up_weight: bfloat16 [6144, 384], P('tensor'), may hold values from -0.3125 to 0.3125
- up_bias: float32 [6144], replicated, may hold values from -3 to 3
- ln_gain: float32 [6144], replicated, may hold values from 0.5 to 1.5
Outputs:
- out_tokens: bfloat16 [4096, 6144], P(('groups', 'tm', 'tensor')), parts along dimension 0
- grad_down: float32 [12288, 384], P(('groups', 'tm', 'tensor')), parts along dimension 0
- grad_up: float32 [12288, 384], P(('groups', 'tm', 'tensor')), parts along dimension 0
- grad_up_bias: float32 [12288], P(('groups', 'tm', 'tensor')), parts along dimension 0
- grad_down_bias: float32 [768], P('groups'), parts along dimension 0
- grad_kernel: float32 [6, 384], P('groups'), parts along dimension 0
There are 2 independent parts, one for each index of `groups`. A program takes and returns all parts, laid end to end along the dimension named above; an argument that names none is the same for every part. Nothing has to cross between parts.
All inputs are finite; a program needn't handle non-finite values.
Results may differ from a plain program's by a relative error of at most 0.0085.
Values may be sent and summed in bfloat16 or wider, within the bound.
No kernel may reach another device: no remote copies, remote signals or barrier semaphores. Data moves between devices by JAX's collectives and lax.ppermute only.
A program may use at most 128 MiB of HBM per device.

v0:
```python
import jax
import jax.numpy as jnp
from jax import lax
from jax.sharding import PartitionSpec as P

epsilon = 1e-06


def extended(block, sides, width):
    for axis, dim in sides:
        count = lax.axis_size(axis)
        forward = [(i, i + 1) for i in range(count - 1)]
        backward = [(target, source) for source, target in forward]
        low = lax.ppermute(
            lax.slice_in_dim(block, block.shape[dim] - width, None, axis=dim), axis, forward
        )
        high = lax.ppermute(lax.slice_in_dim(block, 0, width, axis=dim), axis, backward)
        block = jnp.concatenate([low, block, high], axis=dim)
    return block


def norm_forward(lifted, ln_gain):
    lifted_wide = lifted.astype(jnp.float32)
    center = jnp.mean(lifted_wide, axis=-1, keepdims=True)
    shifted = lifted_wide - center
    spread = jnp.mean(shifted * shifted, axis=-1, keepdims=True)
    inverse = lax.rsqrt(spread + epsilon)
    unit = shifted * inverse
    return (unit, inverse, (unit * ln_gain).astype(jnp.bfloat16))


def norm_backward(grad_normed, unit, inverse, ln_gain):
    scaled = grad_normed * ln_gain
    return inverse * (
        scaled
        - jnp.mean(scaled, axis=-1, keepdims=True)
        - unit * jnp.mean(scaled * unit, axis=-1, keepdims=True)
    )


def inner_rows(left, right):
    return lax.dot_general(
        left, right, (((0,), (0,)), ((), ())), preferred_element_type=jnp.float32
    )


def outer_rows(left, right):
    return lax.dot_general(
        left, right, (((1,), (1,)), ((), ())), preferred_element_type=jnp.float32
    )


def local(frames_in, cotangent, down_weight, down_bias, conv_kernel, up_weight, up_bias, ln_gain):
    tok_rows = frames_in.shape[0]
    down_full, up_full = (
        lax.all_gather(down_weight, "tensor", axis=0, tiled=True),
        lax.all_gather(up_weight, "tensor", axis=0, tiled=True),
    )
    bottle = (jnp.dot(frames_in, down_full, preferred_element_type=jnp.float32) + down_bias).astype(
        jnp.bfloat16
    )
    bottle_width = bottle.shape[1]
    padded = extended(bottle.reshape(1, tok_rows, bottle_width), (("tm", 0),), 1).astype(
        jnp.float32
    )
    conv = (
        conv_kernel[0] * padded[0] + conv_kernel[1] * padded[1] + conv_kernel[2] * padded[2]
    ).astype(jnp.bfloat16)
    lifted = (frames_in.astype(jnp.float32) + outer_rows(conv, up_full) + up_bias).astype(
        jnp.bfloat16
    )
    unit, inverse, out_tokens = norm_forward(lifted, ln_gain)
    grad_lifted = norm_backward(cotangent.astype(jnp.float32), unit, inverse, ln_gain).astype(
        jnp.bfloat16
    )
    grad_conv = jnp.dot(grad_lifted, up_full, preferred_element_type=jnp.float32).astype(
        jnp.bfloat16
    )
    grad_padded = extended(grad_conv.reshape(1, tok_rows, bottle_width), (("tm", 0),), 1).astype(
        jnp.float32
    )
    grad_bottle = (
        conv_kernel[0] * grad_padded[2]
        + conv_kernel[1] * grad_padded[1]
        + conv_kernel[2] * grad_padded[0]
    ).astype(jnp.bfloat16)
    own_grad = grad_padded[1]
    kernel_terms = jnp.stack(
        [
            jnp.sum(padded[0] * own_grad, axis=0),
            jnp.sum(padded[1] * own_grad, axis=0),
            jnp.sum(padded[2] * own_grad, axis=0),
        ],
        axis=0,
    )
    bottle_terms = jnp.sum(grad_bottle.astype(jnp.float32), axis=0)
    summed = lax.psum_scatter(
        jnp.concatenate(
            [inner_rows(grad_lifted, conv), inner_rows(frames_in, grad_bottle)], axis=1
        ),
        ("tm", "tensor"),
        scatter_dimension=0,
        tiled=True,
    )
    grad_up = summed[:, :bottle_width]
    grad_down = summed[:, bottle_width:]
    grad_up_bias = lax.psum_scatter(
        jnp.sum(grad_lifted.astype(jnp.float32), axis=0),
        ("tm", "tensor"),
        scatter_dimension=0,
        tiled=True,
    )
    grad_down_bias, grad_kernel = lax.psum((bottle_terms, kernel_terms), ("tm", "tensor"))
    return (out_tokens, grad_down, grad_up, grad_up_bias, grad_down_bias, grad_kernel)


def solution(mesh):
    return jax.shard_map(
        local,
        mesh=mesh,
        in_specs=(
            P(("groups", "tm", "tensor"), None),
            P(("groups", "tm", "tensor"), None),
            P("tensor", None),
            P(),
            P(),
            P("tensor", None),
            P(),
            P(),
        ),
        out_specs=(
            P(("groups", "tm", "tensor"), None),
            P(("groups", "tm", "tensor"), None),
            P(("groups", "tm", "tensor"), None),
            P(("groups", "tm", "tensor")),
            P("groups"),
            P("groups", None),
        ),
        check_vma=False,
    )
```

profile of v0, /device:TPU:0, one launch (start us, length us, event | category | flops | bytes accessed | tf_op | source)
XLA Modules:
  0.0 278.7 jit_solution(13120542412489386828)
XLA Ops:
  7.2 0.0 copy-start
  7.2 0.0 copy-start.5
  7.2 0.0 all-gather.3.cloned.1.call-start
  7.2 0.7 all-gather.3.cloned.1.call-update
  7.9 0.0 all-gather.5.cloned.1.call-start
  8.0 0.7 all-gather.5.cloned.1.call-update
  8.7 0.0 copy-start.4
  8.7 0.0 copy-start.3
  8.7 0.0 reduce-scatter.2.cloned.1.call-start
  8.7 18.0 %all-gather.3.cloned.1.call-done = bf16[6144,384]{1,0:T(8,128)(2,1)} async-done(((bf16[3072,384]{1,0:T(8,128)(2,1)}), bf16[6144,384]{1,0:T(8,128)(2,1)}) %all-gather.3.cloned.1.call-update) | async-done | bytes 4718608 | tf_op jit(solution)/shard_map/all_gather | solution.py:56
  26.7 0.0 copy-done
  26.7 0.0 copy-done.5
  26.7 3.3 %fusion.6 = bf16[1,128,384]{2,1,0:T(8,128)(2,1)S(1)} fusion(bf16[128,6144]{1,0:T(8,128)(2,1)S(1)} %copy-done, bf16[6144,384]{1,0:T(8,128)(2,1)} %all-gather.3.cloned.1.call-done, f32[384]{0:T(512)S(1)} %copy-done.5), kind=kOutput, calls=%fused_computation.18 | convolution fusion | flops 604078080 | bytes 6391296 | tf_op jit(solution)/shard_map/dot_general | solution.py:59
  30.1 1.3 collective-permute-start.1
  31.4 4.6 %collective-permute-start = (bf16[1,128,384]{2,1,0:T(8,128)(2,1)S(1)}, bf16[1,128,384]{2,1,0:T(8,128)(2,1)S(1)}, u32[]{:S(2)}, u32[]{:S(2)}) collective-permute-start(bf16[1,128,384]{2,1,0:T(8,128)(2,1)S(1)} %fusion.6), channel_id=1, source_target_pairs={{0,2},{2,4},{4,6},{6,8},{8,10},{10,12},{12,14},{1,3},{3,5},{5,7},{... | collective-permute-start | bytes 294920 | tf_op jit(solution)/shard_map/ppermute | solution.py:14
  35.9 0.0 copy-done.4
  36.0 1.0 collective-permute-done.1
  37.0 2.3 collective-permute-done
  39.3 4.6 %all-gather.5.cloned.1.call-done = bf16[6144,384]{1,0:T(8,128)(2,1)} async-done(((bf16[3072,384]{1,0:T(8,128)(2,1)}), bf16[6144,384]{1,0:T(8,128)(2,1)}) %all-gather.5.cloned.1.call-update) | async-done | bytes 4718608 | tf_op jit(solution)/shard_map/all_gather | solution.py:57
  43.9 0.0 copy-done.3
  43.9 4.0 %fusion.14 = (f32[128]{0:T(128)S(1)}, f32[128,6144]{1,0:T(8,128)S(1)}) fusion(f32[6144]{0:T(1024)S(1)} %copy-done.3, bf16[128,384]{1,0:T(8,128)(2,1)S(1)} %add_convert_fusion, bf16[6144,384]{1,0:T(8,128)(2,1)} %all-gather.5.cloned.1.call-done, bf16[128,6144]{1,0:T(8,128)(2,1)S(1)} %copy-done), kind=kOutput, calls=%fused_computation.46 | convolution fusion | flops 608698240 | bytes 9560576 | tf_op jit(solution)/shard_map/dot_general | solution.py:48
  47.9 0.0 copy-start.1
  47.9 0.0 copy-start.2
  48.0 0.5 multiply_reduce_fusion.1
  48.4 0.9 copy-done.1
  49.4 0.0 copy-done.2
  49.4 0.0 slice-start
  49.4 1.0 fusion.3
  50.4 0.0 slice-start.1
  50.4 2.6 convert_reduce_fusion
  53.0 0.0 slice-done
  53.0 0.0 slice-done.1
  53.0 1.0 fusion.5
  54.0 1.3 collective-permute-start.3
  55.3 4.6 %collective-permute-start.2 = (bf16[1,128,384]{2,1,0:T(8,128)(2,1)S(1)}, bf16[1,128,384]{2,1,0:T(8,128)(2,1)S(1)}, u32[]{:S(2)}, u32[]{:S(2)}) collective-permute-start(bf16[1,128,384]{2,1,0:T(8,128)(2,1)S(1)} %fusion.5), channel_id=1, source_target_pairs={{0,2},{2,4},{4,6},{6,8},{8,10},{10,12},{12,14},{1,3},{3,5},{5,7},{... | collective-permute-start | bytes 294920 | tf_op jit(solution)/shard_map/ppermute | solution.py:14
  59.9 1.4 fusion.15
  61.3 0.0 collective-permute-done.3
  61.3 1.9 collective-permute-done.2
  63.2 0.1 multiply_reduce_fusion.4
  63.3 1.4 convolution_bitcast_fusion
  64.7 6.9 %pad_maximum_fusion = f32[6144,768]{0,1:T(8,128)} fusion(f32[6144,384]{0,1:T(8,128)S(1)} %convolution_bitcast_fusion, f32[6144,384]{0,1:T(8,128)S(1)} %fusion.15), kind=kLoop, calls=%fused_computation | loop fusion | flops 4718592 | bytes 37748736 | tf_op jit(solution)/shard_map/concatenate | solution.py:98
  71.6 0.0 copy-start.6
  71.6 0.0 reduce-scatter.2.cloned.1.call-update
  71.7 0.6 copy-done.6
  72.3 0.6 dynamic-slice
  73.6 62.7 %all-reduce.1 = (f32[6144]{0:T(1024)S(1)}, f32[384]{0:T(512)}, f32[3,384]{1,0:T(4,128)}) all-reduce(f32[6144]{0:T(1024)S(1)} %get-tuple-element.31, f32[384]{0:T(512)S(1)} %get-tuple-element.36, f32[3,384]{1,0:T(4,128)S(1)} %pad_maximum_fusion.1), channel_id=3, replica_groups=mesh['groups'=2,'tm'=8,'tensor'=2] {'tm','tensor'}, use_global_device_ids=true, to_apply=%region_6.0.clone | all-reduce | flops 7680 | bytes 61440
  136.3 0.7 dynamic-slice.1
  136.9 131.8 %reduce-scatter.2.cloned.1.call-done = f32[384,768]{0,1:T(8,128)} async-done(((f32[6144,768]{0,1:T(8,128)}), f32[384,768]{0,1:T(8,128)}) %reduce-scatter.2.cloned.1.call-update) | async-done | bytes 1179664 | tf_op jit(solution)/shard_map/reduce_scatter | solution.py:97
  268.7 1.3 fusion.13
  270.1 1.1 copy.17
  271.1 1.0 copy.16
  (12 shorter events, 0.2 us)
Async XLA Ops:
  7.2 19.6 %copy-start = (bf16[128,6144]{1,0:T(8,128)(2,1)S(1)}, bf16[128,6144]{1,0:T(8,128)(2,1)}, u32[]{:S(2)}) copy-start(bf16[128,6144]{1,0:T(8,128)(2,1)} %param.8) | copy-start | bytes 4718596
  7.2 19.6 %copy-start.5 = (f32[384]{0:T(512)S(1)}, f32[384]{0:T(512)}, u32[]{:S(2)}) copy-start(f32[384]{0:T(512)} %param.11) | copy-start | bytes 4612
  7.2 19.6 %all-gather.3.cloned.1.call-start = ((), (), s32[]{:S(2)}) async-start(), calls=%async_computation.1 | async-start | bytes 7077888 | tf_op jit(solution)/shard_map/all_gather | solution.py:56
  7.9 36.0 %all-gather.5.cloned.1.call-start = ((), (), s32[]{:S(2)}) async-start(), calls=%async_computation.2 | async-start | bytes 7077888 | tf_op jit(solution)/shard_map/all_gather | solution.py:57
  8.7 27.3 %copy-start.4 = (f32[3,384]{1,0:T(4,128)S(1)}, f32[3,384]{1,0:T(4,128)}, u32[]{:S(2)}) copy-start(f32[3,384]{1,0:T(4,128)} %param.12) | copy-start | bytes 13828
  8.7 35.2 %copy-start.3 = (f32[6144]{0:T(1024)S(1)}, f32[6144]{0:T(1024)}, u32[]{:S(2)}) copy-start(f32[6144]{0:T(1024)} %param.14) | copy-start | bytes 73732
  8.7 260.0 %reduce-scatter.2.cloned.1.call-start = ((), (), s32[]{:S(2)}) async-start(), calls=%async_computation.3 | async-start | bytes 20054016 | tf_op jit(solution)/shard_map/reduce_scatter | solution.py:97
  30.1 6.9 %collective-permute-start.1 = (bf16[1,128,384]{2,1,0:T(8,128)(2,1)S(1)}, bf16[1,128,384]{2,1,0:T(8,128)(2,1)S(1)}, u32[]{:S(2)}, u32[]{:S(2)}) collective-permute-start(bf16[1,128,384]{2,1,0:T(8,128)(2,1)S(1)} %fusion.6), channel_id=1, source_target_pairs={{2,0},{4,2},{6,4},{8,6},{10,8},{12,10},{14,12},{3,1},{5,3},{7,5},{... | collective-permute-start | bytes 294920 | tf_op jit(solution)/shard_map/ppermute | solution.py:17
  31.4 7.8 %collective-permute-start = (bf16[1,128,384]{2,1,0:T(8,128)(2,1)S(1)}, bf16[1,128,384]{2,1,0:T(8,128)(2,1)S(1)}, u32[]{:S(2)}, u32[]{:S(2)}) collective-permute-start(bf16[1,128,384]{2,1,0:T(8,128)(2,1)S(1)} %fusion.6), channel_id=1, source_target_pairs={{0,2},{2,4},{4,6},{6,8},{8,10},{10,12},{12,14},{1,3},{3,5},{5,7},{... | collective-permute-start | bytes 294920 | tf_op jit(solution)/shard_map/ppermute | solution.py:14
  47.9 1.4 copy-start.1
  47.9 1.4 copy-start.2
  49.4 3.7 %slice-start = ((s8[4718592]{0:T(1024)(128)(4,1)}), s8[4194304]{0:T(1024)(128)(4,1)S(1)}, s32[]{:S(2)}) async-start(s8[4718592]{0:T(1024)(128)(4,1)} %bitcast.64), calls=%async_computation.4 | async-start | bytes 8388608
  50.4 2.6 slice-start.1
  54.0 7.3 %collective-permute-start.3 = (bf16[1,128,384]{2,1,0:T(8,128)(2,1)S(1)}, bf16[1,128,384]{2,1,0:T(8,128)(2,1)S(1)}, u32[]{:S(2)}, u32[]{:S(2)}) collective-permute-start(bf16[1,128,384]{2,1,0:T(8,128)(2,1)S(1)} %fusion.5), channel_id=1, source_target_pairs={{2,0},{4,2},{6,4},{8,6},{10,8},{12,10},{14,12},{3,1},{5,3},{7,5},{... | collective-permute-start | bytes 294920 | tf_op jit(solution)/shard_map/ppermute | solution.py:17
  55.3 7.9 %collective-permute-start.2 = (bf16[1,128,384]{2,1,0:T(8,128)(2,1)S(1)}, bf16[1,128,384]{2,1,0:T(8,128)(2,1)S(1)}, u32[]{:S(2)}, u32[]{:S(2)}) collective-permute-start(bf16[1,128,384]{2,1,0:T(8,128)(2,1)S(1)} %fusion.5), channel_id=1, source_target_pairs={{0,2},{2,4},{4,6},{6,8},{8,10},{10,12},{12,14},{1,3},{3,5},{5,7},{... | collective-permute-start | bytes 294920 | tf_op jit(solution)/shard_map/ppermute | solution.py:14
  71.6 0.7 copy-start.6
Sparse Core Ops, SparseCore 0:
  9.6 17.1 all-gather.2
  28.3 15.5 all-gather.4
  71.8 196.9 reduce-scatter.1
where the time goes:
time: 279 us
  waiting for transfers between devices  161 us (58%)
  blocking collectives  62.7 us (22%)
  between operations  14.6 us (5%)
  starting transfers between devices  11.8 us (4%)
  other arithmetic  11.3 us (4%)
  matrix products  11.2 us (4%)
  local copies, waits for them, and re-layouts  6.25 us (2%)
    reduce_scatter x1, waiting for transfers between devices, local(): lax.psum_scatter(jnp.concatenate([inner_rows(grad_lifted, conv), inner_ro...  132 us
    unnamed x1, blocking collectives  62.7 us
    all_gather x1, waiting for transfers between devices, local(): lax.all_gather(down_weight, 'tensor', axis=0, tiled=True)  18 us
    ppermute x2, starting transfers between devices, extended(): lax.ppermute(lax.slice_in_dim(block, block.shape[dim] - width, None, axis...  9.1 us
    concatenate x1, other arithmetic, local(): jnp.concatenate([inner_rows(grad_lifted, conv), inner_rows(frames_in, gra...  6.88 us
  transfers between devices with their start and end apart: 7, of which 6 were waited for; matrix products, arithmetic and copies ran while one was open for 2% of the time, Pallas kernels for 0%

commit v1 on v0

v1 whole, which is shorter than its diff:
```python
import jax
import jax.numpy as jnp
from jax import lax
from jax.sharding import PartitionSpec as P

epsilon = 1e-06
cores = 2
block_frames = 4
narrow, wide = jnp.bfloat16, jnp.float32


def norm_forward(lifted, ln_gain):
    lifted_wide = lifted.astype(wide)
    center = jnp.mean(lifted_wide, axis=-1, keepdims=True)
    shifted = lifted_wide - center
    spread = jnp.mean(shifted * shifted, axis=-1, keepdims=True)
    inverse = lax.rsqrt(spread + epsilon)
    unit = shifted * inverse
    return (unit, inverse, (unit * ln_gain).astype(narrow))


def norm_backward(grad_normed, unit, inverse, ln_gain):
    scaled = grad_normed * ln_gain
    return inverse * (
        scaled
        - jnp.mean(scaled, axis=-1, keepdims=True)
        - unit * jnp.mean(scaled * unit, axis=-1, keepdims=True)
    )


def inner_rows(left, right):
    return lax.dot_general(
        left, right, (((0,), (0,)), ((), ())), preferred_element_type=wide
    )


def outer_rows(left, right):
    return lax.dot_general(
        left, right, (((1,), (1,)), ((), ())), preferred_element_type=wide
    )


def high_low(values):
    high = values.astype(narrow)
    return jnp.concatenate([high, (values - high.astype(wide)).astype(narrow)], axis=0)


def local(frames_in, cotangent, down_weight, down_bias, conv_kernel, up_weight, up_bias, ln_gain):
    tokens, features = frames_in.shape
    channels = down_weight.shape[1]
    count = lax.axis_size("tm")
    blocks = count // block_frames
    share = features // (count * cores)
    frame, core = lax.axis_index("tm"), lax.axis_index("tensor")
    block, place = frame // block_frames, frame % block_frames

    def core_swap(value):
        return lax.ppermute(value, "tensor", [(0, 1), (1, 0)])

    def block_swap(value, step):
        return lax.ppermute(value, "tm", [(i, i ^ step) for i in range(count)])

    def neighbours(value):
        earlier = lax.ppermute(value, "tm", [(i, i + 1) for i in range(count - 1)])
        later = lax.ppermute(value, "tm", [(i + 1, i) for i in range(count - 1)])
        return earlier, later

    def columns_for(value, step):
        return [
            lax.dynamic_slice_in_dim(
                value,
                ((piece * block_frames + (place ^ step)) * cores) * share,
                cores * share,
                axis=1,
            )
            for piece in range(blocks)
        ]

    def exchange(value):
        parts = [jnp.concatenate(columns_for(value, step), axis=0) for step in range(block_frames)]
        parts = [parts[0]] + [block_swap(parts[step], step) for step in range(1, block_frames)]
        kept = [lax.dynamic_slice_in_dim(p, core * share, share, axis=1) for p in parts]
        sent = [lax.dynamic_slice_in_dim(p, (1 - core) * share, share, axis=1) for p in parts]
        got = core_swap(jnp.concatenate(sent, axis=0))
        kept = jnp.concatenate(kept, axis=0)
        return [v.reshape(block_frames, blocks, tokens, share) for v in (kept, got)]

    def gather(value):
        rows = value.shape[0]
        own = jnp.concatenate(
            [value] + [block_swap(value, step) for step in range(1, block_frames)], axis=0
        )
        return [v.reshape(block_frames, rows, -1) for v in (own, core_swap(own))]

    def contract(pairs, rows, piece):
        total = 0.0
        for features_of, row in zip(pairs, rows):
            chosen = lax.dynamic_index_in_dim(features_of, piece, axis=1, keepdims=False)
            total = total + inner_rows(chosen.reshape(-1, share), row.reshape(-1, channels))
        return total

    down_other = core_swap(down_weight)
    half = features // cores
    bottle = (
        jnp.dot(
            lax.dynamic_slice_in_dim(frames_in, core * half, half, axis=1),
            down_weight,
            preferred_element_type=wide,
        )
        + jnp.dot(
            lax.dynamic_slice_in_dim(frames_in, (1 - core) * half, half, axis=1),
            down_other,
            preferred_element_type=wide,
        )
        + down_bias
    ).astype(narrow)
    up_other = core_swap(up_weight)
    up_full = jnp.where(
        core == 0,
        jnp.concatenate([up_weight, up_other], axis=0),
        jnp.concatenate([up_other, up_weight], axis=0),
    )
    frames_share = exchange(frames_in)
    before, after = [v.astype(wide) for v in neighbours(bottle)]
    here = bottle.astype(wide)
    conv = (conv_kernel[0] * before + conv_kernel[1] * here + conv_kernel[2] * after).astype(narrow)
    conv_rows = gather(conv)
    lifted = (frames_in.astype(wide) + outer_rows(conv, up_full) + up_bias).astype(narrow)
    unit, inverse, out_tokens = norm_forward(lifted, ln_gain)
    grad_lifted = norm_backward(cotangent.astype(wide), unit, inverse, ln_gain).astype(narrow)
    grad_conv = jnp.dot(grad_lifted, up_full, preferred_element_type=wide).astype(narrow)
    own_grad = grad_conv.astype(wide)
    grad_before, grad_after = [v.astype(wide) for v in neighbours(grad_conv)]
    grad_bottle = (
        conv_kernel[0] * grad_after + conv_kernel[1] * own_grad + conv_kernel[2] * grad_before
    ).astype(narrow)
    small = jnp.stack(
        [
            jnp.sum(before * own_grad, axis=0),
            jnp.sum(here * own_grad, axis=0),
            jnp.sum(after * own_grad, axis=0),
            jnp.sum(grad_bottle.astype(wide), axis=0),
        ],
        axis=0,
    )
    pad = jnp.zeros((8, channels), narrow)
    bottle_rows = gather(jnp.concatenate([grad_bottle, high_low(small), pad], axis=0))
    small_rows = [v[:, tokens:] for v in bottle_rows]
    bottle_rows = [v[:, :tokens] for v in bottle_rows]
    small = sum(
        jnp.sum(v[:, :4].astype(wide), axis=0) + jnp.sum(v[:, 4:8].astype(wide), axis=0)
        for v in small_rows
    )
    grad_share = exchange(grad_lifted)

    def bias_of(piece):
        total = 0.0
        for value in grad_share:
            chosen = lax.dynamic_index_in_dim(value, piece, axis=1, keepdims=False)
            total = total + jnp.sum(chosen.astype(wide), axis=(0, 1))
        return total

    def across(value, step):
        return lax.ppermute(
            value,
            "tm",
            [(i, (i + step * block_frames) % count) for i in range(count)],
        )

    grad_down = contract(frames_share, bottle_rows, block)
    grad_up = contract(grad_share, conv_rows, block)
    grad_up_bias = bias_of(block)
    own_small = small
    for step in range(1, blocks):
        target = (block + step) % blocks
        down_got = across(
            jnp.concatenate(
                [
                    contract(frames_share, bottle_rows, target).astype(narrow),
                    high_low(own_small),
                    pad,
                ],
                axis=0,
            ),
            step,
        ).astype(wide)
        up_bias_row = jnp.pad(bias_of(target), (0, channels - share))[None]
        up_got = across(
            jnp.concatenate(
                [
                    contract(grad_share, conv_rows, target).astype(narrow),
                    high_low(up_bias_row),
                    jnp.zeros((14, channels), narrow),
                ],
                axis=0,
            ),
            step,
        ).astype(wide)
        grad_down = grad_down + down_got[:share]
        small = small + down_got[share : share + 4] + down_got[share + 4 : share + 8]
        grad_up = grad_up + up_got[:share]
        grad_up_bias = grad_up_bias + (up_got[share] + up_got[share + 1])[:share]
    return (out_tokens, grad_down, grad_up, grad_up_bias, small[3], small[:3])


def solution(mesh):
    tokens = P(("groups", "tm", "tensor"), None)
    return jax.shard_map(
        local,
        mesh=mesh,
        in_specs=(tokens, tokens, P("tensor", None), P(), P(), P("tensor", None), P(), P()),
        out_specs=(
            tokens,
            tokens,
            tokens,
            P(("groups", "tm", "tensor")),
            P("groups"),
            P("groups", None),
        ),
        check_vma=False,
    )
```

time: 279 us -> 141 us (0.51)
  waiting for transfers between devices: 161 us -> 68.6 us
  blocking collectives: 62.7 us -> 0 us
  starting transfers between devices: 11.8 us -> 30.6 us
  between operations: 14.6 us -> 1.24 us
  matrix products: 11.2 us -> 19 us
  local copies, waits for them, and re-layouts: 6.25 us -> 10 us
    reduce_scatter x1 -> x0, waiting for transfers between devices: 132 us -> none  [local(): lax.psum_scatter(jnp.concatenate([inner_rows(grad_lifted, conv), inner_ro...]
    ppermute x4 -> x24, waiting for transfers between devices: 5.1 us -> 68.6 us  [the longest x12 33.7 us: block_swap(): return lax.ppermute(value, 'tm', [(i, i ^ step) for i in range(count)])]
    unnamed x1 -> x0, blocking collectives: 62.7 us -> none
    all_gather x2 -> x0, waiting for transfers between devices: 22.6 us -> none  [the longest x1 18 us: local(): lax.all_gather(down_weight, 'tensor', axis=0, tiled=True)]
    ppermute x4 -> x24, starting transfers between devices: 11.7 us -> 30.6 us  [the longest x12 16.2 us: block_swap(): return lax.ppermute(value, 'tm', [(i, i ^ step) for i in range(count)])]
    dynamic_slice x0 -> x9, local copies, waits for them, and re-layouts: none -> 6.31 us  [the longest x6 4.35 us: exchange(): lax.dynamic_slice_in_dim(p, core * share, share, axis=1)]
    dot_general x1, matrix products: 4.01 us -> 9.08 us  [outer_rows(): lax.dot_general(left, right, (((1,), (1,)), ((), ())), preferred_element_...]
    unnamed x22 -> x30, local copies, waits for them, and re-layouts: 4.89 us -> 0.97 us
  transfers between devices with their start and end apart: 7 -> 24, of which waited for: 6 -> 10; matrix products, arithmetic and copies ran while one was open for 2% -> 14% of each run, Pallas kernels for 0% -> 0%
where the time goes in v1:
time: 141 us; the launch traced here: 140 us
  waiting for transfers between devices  68.6 us (49%)
  starting transfers between devices  30.6 us (22%)
  matrix products  19 us (13%)
  other arithmetic  10.7 us (8%)
  local copies, waits for them, and re-layouts  10 us (7%)
    ppermute x12, waiting for transfers between devices, block_swap(): return lax.ppermute(value, 'tm', [(i, i ^ step) for i in range(count)])  33.7 us
    ppermute x2, waiting for transfers between devices, across(): lax.ppermute(value, 'tm', [(i, (i + step * block_frames) % count) for i i...  29.6 us
    ppermute x12, starting transfers between devices, block_swap(): return lax.ppermute(value, 'tm', [(i, i ^ step) for i in range(count)])  16.2 us
    dot_general x1, matrix products, outer_rows(): lax.dot_general(left, right, (((1,), (1,)), ((), ())), preferred_element_...  9.08 us
    ppermute x2, starting transfers between devices, neighbours(): earlier = lax.ppermute(value, 'tm', [(i, i + 1) for i in range(count - 1)])  8.86 us
    dot_general x8, matrix products, inner_rows(): lax.dot_general(left, right, (((0,), (0,)), ((), ())), preferred_element_...  4.83 us
    concatenate x8, other arithmetic, exchange(): jnp.concatenate(columns_for(value, step), axis=0)  4.71 us
    dynamic_slice x6, local copies, waits for them, and re-layouts, exchange(): lax.dynamic_slice_in_dim(p, core * share, share, axis=1)  4.35 us
  transfers between devices with their start and end apart: 24, of which 10 were waited for; matrix products, arithmetic and copies ran while one was open for 14% of the time, Pallas kernels for 0%

profile of v1, /device:TPU:0, one launch (start us, length us, event | category | flops | bytes accessed | tf_op | source)
XLA Modules:
  0.0 140.1 jit_solution(16640754956534507933)
XLA Ops:
  0.6 0.5 collective-permute-start
  1.2 1.6 %constant_dynamic-slice_fusion.34 = (bf16[128,768]{1,0:T(8,128)(2,1)S(1)}, bf16[128,768]{1,0:T(8,128)(2,1)S(1)}, bf16[128,768]{1,0:T(8,128)(2,1)S(1)}, bf16[128,...) fusion(bf16[128,6144]{1,0:T(8,128)(2,1)} %param.8, ...), kind=kLoop, calls=%fused_computation.112 | loop fusion | bytes 3145760 | tf_op jit(solution)/shard_map/dynamic_slice | solution.py:70
  2.8 0.8 pad_maximum_fusion.4
  3.6 2.9 %collective-permute-start.4 = (bf16[256,768]{1,0:T(8,128)(2,1)}, bf16[256,768]{1,0:T(8,128)(2,1)}, u32[]{:S(2)}, u32[]{:S(2)}) collective-permute-start(bf16[256,768]{1,0:T(8,128)(2,1)} %pad_maximum_fusion.4), channel_id=1, source_target_pairs={{0,2},{2,0},{4,6},{6,4},{8,10},{10,8},{12,14},{14,12},{1,3},{3,1},... | collective-permute-start | bytes 1179656 | tf_op jit(solution)/shard_map/ppermute | solution.py:61
  6.5 0.8 pad_maximum_fusion.5
  7.3 1.6 %collective-permute-start.5 = (bf16[256,768]{1,0:T(8,128)(2,1)}, bf16[256,768]{1,0:T(8,128)(2,1)S(1)}, u32[]{:S(2)}, u32[]{:S(2)}) collective-permute-start(bf16[256,768]{1,0:T(8,128)(2,1)} %pad_maximum_fusion.5), channel_id=1, source_target_pairs={{0,4},{2,6},{4,0},{6,2},{8,12},{10,14},{12,8},{14,10},{1,5},{3,7},... | collective-permute-start | bytes 1179656 | tf_op jit(solution)/shard_map/ppermute | solution.py:61
  8.9 0.8 pad_maximum_fusion.6
  9.8 6.4 %collective-permute-done.4 = bf16[256,768]{1,0:T(8,128)(2,1)} collective-permute-done((bf16[256,768]{1,0:T(8,128)(2,1)}, bf16[256,768]{1,0:T(8,128)(2,1)}, u32[]{:S(2)}, u32[]{:S(2)}) %collective-permute-start.4) | collective-permute-done | bytes 393248 | tf_op jit(solution)/shard_map/ppermute | solution.py:61
  16.2 1.1 constant_dynamic-slice_fusion.31
  17.3 2.3 %collective-permute-done.5 = bf16[256,768]{1,0:T(8,128)(2,1)S(1)} collective-permute-done((bf16[256,768]{1,0:T(8,128)(2,1)}, bf16[256,768]{1,0:T(8,128)(2,1)S(1)}, u32[]{:S(2)}, u32[]{:S(2)}) %collective-permute-start.5) | collective-permute-done | bytes 393248 | tf_op jit(solution)/shard_map/ppermute | solution.py:61
  19.6 7.0 %collective-permute-done.6 = bf16[256,768]{1,0:T(8,128)(2,1)S(1)} collective-permute-done((bf16[256,768]{1,0:T(8,128)(2,1)}, bf16[256,768]{1,0:T(8,128)(2,1)S(1)}, u32[]{:S(2)}, u32[]{:S(2)}) %collective-permute-start.6) | collective-permute-done | bytes 393248 | tf_op jit(solution)/shard_map/ppermute | solution.py:61
  26.6 0.1 pad_maximum_fusion.1
  26.8 0.6 fusion.11
  27.5 0.6 fusion.9
  28.1 3.7 %collective-permute-start.1 = (bf16[128,384]{1,0:T(8,128)(2,1)S(1)}, bf16[128,384]{1,0:T(8,128)(2,1)S(1)}, u32[]{:S(2)}, u32[]{:S(2)}) collective-permute-start(bf16[128,384]{1,0:T(8,128)(2,1)S(1)} %fusion.9), channel_id=1, source_target_pairs={{0,2},{2,4},{4,6},{6,8},{8,10},{10,12},{12,14},{1,3},{3,5},{5,7},{... | collective-permute-start | bytes 294920 | tf_op jit(solution)/shard_map/ppermute | solution.py:64
  31.9 1.3 collective-permute-start.2
  33.2 0.2 constant_dynamic-slice_fusion.18
  33.4 1.2 collective-permute-done.1
  34.6 4.1 %collective-permute-done.2 = bf16[128,384]{1,0:T(8,128)(2,1)S(1)} collective-permute-done((bf16[128,384]{1,0:T(8,128)(2,1)S(1)}, bf16[128,384]{1,0:T(8,128)(2,1)S(1)}, u32[]{:S(2)}, u32[]{:S(2)}) %collective-permute-start.2) | collective-permute-done | bytes 98336 | tf_op jit(solution)/shard_map/ppermute | solution.py:65
  38.8 9.1 %fusion.33 = (f32[128]{0:T(128)S(1)}, f32[128,6144]{1,0:T(8,128)S(1)}) fusion(f32[6144]{0:T(1024)S(1)} %copy-done.14, bf16[128,384]{1,0:T(8,128)(2,1)S(1)} %fusion.15, bf16[3072,384]{1,0:T(8,128)(2,1)} %collective-permute-done.3, bf16[3072,384]{1,0:T(8,128)(2,1)S(1)} %copy-done.13, pred[]{:T(512)S(6)} %eq.6, bf16[128,6144]{1,0:T(8,128)(2,1)S(1)} %copy-done.1), kind=kOutput, calls=%fused_computation.138 | convolution fusion | flops 629931904 | bytes 9560577 | tf_op jit(solution)/shard_map/dot_general | solution.py:38
  47.9 0.5 multiply_reduce_fusion.1
  48.4 0.9 copy-done
  49.3 1.0 fusion.3
  50.2 2.5 %multiply_convert_fusion = (bf16[128,6144]{1,0:T(8,128)(2,1)S(1)}, bf16[128,6144]{1,0:T(8,128)(2,1)}) fusion(bf16[128,6144]{1,0:T(8,128)(2,1)S(1)} %copy-done, f32[128,6144]{1,0:T(8,128)S(1)} %get-tuple-element.76, f32[128]{0:T(128)S(1)} %get-tuple-element.77, f32[128]{0:T(128)S(1)} %get-tuple-element.78, f32[6144]{0:T(1024)S(1)} %copy-done.3, ...), kind=kLoop, calls=%fused_computation.5 | loop fusion | flops 8650752 | bytes 7890944 | tf_op jit(solution)/shard_map/convert_element_type | solution.py:130
  52.8 3.9 %convolution_convert_fusion = bf16[128,384]{1,0:T(8,128)(2,1)S(1)} fusion(bf16[128,6144]{1,0:T(8,128)(2,1)S(1)} %get-tuple-element.31, bf16[3072,384]{1,0:T(8,128)(2,1)} %collective-permute-done.3, bf16[3072,384]{1,0:T(8,128)(2,1)S(1)} %copy-done.13, pred[]{:T(512)S(6)} %eq.6), kind=kOutput, calls=%fused_computation.23 | convolution fusion | flops 625262592 | bytes 6389761 | tf_op jit(solution)/shard_map/dot_general | solution.py:131
  56.6 1.3 collective-permute-start.7
  57.9 5.1 %collective-permute-start.8 = (bf16[128,384]{1,0:T(8,128)(2,1)S(1)}, bf16[128,384]{1,0:T(8,128)(2,1)S(1)}, u32[]{:S(2)}, u32[]{:S(2)}) collective-permute-start(bf16[128,384]{1,0:T(8,128)(2,1)S(1)} %convolution_convert_fusion), channel_id=1, source_target_pairs={{0,2},{2,4},{4,6},{6,8},{8,10},{10,12},{12,14},{1,3},{3,5},{5,7},{... | collective-permute-start | bytes 294920 | tf_op jit(solution)/shard_map/ppermute | solution.py:64
  63.1 0.2 constant_dynamic-slice_fusion.16
  63.3 3.0 %collective-permute-start.18 = (bf16[128,384]{1,0:T(8,128)(2,1)S(1)}, bf16[128,384]{1,0:T(8,128)(2,1)S(1)}, u32[]{:S(2)}, u32[]{:S(2)}) collective-permute-start(bf16[128,384]{1,0:T(8,128)(2,1)S(1)} %fusion.15), channel_id=1, source_target_pairs={{0,2},{2,0},{4,6},{6,4},{8,10},{10,8},{12,14},{14,12},{1,3},{3,1},... | collective-permute-start | bytes 294920 | tf_op jit(solution)/shard_map/ppermute | solution.py:61
  66.2 1.6 %collective-permute-start.19 = (bf16[128,384]{1,0:T(8,128)(2,1)S(1)}, bf16[128,384]{1,0:T(8,128)(2,1)S(1)}, u32[]{:S(2)}, u32[]{:S(2)}) collective-permute-start(bf16[128,384]{1,0:T(8,128)(2,1)S(1)} %fusion.15), channel_id=1, source_target_pairs={{0,4},{2,6},{4,0},{6,2},{8,12},{10,14},{12,8},{14,10},{1,5},{3,7},... | collective-permute-start | bytes 294920 | tf_op jit(solution)/shard_map/ppermute | solution.py:61
  67.8 0.8 pad_maximum_fusion.7
  68.6 0.8 pad_maximum_fusion.8
  69.4 2.0 %collective-permute-start.15 = (bf16[256,768]{1,0:T(8,128)(2,1)}, bf16[256,768]{1,0:T(8,128)(2,1)}, u32[]{:S(2)}, u32[]{:S(2)}) collective-permute-start(bf16[256,768]{1,0:T(8,128)(2,1)} %pad_maximum_fusion.7), channel_id=1, source_target_pairs={{0,2},{2,0},{4,6},{6,4},{8,10},{10,8},{12,14},{14,12},{1,3},{3,1},... | collective-permute-start | bytes 1179656 | tf_op jit(solution)/shard_map/ppermute | solution.py:61
  71.4 1.6 %collective-permute-start.16 = (bf16[256,768]{1,0:T(8,128)(2,1)}, bf16[256,768]{1,0:T(8,128)(2,1)}, u32[]{:S(2)}, u32[]{:S(2)}) collective-permute-start(bf16[256,768]{1,0:T(8,128)(2,1)} %pad_maximum_fusion.8), channel_id=1, source_target_pairs={{0,4},{2,6},{4,0},{6,2},{8,12},{10,14},{12,8},{14,10},{1,5},{3,7},... | collective-permute-start | bytes 1179656 | tf_op jit(solution)/shard_map/ppermute | solution.py:61
  73.0 0.1 fusion.19
  73.3 0.5 collective-permute-start.10
  73.8 0.8 pad_maximum_fusion.9
  74.5 1.1 collective-permute-start.17
  75.7 1.8 %collective-permute-start.11 = (bf16[144,384]{1,0:T(8,128)(2,1)S(1)}, bf16[144,384]{1,0:T(8,128)(2,1)}, u32[]{:S(2)}, u32[]{:S(2)}) collective-permute-start(bf16[144,384]{1,0:T(8,128)(2,1)S(1)} %pad_maximum_fusion.12), channel_id=1, source_target_pairs={{0,6},{2,4},{4,2},{6,0},{8,14},{10,12},{12,10},{14,8},{1,7},{3,5},... | collective-permute-start | bytes 331784 | tf_op jit(solution)/shard_map/ppermute | solution.py:61
  77.5 8.5 %collective-permute-done.10 = bf16[144,384]{1,0:T(8,128)(2,1)S(1)} collective-permute-done((bf16[144,384]{1,0:T(8,128)(2,1)S(1)}, bf16[144,384]{1,0:T(8,128)(2,1)S(1)}, u32[]{:S(2)}, u32[]{:S(2)}) %collective-permute-start.10) | collective-permute-done | bytes 110624 | tf_op jit(solution)/shard_map/ppermute | solution.py:61
  86.0 0.1 collective-permute-start.9
  86.2 8.4 %collective-permute-done.11 = bf16[144,384]{1,0:T(8,128)(2,1)} collective-permute-done((bf16[144,384]{1,0:T(8,128)(2,1)S(1)}, bf16[144,384]{1,0:T(8,128)(2,1)}, u32[]{:S(2)}, u32[]{:S(2)}) %collective-permute-start.11) | collective-permute-done | bytes 110624 | tf_op jit(solution)/shard_map/ppermute | solution.py:61
  94.6 1.1 collective-permute-done.9
  95.7 1.9 %concatenate.66 = bf16[576,384]{1,0:T(8,128)(2,1)S(1)} concatenate(bf16[128,384]{1,0:T(8,128)(2,1)S(1)} %get-tuple-element.74, bf16[4,384]{1,0:T(4,128)(2,1)S(1)} %fusion.29, bf16[4,384]{1,0:T(4,128)(2,1)S(1)} %subtract_convert_fusion.1, bf16[8,384]{1,0:T(8,128)(2,1)S(1)} %broadcast_in_dim.4, bf16[144,384]{1,0:T(8,128)(2,1)} %collective-permute-done.9, ...), dimensions={0} | concatenate | bytes 884736 | tf_op jit(solution)/shard_map/concatenate | solution.py:90
  97.8 1.1 constant_dynamic-slice_fusion.13
  98.9 1.1 constant_dynamic-slice_fusion.10
  100.0 1.1 constant_dynamic-slice_fusion.7
  101.2 0.6 collective-permute-start.21
  101.9 0.4 fusion.35
  102.3 0.4 fusion.6
  102.8 1.6 %collective-permute-start.14 = (bf16[400,384]{1,0:T(8,128)(2,1)S(1)}, bf16[400,384]{1,0:T(8,128)(2,1)S(1)}, u32[]{:S(2)}, u32[]{:S(2)}) collective-permute-start(bf16[400,384]{1,0:T(8,128)(2,1)S(1)} %pad_maximum_fusion.11), channel_id=1, source_target_pairs={{0,8},{2,10},{4,12},{6,14},{8,0},{10,2},{12,4},{14,6},{1,9},{3,11}... | collective-permute-start | bytes 921608 | tf_op jit(solution)/shard_map/ppermute | solution.py:164
  104.3 0.2 convert_reduce_fusion.3
  104.6 0.4 fusion.34
  105.0 14.5 %collective-permute-done.14 = bf16[400,384]{1,0:T(8,128)(2,1)S(1)} collective-permute-done((bf16[400,384]{1,0:T(8,128)(2,1)S(1)}, bf16[400,384]{1,0:T(8,128)(2,1)S(1)}, u32[]{:S(2)}, u32[]{:S(2)}) %collective-permute-start.14) | collective-permute-done | bytes 307232 | tf_op jit(solution)/shard_map/ppermute | solution.py:164
  119.6 1.2 fusion.5
  120.8 0.2 convert_reduce_fusion.2
  121.1 0.4 fusion.37
  121.6 0.4 fusion.7
  122.0 0.1 maximum_maximum_fusion
  122.2 0.6 slice_reduce_fusion
  122.8 0.4 fusion.36
  123.2 15.1 %collective-permute-done.23 = bf16[400,384]{1,0:T(8,128)(2,1)S(1)} collective-permute-done((bf16[400,384]{1,0:T(8,128)(2,1)S(1)}, bf16[400,384]{1,0:T(8,128)(2,1)S(1)}, u32[]{:S(2)}, u32[]{:S(2)}) %collective-permute-start.23) | collective-permute-done | bytes 307232 | tf_op jit(solution)/shard_map/ppermute | solution.py:164
  138.3 0.6 add_add_fusion.1
  138.9 1.2 fusion.4
  (86 shorter events, 1.4 us)
Async XLA Ops:
  0.6 26.9 %collective-permute-start = (bf16[3072,384]{1,0:T(8,128)(2,1)}, bf16[3072,384]{1,0:T(8,128)(2,1)S(1)}, u32[]{:S(2)}, u32[]{:S(2)}) collective-permute-start(bf16[3072,384]{1,0:T(8,128)(2,1)} %param.10), channel_id=1, source_target_pairs={{0,1},{1,0},{2,3},{3,2},{4,5},{5,4},{6,7},{7,6},{8,9},{9,8},{10,11... | collective-permute-start | bytes 7077896 | tf_op jit(solution)/shard_map/ppermute | solution.py:58
  1.1 37.6 %collective-permute-start.3 = (bf16[3072,384]{1,0:T(8,128)(2,1)}, bf16[3072,384]{1,0:T(8,128)(2,1)}, u32[]{:S(2)}, u32[]{:S(2)}) collective-permute-start(bf16[3072,384]{1,0:T(8,128)(2,1)} %param.13), channel_id=1, source_target_pairs={{0,1},{1,0},{2,3},{3,2},{4,5},{5,4},{6,7},{7,6},{8,9},{9,8},{10,11... | collective-permute-start | bytes 7077896 | tf_op jit(solution)/shard_map/ppermute | solution.py:58
  3.6 12.6 %collective-permute-start.4 = (bf16[256,768]{1,0:T(8,128)(2,1)}, bf16[256,768]{1,0:T(8,128)(2,1)}, u32[]{:S(2)}, u32[]{:S(2)}) collective-permute-start(bf16[256,768]{1,0:T(8,128)(2,1)} %pad_maximum_fusion.4), channel_id=1, source_target_pairs={{0,2},{2,0},{4,6},{6,4},{8,10},{10,8},{12,14},{14,12},{1,3},{3,1},... | collective-permute-start | bytes 1179656 | tf_op jit(solution)/shard_map/ppermute | solution.py:61
  7.3 12.2 %collective-permute-start.5 = (bf16[256,768]{1,0:T(8,128)(2,1)}, bf16[256,768]{1,0:T(8,128)(2,1)S(1)}, u32[]{:S(2)}, u32[]{:S(2)}) collective-permute-start(bf16[256,768]{1,0:T(8,128)(2,1)} %pad_maximum_fusion.5), channel_id=1, source_target_pairs={{0,4},{2,6},{4,0},{6,2},{8,12},{10,14},{12,8},{14,10},{1,5},{3,7},... | collective-permute-start | bytes 1179656 | tf_op jit(solution)/shard_map/ppermute | solution.py:61
  9.6 16.9 %collective-permute-start.6 = (bf16[256,768]{1,0:T(8,128)(2,1)}, bf16[256,768]{1,0:T(8,128)(2,1)S(1)}, u32[]{:S(2)}, u32[]{:S(2)}) collective-permute-start(bf16[256,768]{1,0:T(8,128)(2,1)} %pad_maximum_fusion.6), channel_id=1, source_target_pairs={{0,6},{2,4},{4,2},{6,0},{8,14},{10,12},{12,10},{14,8},{1,7},{3,5},... | collective-permute-start | bytes 1179656 | tf_op jit(solution)/shard_map/ppermute | solution.py:61
  9.7 17.0 %copy-start.11 = (f32[3,384]{1,0:T(4,128)S(1)}, f32[3,384]{1,0:T(4,128)}, u32[]{:S(2)}) copy-start(f32[3,384]{1,0:T(4,128)} %param.12) | copy-start | bytes 13828
  9.7 17.1 %copy-start.1 = (bf16[128,6144]{1,0:T(8,128)(2,1)S(1)}, bf16[128,6144]{1,0:T(8,128)(2,1)}, u32[]{:S(2)}) copy-start(bf16[128,6144]{1,0:T(8,128)(2,1)} %param.8) | copy-start | bytes 4718596
  9.7 17.1 %copy-start.2 = (bf16[3072,384]{1,0:T(8,128)(2,1)S(1)}, bf16[3072,384]{1,0:T(8,128)(2,1)}, u32[]{:S(2)}) copy-start(bf16[3072,384]{1,0:T(8,128)(2,1)} %param.10) | copy-start | bytes 7077892
  26.7 6.5 %collective-permute-start.12 = (bf16[1024,384]{1,0:T(8,128)(2,1)S(1)}, bf16[1024,384]{1,0:T(8,128)(2,1)S(1)}, u32[]{:S(2)}, u32[]{:S(2)}) collective-permute-start(bf16[1024,384]{1,0:T(8,128)(2,1)S(1)} %pad_maximum_fusion.1), channel_id=1, source_target_pairs={{0,1},{1,0},{2,3},{3,2},{4,5},{5,4},{6,7},{7,6},{8,9},{9,8},{10,11... | collective-permute-start | bytes 2359304 | tf_op jit(solution)/shard_map/ppermute | solution.py:58
  26.8 0.7 copy-start.12
  28.1 10.6 %copy-start.13 = (bf16[3072,384]{1,0:T(8,128)(2,1)S(1)}, bf16[3072,384]{1,0:T(8,128)(2,1)}, u32[]{:S(2)}) copy-start(bf16[3072,384]{1,0:T(8,128)(2,1)} %param.13) | copy-start | bytes 7077892
  28.1 10.6 %copy-start.14 = (f32[6144]{0:T(1024)S(1)}, f32[6144]{0:T(1024)}, u32[]{:S(2)}) copy-start(f32[6144]{0:T(1024)} %param.14) | copy-start | bytes 73732
  28.1 6.4 %collective-permute-start.1 = (bf16[128,384]{1,0:T(8,128)(2,1)S(1)}, bf16[128,384]{1,0:T(8,128)(2,1)S(1)}, u32[]{:S(2)}, u32[]{:S(2)}) collective-permute-start(bf16[128,384]{1,0:T(8,128)(2,1)S(1)} %fusion.9), channel_id=1, source_target_pairs={{0,2},{2,4},{4,6},{6,8},{8,10},{10,12},{12,14},{1,3},{3,5},{5,7},{... | collective-permute-start | bytes 294920 | tf_op jit(solution)/shard_map/ppermute | solution.py:64
  31.9 6.8 %collective-permute-start.2 = (bf16[128,384]{1,0:T(8,128)(2,1)S(1)}, bf16[128,384]{1,0:T(8,128)(2,1)S(1)}, u32[]{:S(2)}, u32[]{:S(2)}) collective-permute-start(bf16[128,384]{1,0:T(8,128)(2,1)S(1)} %fusion.9), channel_id=1, source_target_pairs={{2,0},{4,2},{6,4},{8,6},{10,8},{12,10},{14,12},{3,1},{5,3},{7,5},{... | collective-permute-start | bytes 294920 | tf_op jit(solution)/shard_map/ppermute | solution.py:65
  47.9 1.4 %copy-start = (bf16[128,6144]{1,0:T(8,128)(2,1)S(1)}, bf16[128,6144]{1,0:T(8,128)(2,1)}, u32[]{:S(2)}) copy-start(bf16[128,6144]{1,0:T(8,128)(2,1)} %param.9) | copy-start | bytes 4718596
  47.9 1.4 %copy-start.3 = (f32[6144]{0:T(1024)S(1)}, f32[6144]{0:T(1024)}, u32[]{:S(2)}) copy-start(f32[6144]{0:T(1024)} %param.15) | copy-start | bytes 73732
  56.6 12.8 %collective-permute-start.7 = (bf16[128,384]{1,0:T(8,128)(2,1)S(1)}, bf16[128,384]{1,0:T(8,128)(2,1)S(1)}, u32[]{:S(2)}, u32[]{:S(2)}) collective-permute-start(bf16[128,384]{1,0:T(8,128)(2,1)S(1)} %convolution_convert_fusion), channel_id=1, source_target_pairs={{2,0},{4,2},{6,4},{8,6},{10,8},{12,10},{14,12},{3,1},{5,3},{7,5},{... | collective-permute-start | bytes 294920 | tf_op jit(solution)/shard_map/ppermute | solution.py:65
  57.9 13.4 %collective-permute-start.8 = (bf16[128,384]{1,0:T(8,128)(2,1)S(1)}, bf16[128,384]{1,0:T(8,128)(2,1)S(1)}, u32[]{:S(2)}, u32[]{:S(2)}) collective-permute-start(bf16[128,384]{1,0:T(8,128)(2,1)S(1)} %convolution_convert_fusion), channel_id=1, source_target_pairs={{0,2},{2,4},{4,6},{6,8},{8,10},{10,12},{12,14},{1,3},{3,5},{5,7},{... | collective-permute-start | bytes 294920 | tf_op jit(solution)/shard_map/ppermute | solution.py:64
  63.3 10.0 %collective-permute-start.18 = (bf16[128,384]{1,0:T(8,128)(2,1)S(1)}, bf16[128,384]{1,0:T(8,128)(2,1)S(1)}, u32[]{:S(2)}, u32[]{:S(2)}) collective-permute-start(bf16[128,384]{1,0:T(8,128)(2,1)S(1)} %fusion.15), channel_id=1, source_target_pairs={{0,2},{2,0},{4,6},{6,4},{8,10},{10,8},{12,14},{14,12},{1,3},{3,1},... | collective-permute-start | bytes 294920 | tf_op jit(solution)/shard_map/ppermute | solution.py:61
  66.2 8.3 %collective-permute-start.19 = (bf16[128,384]{1,0:T(8,128)(2,1)S(1)}, bf16[128,384]{1,0:T(8,128)(2,1)S(1)}, u32[]{:S(2)}, u32[]{:S(2)}) collective-permute-start(bf16[128,384]{1,0:T(8,128)(2,1)S(1)} %fusion.15), channel_id=1, source_target_pairs={{0,4},{2,6},{4,0},{6,2},{8,12},{10,14},{12,8},{14,10},{1,5},{3,7},... | collective-permute-start | bytes 294920 | tf_op jit(solution)/shard_map/ppermute | solution.py:61
  67.8 7.8 %collective-permute-start.20 = (bf16[128,384]{1,0:T(8,128)(2,1)S(1)}, bf16[128,384]{1,0:T(8,128)(2,1)S(1)}, u32[]{:S(2)}, u32[]{:S(2)}) collective-permute-start(bf16[128,384]{1,0:T(8,128)(2,1)S(1)} %fusion.15), channel_id=1, source_target_pairs={{0,6},{2,4},{4,2},{6,0},{8,14},{10,12},{12,10},{14,8},{1,7},{3,5},... | collective-permute-start | bytes 294920 | tf_op jit(solution)/shard_map/ppermute | solution.py:61
  69.4 28.4 %collective-permute-start.15 = (bf16[256,768]{1,0:T(8,128)(2,1)}, bf16[256,768]{1,0:T(8,128)(2,1)}, u32[]{:S(2)}, u32[]{:S(2)}) collective-permute-start(bf16[256,768]{1,0:T(8,128)(2,1)} %pad_maximum_fusion.7), channel_id=1, source_target_pairs={{0,2},{2,0},{4,6},{6,4},{8,10},{10,8},{12,14},{14,12},{1,3},{3,1},... | collective-permute-start | bytes 1179656 | tf_op jit(solution)/shard_map/ppermute | solution.py:61
  71.4 27.5 %collective-permute-start.16 = (bf16[256,768]{1,0:T(8,128)(2,1)}, bf16[256,768]{1,0:T(8,128)(2,1)}, u32[]{:S(2)}, u32[]{:S(2)}) collective-permute-start(bf16[256,768]{1,0:T(8,128)(2,1)} %pad_maximum_fusion.8), channel_id=1, source_target_pairs={{0,4},{2,6},{4,0},{6,2},{8,12},{10,14},{12,8},{14,10},{1,5},{3,7},... | collective-permute-start | bytes 1179656 | tf_op jit(solution)/shard_map/ppermute | solution.py:61
  73.3 21.4 %copy-start.4 = (bf16[128,384]{1,0:T(8,128)(2,1)}, bf16[128,384]{1,0:T(8,128)(2,1)S(1)}, u32[]{:S(2)}) copy-start(bf16[128,384]{1,0:T(8,128)(2,1)S(1)} %collective-permute-done.18) | copy-start | bytes 294916
  73.3 12.8 %collective-permute-start.10 = (bf16[144,384]{1,0:T(8,128)(2,1)S(1)}, bf16[144,384]{1,0:T(8,128)(2,1)S(1)}, u32[]{:S(2)}, u32[]{:S(2)}) collective-permute-start(bf16[144,384]{1,0:T(8,128)(2,1)S(1)} %pad_maximum_fusion.12), channel_id=1, source_target_pairs={{0,4},{2,6},{4,0},{6,2},{8,12},{10,14},{12,8},{14,10},{1,5},{3,7},... | collective-permute-start | bytes 331784 | tf_op jit(solution)/shard_map/ppermute | solution.py:61
  74.5 20.1 %copy-start.6 = (bf16[128,384]{1,0:T(8,128)(2,1)}, bf16[128,384]{1,0:T(8,128)(2,1)S(1)}, u32[]{:S(2)}) copy-start(bf16[128,384]{1,0:T(8,128)(2,1)S(1)} %collective-permute-done.19) | copy-start | bytes 294916
  74.5 25.4 %collective-permute-start.17 = (bf16[256,768]{1,0:T(8,128)(2,1)}, bf16[256,768]{1,0:T(8,128)(2,1)}, u32[]{:S(2)}, u32[]{:S(2)}) collective-permute-start(bf16[256,768]{1,0:T(8,128)(2,1)} %pad_maximum_fusion.9), channel_id=1, source_target_pairs={{0,6},{2,4},{4,2},{6,0},{8,14},{10,12},{12,10},{14,8},{1,7},{3,5},... | collective-permute-start | bytes 1179656 | tf_op jit(solution)/shard_map/ppermute | solution.py:61
  75.7 19.0 %copy-start.8 = (bf16[128,384]{1,0:T(8,128)(2,1)}, bf16[128,384]{1,0:T(8,128)(2,1)S(1)}, u32[]{:S(2)}) copy-start(bf16[128,384]{1,0:T(8,128)(2,1)S(1)} %collective-permute-done.20) | copy-start | bytes 294916
  75.7 19.0 %collective-permute-start.11 = (bf16[144,384]{1,0:T(8,128)(2,1)S(1)}, bf16[144,384]{1,0:T(8,128)(2,1)}, u32[]{:S(2)}, u32[]{:S(2)}) collective-permute-start(bf16[144,384]{1,0:T(8,128)(2,1)S(1)} %pad_maximum_fusion.12), channel_id=1, source_target_pairs={{0,6},{2,4},{4,2},{6,0},{8,14},{10,12},{12,10},{14,8},{1,7},{3,5},... | collective-permute-start | bytes 331784 | tf_op jit(solution)/shard_map/ppermute | solution.py:61
  86.0 9.7 %collective-permute-start.9 = (bf16[144,384]{1,0:T(8,128)(2,1)S(1)}, bf16[144,384]{1,0:T(8,128)(2,1)}, u32[]{:S(2)}, u32[]{:S(2)}) collective-permute-start(bf16[144,384]{1,0:T(8,128)(2,1)S(1)} %pad_maximum_fusion.12), channel_id=1, source_target_pairs={{0,2},{2,0},{4,6},{6,4},{8,10},{10,8},{12,14},{14,12},{1,3},{3,1},... | collective-permute-start | bytes 331784 | tf_op jit(solution)/shard_map/ppermute | solution.py:61
  94.6 26.5 %collective-permute-start.22 = (bf16[512,384]{1,0:T(8,128)(2,1)S(1)}, bf16[512,384]{1,0:T(8,128)(2,1)S(1)}, u32[]{:S(2)}, u32[]{:S(2)}) collective-permute-start(bf16[512,384]{1,0:T(8,128)(2,1)S(1)} %pad_maximum_fusion.10), channel_id=1, source_target_pairs={{0,1},{1,0},{2,3},{3,2},{4,5},{5,4},{6,7},{7,6},{8,9},{9,8},{10,11... | collective-permute-start | bytes 1179656 | tf_op jit(solution)/shard_map/ppermute | solution.py:58
  97.7 4.1 %collective-permute-start.13 = (bf16[576,384]{1,0:T(8,128)(2,1)S(1)}, bf16[576,384]{1,0:T(8,128)(2,1)S(1)}, u32[]{:S(2)}, u32[]{:S(2)}) collective-permute-start(bf16[576,384]{1,0:T(8,128)(2,1)S(1)} %concatenate.66), channel_id=1, source_target_pairs={{0,1},{1,0},{2,3},{3,2},{4,5},{5,4},{6,7},{7,6},{8,9},{9,8},{10,11... | collective-permute-start | bytes 1327112 | tf_op jit(solution)/shard_map/ppermute | solution.py:58
  101.2 19.7 %collective-permute-start.21 = (bf16[1024,384]{1,0:T(8,128)(2,1)S(1)}, bf16[1024,384]{1,0:T(8,128)(2,1)S(1)}, u32[]{:S(2)}, u32[]{:S(2)}) collective-permute-start(bf16[1024,384]{1,0:T(8,128)(2,1)S(1)} %pad_maximum_fusion.3), channel_id=1, source_target_pairs={{0,1},{1,0},{2,3},{3,2},{4,5},{5,4},{6,7},{7,6},{8,9},{9,8},{10,11... | collective-permute-start | bytes 2359304 | tf_op jit(solution)/shard_map/ppermute | solution.py:58
  102.8 16.7 %collective-permute-start.14 = (bf16[400,384]{1,0:T(8,128)(2,1)S(1)}, bf16[400,384]{1,0:T(8,128)(2,1)S(1)}, u32[]{:S(2)}, u32[]{:S(2)}) collective-permute-start(bf16[400,384]{1,0:T(8,128)(2,1)S(1)} %pad_maximum_fusion.11), channel_id=1, source_target_pairs={{0,8},{2,10},{4,12},{6,14},{8,0},{10,2},{12,4},{14,6},{1,9},{3,11}... | collective-permute-start | bytes 921608 | tf_op jit(solution)/shard_map/ppermute | solution.py:164
  119.5 2.0 %copy-start.5 = (bf16[128,384]{1,0:T(8,128)(2,1)S(1)}, bf16[128,384]{1,0:T(8,128)(2,1)}, u32[]{:S(2)}) copy-start(bf16[128,384]{1,0:T(8,128)(2,1)} %copy-done.4) | copy-start | bytes 294916
  119.6 2.0 %copy-start.7 = (bf16[128,384]{1,0:T(8,128)(2,1)S(1)}, bf16[128,384]{1,0:T(8,128)(2,1)}, u32[]{:S(2)}) copy-start(bf16[128,384]{1,0:T(8,128)(2,1)} %copy-done.6) | copy-start | bytes 294916
  119.6 2.0 %copy-start.9 = (bf16[128,384]{1,0:T(8,128)(2,1)S(1)}, bf16[128,384]{1,0:T(8,128)(2,1)}, u32[]{:S(2)}) copy-start(bf16[128,384]{1,0:T(8,128)(2,1)} %copy-done.8) | copy-start | bytes 294916
  120.8 1.3 copy-start.10
  122.1 16.1 %collective-permute-start.23 = (bf16[400,384]{1,0:T(8,128)(2,1)S(1)}, bf16[400,384]{1,0:T(8,128)(2,1)S(1)}, u32[]{:S(2)}, u32[]{:S(2)}) collective-permute-start(bf16[400,384]{1,0:T(8,128)(2,1)S(1)} %maximum_maximum_fusion), channel_id=1, source_target_pairs={{0,8},{2,10},{4,12},{6,14},{8,0},{10,2},{12,4},{14,6},{1,9},{3,11}... | collective-permute-start | bytes 921608 | tf_op jit(solution)/shard_map/ppermute | solution.py:164

commit v2 on v0

v2 whole, which is shorter than its diff:
```python
import functools

import jax
import jax.numpy as jnp
from jax import lax
from jax.experimental import pallas as pl
from jax.experimental.pallas import tpu as pltpu
from jax.sharding import PartitionSpec as P

epsilon = 1e-06
cores = 2
block_frames = 4
members = cores * block_frames
lanes = 128
chunk = 768
narrow, wide = jnp.bfloat16, jnp.float32


def inner_rows(left, right):
    return lax.dot_general(
        left, right, (((0,), (0,)), ((), ())), preferred_element_type=wide
    )


def outer_rows(left, right):
    return lax.dot_general(
        left, right, (((1,), (1,)), ((), ())), preferred_element_type=wide
    )


def folded(values):
    return sum(
        values[:, start : start + lanes] for start in range(0, values.shape[1], lanes)
    )


def lift_kernel(
    index_ref,
    frames_ref,
    cotangent_ref,
    conv_ref,
    own_ref,
    other_ref,
    bias_ref,
    gain_ref,
    out_ref,
    *other_refs,
):
    *sent_refs, grad_conv_ref, lifted_ref = other_refs
    tokens, features = frames_ref.shape
    half = features // cores
    share, half_blocks = sent_refs[0].shape[-1], sent_refs[0].shape[1] // cores
    core, place = index_ref[0], index_ref[1]
    conv = conv_ref[...]
    pieces = []
    for weight_ref, side in ((own_ref, core), (other_ref, 1 - core)):
        for start in range(0, half, chunk):
            pieces.append((weight_ref, start, side))

    def columns(start, side):
        return pl.ds(pl.multiple_of(side * half + start, lanes), chunk)

    total = jnp.zeros((tokens, lanes), wide)
    for weight_ref, start, side in pieces:
        where = columns(start, side)
        raised = outer_rows(conv, weight_ref[start : start + chunk, :])
        lifted = (frames_ref[:, where].astype(wide) + raised + bias_ref[:, where]).astype(narrow)
        lifted_ref[:, where] = lifted
        total = total + folded(lifted.astype(wide))
    center = jnp.sum(total, axis=1, keepdims=True) / features

    squares = jnp.zeros((tokens, lanes), wide)
    plain = jnp.zeros((tokens, lanes), wide)
    crossed = jnp.zeros((tokens, lanes), wide)
    for weight_ref, start, side in pieces:
        where = columns(start, side)
        shifted = lifted_ref[:, where].astype(wide) - center
        scaled = cotangent_ref[:, where].astype(wide) * gain_ref[:, where]
        squares = squares + folded(shifted * shifted)
        plain = plain + folded(scaled)
        crossed = crossed + folded(scaled * shifted)
    inverse = lax.rsqrt(jnp.sum(squares, axis=1, keepdims=True) / features + epsilon)
    mean_plain = jnp.sum(plain, axis=1, keepdims=True) / features
    mean_crossed = inverse * jnp.sum(crossed, axis=1, keepdims=True) / features

    grad_conv = jnp.zeros(grad_conv_ref.shape, wide)
    for weight_ref, start, side in pieces:
        where = columns(start, side)
        unit = (lifted_ref[:, where].astype(wide) - center) * inverse
        gain = gain_ref[:, where]
        out_ref[:, where] = (unit * gain).astype(narrow)
        scaled = cotangent_ref[:, where].astype(wide) * gain
        grad = (inverse * (scaled - mean_plain - unit * mean_crossed)).astype(narrow)
        for piece in range(chunk // share):
            slot = start // share + piece
            member, block = slot % members // cores, side * half_blocks + slot // members
            for step, sent_ref in enumerate(sent_refs):

                @pl.when((place ^ step) == member)
                def _():
                    sent_ref[core ^ (slot % cores), block] = grad[
                        :, piece * share : (piece + 1) * share
                    ]

        grad_conv = grad_conv + jnp.dot(
            grad, weight_ref[start : start + chunk, :], preferred_element_type=wide
        )
    grad_conv_ref[...] = grad_conv.astype(narrow)


def lift(index, frames_in, cotangent, conv, own, other, bias, gain, blocks, share):
    tokens, features = frames_in.shape
    channels = conv.shape[1]
    vmem = pl.BlockSpec(memory_space=pltpu.VMEM)
    return pl.pallas_call(
        lift_kernel,
        out_shape=(
            jax.ShapeDtypeStruct((tokens, features), narrow),
            *[jax.ShapeDtypeStruct((cores, blocks, tokens, share), narrow)] * block_frames,
            jax.ShapeDtypeStruct((tokens, channels), narrow),
        ),
        in_specs=[pl.BlockSpec(memory_space=pltpu.SMEM)] + [vmem] * 7,
        out_specs=(vmem,) * (2 + block_frames),
        scratch_shapes=[pltpu.VMEM((tokens, features), narrow)],
        compiler_params=pltpu.CompilerParams(vmem_limit_bytes=32 * 1024 * 1024),
        cost_estimate=pl.CostEstimate(
            flops=0,
            bytes_accessed=0,
            transcendentals=0,
        ),
        name="lift",
    )(index, frames_in, cotangent, conv, own, other, bias[None], gain[None])


def split_kernel(index_ref, value_ref, *out_refs):
    core, place = index_ref[0], index_ref[1]
    blocks, share = out_refs[0].shape[1], out_refs[0].shape[-1]
    for member in range(block_frames):
        for step in range(block_frames):

            @pl.when((place ^ step) == member)
            def _():
                for block in range(blocks):
                    for side in range(cores):
                        start = ((block * block_frames + member) * cores + side) * share
                        out_refs[step][core ^ side, block] = value_ref[:, start : start + share]


def split(index, value, blocks, share):
    vmem = pl.BlockSpec(memory_space=pltpu.VMEM)
    part = jax.ShapeDtypeStruct((cores, blocks, value.shape[0], share), value.dtype)
    return pl.pallas_call(
        split_kernel,
        out_shape=(part,) * block_frames,
        in_specs=[pl.BlockSpec(memory_space=pltpu.SMEM), vmem],
        out_specs=(vmem,) * block_frames,
        compiler_params=pltpu.CompilerParams(vmem_limit_bytes=16 * 1024 * 1024),
        name="split",
    )(index, value)


def squeeze_kernel(index_ref, frames_ref, weight_ref, start_ref, out_ref, *, side):
    half = weight_ref.shape[0]
    columns = pl.ds(pl.multiple_of((index_ref[0] ^ side) * half, lanes), half)
    total = start_ref[...] + jnp.dot(
        frames_ref[:, columns], weight_ref[...], preferred_element_type=wide
    )
    out_ref[...] = total.astype(out_ref.dtype)


def squeeze(index, frames_in, weight, start, side, dtype):
    vmem = pl.BlockSpec(memory_space=pltpu.VMEM)
    return pl.pallas_call(
        functools.partial(squeeze_kernel, side=side),
        out_shape=jax.ShapeDtypeStruct((frames_in.shape[0], weight.shape[1]), dtype),
        in_specs=[pl.BlockSpec(memory_space=pltpu.SMEM)] + [vmem] * 3,
        out_specs=vmem,
        compiler_params=pltpu.CompilerParams(vmem_limit_bytes=24 * 1024 * 1024),
        name="squeeze",
    )(index, frames_in, weight, start)


def block_frames_of(index_ref, refs):
    place, has_low, has_high = [index_ref[k] for k in range(3)]
    odd, upper = place % 2 == 1, place // 2 == 1
    parts = [ref[...].astype(wide) for ref in refs]
    low = [jnp.where(odd, parts[j ^ 1], parts[j]) for j in range(block_frames)]
    full = [jnp.where(upper, low[j ^ 2], low[j]) for j in range(block_frames)]
    before = jnp.where(has_low > 0, parts[block_frames], 0.0)
    behind = jnp.where(has_high > 0, parts[block_frames + 1], 0.0)
    return [before] + full + [behind]


def mix_grad_kernel(index_ref, taps_ref, *refs):
    earlier, same, later = [taps_ref[k : k + 1, :] for k in range(3)]
    per_core = block_frames + 2
    for side in range(cores):
        grads = block_frames_of(index_ref, refs[side * per_core : (side + 1) * per_core])
        for f in range(block_frames):
            mixed = earlier * grads[f + 2] + same * grads[f + 1] + later * grads[f]
            refs[-1][side, f ^ index_ref[0]] = mixed.astype(narrow)


def mix_conv_kernel(index_ref, taps_ref, grad_ref, *refs):
    earlier, same, later = [taps_ref[k : k + 1, :] for k in range(3)]
    per_core = block_frames + 2
    *inputs, conv_ref, small_ref = refs
    sums = [0.0] * 4
    for side in range(cores):
        bottles = block_frames_of(index_ref, inputs[side * per_core : (side + 1) * per_core])
        grads = inputs[cores * per_core + side * block_frames :][:block_frames]
        for f in range(block_frames):
            down, here, up = bottles[f : f + 3]
            conv_ref[side, f ^ index_ref[0]] = (
                earlier * down + same * here + later * up
            ).astype(narrow)
        for step in range(block_frames):
            grad = grads[step][...].astype(wide)
            f = index_ref[0] ^ step
            mixed = grad_ref[side, step].astype(wide)
            near = [
                sum(jnp.where(f == j, bottles[j + k], 0.0) for j in range(block_frames))
                for k in range(3)
            ]
            for k, value in enumerate([v * grad for v in near] + [mixed]):
                sums[k] = sums[k] + jnp.sum(value, axis=0, keepdims=True)
    small_ref[...] = jnp.zeros_like(small_ref)
    for k in range(4):
        small_ref[k : k + 1, :] = sums[k]


def mix(index, taps, parts, grad_rows=None):
    tokens, channels = parts[0].shape
    vmem = pl.BlockSpec(memory_space=pltpu.VMEM)
    rows = jax.ShapeDtypeStruct((cores, block_frames, tokens, channels), narrow)
    last = grad_rows is None
    operands = list(parts) if last else [grad_rows, *parts]
    return pl.pallas_call(
        mix_grad_kernel if last else mix_conv_kernel,
        out_shape=rows if last else (rows, jax.ShapeDtypeStruct((8, channels), wide)),
        in_specs=[pl.BlockSpec(memory_space=pltpu.SMEM)] + [vmem] * (1 + len(operands)),
        out_specs=vmem if last else (vmem, vmem),
        compiler_params=pltpu.CompilerParams(vmem_limit_bytes=24 * 1024 * 1024),
        name="mix_grad" if last else "mix_conv",
    )(index, taps, *operands)


def contract_kernel(targets_ref, rows_ref, small_ref, *refs):
    own, other = refs[:block_frames], refs[block_frames:members]
    total_ref, bias_ref, *sent_refs = refs[members:-1]
    extra_ref = refs[-1]
    share, channels = total_ref.shape

    def product(target):
        total = jnp.zeros((share, channels), wide)
        bias = jnp.zeros((1, share), wide)
        for step in range(block_frames):
            for side, value in ((0, own[step][0, target]), (1, other[step][target])):
                total = total + inner_rows(value, rows_ref[side, step])
                bias = bias + jnp.sum(value.astype(wide), axis=0, keepdims=True)
        return total, bias

    for index, sent_ref in enumerate(sent_refs):
        total, bias = product(targets_ref[index + 1])
        sent_ref[:share, :] = total.astype(narrow)
        if small_ref is not None:
            extra_ref[...] = jnp.zeros_like(extra_ref)
            extra_ref[0:4, :] = small_ref[0:4, :]
            extra_ref[4:5, :share] = bias
            high = extra_ref[0:8, :].astype(narrow).astype(wide)
            extra_ref[8:16, :] = extra_ref[0:8, :] - high
            sent_ref[share:, :] = extra_ref[...].astype(narrow)
    total_ref[...], bias_ref[...] = product(targets_ref[0])


def contract(targets, rows, small, parts):
    share, channels = parts[0].shape[-1], rows.shape[-1]
    blocks = parts[0].shape[1]
    vmem = pl.BlockSpec(memory_space=pltpu.VMEM)
    body = contract_kernel
    operands = [targets, rows] + ([] if small is None else [small]) + list(parts)
    if small is None:
        body = lambda targets_ref, rows_ref, *refs: contract_kernel(
            targets_ref, rows_ref, None, *refs
        )
    sent = jax.ShapeDtypeStruct((share + (0 if small is None else 16), channels), narrow)
    return pl.pallas_call(
        body,
        out_shape=(
            jax.ShapeDtypeStruct((share, channels), wide),
            jax.ShapeDtypeStruct((1, share), wide),
        )
        + (sent,) * (blocks - 1),
        in_specs=[pl.BlockSpec(memory_space=pltpu.SMEM)] + [vmem] * (len(operands) - 1),
        out_specs=(vmem,) * (blocks + 1),
        scratch_shapes=[pltpu.VMEM((16, channels), wide)],
        compiler_params=pltpu.CompilerParams(vmem_limit_bytes=24 * 1024 * 1024),
        name="contract_down" if small is None else "contract_up",
    )(*operands)


def after(values, other):
    return list(lax.optimization_barrier((tuple(values), other))[0])


def local(frames_in, cotangent, down_weight, down_bias, conv_kernel, up_weight, up_bias, ln_gain):
    tokens, features = frames_in.shape
    channels = down_weight.shape[1]
    count = lax.axis_size("tm")
    blocks = count // block_frames
    share = features // (count * cores)
    frame, core = lax.axis_index("tm"), lax.axis_index("tensor")
    block, place = frame // block_frames, frame % block_frames
    groups = [
        list(range(start, start + members)) for start in range(0, count * cores, members)
    ]

    def core_swap(value):
        return lax.ppermute(value, "tensor", [(0, 1), (1, 0)])

    def block_swap(value, step):
        return lax.ppermute(value, "tm", [(i, i ^ step) for i in range(count)])

    def to_members(value):
        return lax.all_to_all(
            value,
            ("tm", "tensor"),
            split_axis=0,
            concat_axis=0,
            tiled=True,
            axis_index_groups=groups,
        )

    def edge_swap(value):
        edges = range(block_frames - 1, count - 1, block_frames)
        return lax.ppermute(
            value, "tm", [p for i in edges for p in ((i, i + 1), (i + 1, i))]
        )

    def across(value, step):
        return lax.ppermute(
            value, "tm", [(i, (i + step * block_frames) % count) for i in range(count)]
        )

    def shifted(value, step):
        pairs = [(i, i + step * block_frames) for i in range(count)]
        return lax.ppermute(value, "tm", [p for p in pairs if 0 <= p[1] < count])

    def ordered(parts):
        low = [
            jnp.where(place % 2 == 1, parts[j ^ 1], parts[j]) for j in range(block_frames)
        ]
        return [jnp.where(place // 2 == 1, low[j ^ 2], low[j]) for j in range(block_frames)]

    index = jnp.stack([core, place]).astype(jnp.int32)
    down_other = core_swap(down_weight)
    frames_parts = list(
        split(index, frames_in, blocks, share)
    )
    index_after = after([index], frames_parts[3])[0]
    for step in (1, 2):
        frames_parts[step] = block_swap(frames_parts[step], step)
    bottle = squeeze(index_after, frames_in, down_weight, down_bias[None], 0, wide)
    bottle = squeeze(index, frames_in, down_other, bottle, 1, narrow)
    up_other = core_swap(up_weight)
    bottle_parts = [bottle] + [block_swap(bottle, step) for step in range(1, block_frames)]
    bottle_edge = edge_swap(bottle)
    frames_parts[3] = block_swap(
        after([frames_parts[3]], (bottle_parts[1:], bottle_edge))[0], 3
    )

    def pick(value, *places):
        chosen = sum([(place == p) for p in places[1:]], place == places[0])
        return jnp.where(chosen, value, 0.0)

    earlier, same, later = conv_kernel
    odd = place % 2 == 1
    conv = (
        jnp.where(odd, earlier, later) * bottle_parts[1].astype(wide)
        + same * bottle.astype(wide)
        + (pick(later, 1) + pick(earlier, 2)) * bottle_parts[3].astype(wide)
        + (pick(earlier, 0) + pick(later, 3)) * bottle_edge.astype(wide)
    ).astype(narrow)
    out_tokens, *grad_sent, grad_conv = lift(
        index,
        frames_in,
        cotangent,
        conv,
        up_weight,
        up_other,
        up_bias,
        ln_gain,
        blocks,
        share,
    )
    grad_conv, *grad_sent = after([grad_conv, *grad_sent], frames_parts[1:])
    grad_parts = [grad_conv] + [block_swap(grad_conv, step) for step in range(1, block_frames)]
    grad_sent = after(grad_sent, grad_parts[1])
    lifted_parts = [grad_sent[0]] + [
        block_swap(grad_sent[step], step) for step in range(1, block_frames)
    ]

    def by_core(parts):
        return list(parts) + [core_swap(v[1]) for v in parts]

    frames_got = by_core(after(frames_parts, grad_parts[1]))

    def whole_block(parts):
        if blocks == 2:
            beside = across(
                lax.select_n(jnp.where(block == 0, block_frames - 1, 0) ^ place, *parts), 1
            )
            sides = [beside, beside]
        else:
            frames = ordered(parts)
            sides = [shifted(frames[-1], 1), shifted(frames[0], -1)]
        own = list(parts) + sides[: 1 if blocks == 2 else 2]
        other = [core_swap(value) for value in own]
        return own[:block_frames] + sides, other[:block_frames] + [other[block_frames], other[-1]]

    grad_own, grad_other = whole_block(grad_parts)
    ends = jnp.stack([place, block, blocks - 1 - block]).astype(jnp.int32)
    grad_bottle = mix(ends, conv_kernel, after(grad_own + grad_other, lifted_parts[1:3]))
    targets = jnp.stack([(block + step) % blocks for step in range(blocks)]).astype(jnp.int32)
    grad_down, _, *down_sent = contract(targets, grad_bottle, None, frames_got)
    down_sent = after(down_sent, lifted_parts[3])
    down_got = [across(value, step + 1) for step, value in enumerate(down_sent)]
    bottle_own, bottle_other = whole_block(after(bottle_parts, lifted_parts[2]))
    conv_rows, small = mix(
        ends,
        conv_kernel,
        bottle_own + bottle_other + grad_own[:block_frames] + grad_other[:block_frames],
        grad_bottle,
    )
    grad_up, grad_up_bias, *up_sent = contract(targets, conv_rows, small, by_core(lifted_parts))
    up_got = [across(value, step + 1) for step, value in enumerate(up_sent)]
    down_got = after(down_got, up_sent[0])
    grad_up_bias, small = grad_up_bias[0], small[:5]
    small = small.at[4, :share].set(grad_up_bias)
    for down, up in zip(down_got, up_got):
        down, up = down.astype(wide), up.astype(wide)
        grad_down = grad_down + down[:share]
        grad_up = grad_up + up[:share]
        small = small + up[share : share + 5] + up[share + 8 : share + 13]
    grad_up_bias = small[4, :share]
    return (out_tokens, grad_down, grad_up, grad_up_bias, small[3], small[:3])


def solution(mesh):
    tokens = P(("groups", "tm", "tensor"), None)
    return jax.shard_map(
        local,
        mesh=mesh,
        in_specs=(tokens, tokens, P("tensor", None), P(), P(), P("tensor", None), P(), P()),
        out_specs=(
            tokens,
            tokens,
            tokens,
            P(("groups", "tm", "tensor")),
            P("groups"),
            P("groups", None),
        ),
        check_vma=False,
    )
```

time: 279 us -> 106 us (0.38)
  waiting for transfers between devices: 161 us -> 33.7 us
  blocking collectives: 62.7 us -> 0 us
  Pallas kernels: 0 us -> 22.9 us
  starting transfers between devices: 11.8 us -> 30.6 us
  between operations: 14.6 us -> 0.93 us
  matrix products: 11.2 us -> 0 us
  other arithmetic: 11.3 us -> 3.12 us
  local copies, waits for them, and re-layouts: 6.25 us -> 14.1 us
    reduce_scatter x1 -> x0, waiting for transfers between devices: 132 us -> none  [local(): lax.psum_scatter(jnp.concatenate([inner_rows(grad_lifted, conv), inner_ro...]
    unnamed x1 -> x0, blocking collectives: 62.7 us -> none
    ppermute x4 -> x37, waiting for transfers between devices: 5.1 us -> 33.7 us  [the longest x4 17.7 us: across(): lax.ppermute(value, 'tm', [(i, (i + step * block_frames) % count) for i i...]
    pallas_call x0 -> x8, Pallas kernels: none -> 22.9 us  [the longest x1 9.57 us: lift(): pl.pallas_call(lift_kernel, out_shape=(jax.ShapeDtypeStruct((tokens, feat...]
    all_gather x2 -> x0, waiting for transfers between devices: 22.6 us -> none  [the longest x1 18 us: local(): lax.all_gather(down_weight, 'tensor', axis=0, tiled=True)]
    ppermute x4 -> x37, starting transfers between devices: 11.7 us -> 30.6 us  [the longest x12 18.6 us: block_swap(): return lax.ppermute(value, 'tm', [(i, i ^ step) for i in range(count)])]
    dot_general x5 -> x0, matrix products: 11.2 us -> none  [the longest x1 4.01 us: outer_rows(): lax.dot_general(left, right, (((1,), (1,)), ((), ())), preferred_element_...]
    concatenate x1 -> x0, other arithmetic: 6.88 us -> none  [local(): jnp.concatenate([inner_rows(grad_lifted, conv), inner_rows(frames_in, gra...]
  transfers between devices with their start and end apart: 7 -> 37, of which waited for: 6 -> 11; matrix products, arithmetic and copies ran while one was open for 2% -> 6% of each run, Pallas kernels for 0% -> 22%
where the time goes in v2:
time: 106 us; the launch traced here: 105 us
  waiting for transfers between devices  33.7 us (32%)
  starting transfers between devices  30.6 us (29%)
  Pallas kernels  22.9 us (22%)
  local copies, waits for them, and re-layouts  14.1 us (13%)
  other arithmetic  3.12 us (3%)
    ppermute x12, starting transfers between devices, block_swap(): return lax.ppermute(value, 'tm', [(i, i ^ step) for i in range(count)])  18.6 us
    ppermute x4, waiting for transfers between devices, across(): lax.ppermute(value, 'tm', [(i, (i + step * block_frames) % count) for i i...  17.7 us
    ppermute x12, waiting for transfers between devices, block_swap(): return lax.ppermute(value, 'tm', [(i, i ^ step) for i in range(count)])  14.4 us
    pallas_call x1, Pallas kernels, lift(): pl.pallas_call(lift_kernel, out_shape=(jax.ShapeDtypeStruct((tokens, feat...  9.57 us
    unnamed x26, local copies, waits for them, and re-layouts  9.22 us
    ppermute x4, starting transfers between devices, across(): lax.ppermute(value, 'tm', [(i, (i + step * block_frames) % count) for i i...  6.33 us
    pallas_call x2, Pallas kernels, contract(): pl.pallas_call(body, out_shape=(jax.ShapeDtypeStruct((share, channels), w...  5.13 us
    ppermute x20, starting transfers between devices, core_swap(): return lax.ppermute(value, 'tensor', [(0, 1), (1, 0)])  4.33 us
  transfers between devices with their start and end apart: 37, of which 11 were waited for; matrix products, arithmetic and copies ran while one was open for 6% of the time, Pallas kernels for 22%

profile of v2, /device:TPU:0, one launch (start us, length us, event | category | flops | bytes accessed | tf_op | source)
XLA Modules:
  0.0 105.4 jit_solution(8326410763951341025)
XLA Ops:
  0.6 0.5 collective-permute-start
  1.1 0.1 collective-permute-start.4
  1.3 1.4 %copy-done = bf16[128,6144]{1,0:T(8,128)(2,1)S(1)} copy-done((bf16[128,6144]{1,0:T(8,128)(2,1)S(1)}, bf16[128,6144]{1,0:T(8,128)(2,1)}, u32[]{:S(2)}) %copy-start) | copy-done | bytes 1572888
  2.7 0.8 split.1
  3.5 0.7 copy-done.5
  4.2 0.8 copy-done.10
  5.0 0.7 copy-done.11
  5.7 0.7 copy-done.12
  6.5 0.7 broadcast_in_dim.19.start_ref
  7.2 1.7 %copy-done.2 = bf16[3072,384]{1,0:T(8,128)(2,1)S(1)} copy-done((bf16[3072,384]{1,0:T(8,128)(2,1)S(1)}, bf16[3072,384]{1,0:T(8,128)(2,1)}, u32[]{:S(2)}) %copy-start.2) | copy-done | bytes 2359320
  8.8 1.1 %squeeze.43.start_ref = f32[128,384]{1,0:T(8,128)S(1)} custom-call(s32[2]{0:T(128)S(1)} %pad_add_fusion.index_ref, bf16[128,6144]{1,0:T(8,128)(2,1)S(1)} %copy-done.1, bf16[3072,384]{1,0:T(8,128)(2,1)S(1)} %copy-done.2, f32[1,384]{1,0:T(1,128)S(1)} %broadcast_in_dim.19.start_ref), custom_call_target="tpu_custom_call" | custom-call | tf_op jit(solution)/shard_map/squeeze/pallas_call | solution.py:173
  10.0 2.4 %squeeze.44.refs_0_ = bf16[128,384]{1,0:T(8,128)(2,1)S(1)} custom-call(s32[2]{0:T(128)S(1)} %pad_add_fusion.index_ref, bf16[128,6144]{1,0:T(8,128)(2,1)S(1)} %copy-done.1, bf16[3072,384]{1,0:T(8,128)(2,1)} %collective-permute-done.weight_ref, f32[128,384]{1,0:T(8,128)S(1)} %squeeze.43.start_ref), custom_call_target="tpu_custom_call" | custom-call | tf_op jit(solution)/shard_map/squeeze/pallas_call | solution.py:173
  12.4 3.0 %collective-permute-start.1 = (bf16[128,384]{1,0:T(8,128)(2,1)S(1)}, bf16[128,384]{1,0:T(8,128)(2,1)S(1)}, u32[]{:S(2)}, u32[]{:S(2)}) collective-permute-start(bf16[128,384]{1,0:T(8,128)(2,1)S(1)} %squeeze.44.refs_0_), channel_id=1, source_target_pairs={{0,2},{2,0},{4,6},{6,4},{8,10},{10,8},{12,14},{14,12},{1,3},{3,1},... | collective-permute-start | bytes 294920 | tf_op jit(solution)/shard_map/ppermute | solution.py:322
  15.4 1.5 %collective-permute-start.2 = (bf16[128,384]{1,0:T(8,128)(2,1)S(1)}, bf16[128,384]{1,0:T(8,128)(2,1)S(1)}, u32[]{:S(2)}, u32[]{:S(2)}) collective-permute-start(bf16[128,384]{1,0:T(8,128)(2,1)S(1)} %squeeze.44.refs_0_), channel_id=1, source_target_pairs={{0,6},{2,4},{4,2},{6,0},{8,14},{10,12},{12,10},{14,8},{1,7},{3,5},... | collective-permute-start | bytes 294920 | tf_op jit(solution)/shard_map/ppermute | solution.py:322
  16.9 1.3 %collective-permute-start.3 = (bf16[128,384]{1,0:T(8,128)(2,1)S(1)}, bf16[128,384]{1,0:T(8,128)(2,1)}, u32[]{:S(2)}, u32[]{:S(2)}) collective-permute-start(bf16[128,384]{1,0:T(8,128)(2,1)S(1)} %squeeze.44.refs_0_), channel_id=1, source_target_pairs={{6,8},{8,6},{7,9},{9,7},{22,24},{24,22},{23,25},{25,23}} | collective-permute-start | bytes 294920 | tf_op jit(solution)/shard_map/ppermute | solution.py:336
  18.3 1.5 %collective-permute-done.1.refs_1_ = bf16[128,384]{1,0:T(8,128)(2,1)S(1)} collective-permute-done((bf16[128,384]{1,0:T(8,128)(2,1)S(1)}, bf16[128,384]{1,0:T(8,128)(2,1)S(1)}, u32[]{:S(2)}, u32[]{:S(2)}) %collective-permute-start.1) | collective-permute-done | bytes 98336 | tf_op jit(solution)/shard_map/ppermute | solution.py:322
  19.8 3.7 %collective-permute-start.5 = (bf16[2,2,128,384]{3,2,1,0:T(8,128)(2,1)}, bf16[2,2,128,384]{3,2,1,0:T(8,128)(2,1)}, u32[]{:S(2)}, u32[]{:S(2)}) collective-permute-start(bf16[2,2,128,384]{3,2,1,0:T(8,128)(2,1)} %copy-done.12), channel_id=1, source_target_pairs={{0,2},{2,0},{4,6},{6,4},{8,10},{10,8},{12,14},{14,12},{1,3},{3,1},... | collective-permute-start | bytes 1179656 | tf_op jit(solution)/shard_map/ppermute | solution.py:322
  23.5 1.4 %collective-permute-start.6 = (bf16[2,2,128,384]{3,2,1,0:T(8,128)(2,1)}, bf16[2,2,128,384]{3,2,1,0:T(8,128)(2,1)}, u32[]{:S(2)}, u32[]{:S(2)}) collective-permute-start(bf16[2,2,128,384]{3,2,1,0:T(8,128)(2,1)} %copy-done.11), channel_id=1, source_target_pairs={{0,4},{2,6},{4,0},{6,2},{8,12},{10,14},{12,8},{14,10},{1,5},{3,7},... | collective-permute-start | bytes 1179656 | tf_op jit(solution)/shard_map/ppermute | solution.py:322
  24.9 3.8 %collective-permute-start.8 = (bf16[2,2,128,384]{3,2,1,0:T(8,128)(2,1)}, bf16[2,2,128,384]{3,2,1,0:T(8,128)(2,1)}, u32[]{:S(2)}, u32[]{:S(2)}) collective-permute-start(bf16[2,2,128,384]{3,2,1,0:T(8,128)(2,1)} %copy-done.10), channel_id=1, source_target_pairs={{0,6},{2,4},{4,2},{6,0},{8,14},{10,12},{12,10},{14,8},{1,7},{3,5},... | collective-permute-start | bytes 1179656 | tf_op jit(solution)/shard_map/ppermute | solution.py:322
  28.8 1.0 add_convert_fusion.conv_ref
  29.8 1.7 %copy-done.3 = bf16[3072,384]{1,0:T(8,128)(2,1)S(1)} copy-done((bf16[3072,384]{1,0:T(8,128)(2,1)S(1)}, bf16[3072,384]{1,0:T(8,128)(2,1)}, u32[]{:S(2)}) %copy-start.3) | copy-done | bytes 2359320
  31.5 0.7 copy-done.8
  32.2 0.7 copy-done.9
  32.9 9.6 %lift.1 = (bf16[128,6144]{1,0:T(8,128)(2,1)}, bf16[2,2,128,384]{3,2,1,0:T(8,128)(2,1)S(1)}, bf16[2,2,128,384]{3,2,1,0:T(8,128)(2,1)S(1)}, bf16[2,2,128,384]{3,2,...) custom-call(s32[2]{0:T(128)S(1)} %pad_add_fusion.index_ref, ...), custom_call_target="tpu_custom_call" | custom-call | tf_op jit(solution)/shard_map/lift/pallas_call | solution.py:115
  42.5 0.9 collective-permute-start.9
  43.4 0.4 collective-permute-start.10
  43.8 2.2 %collective-permute-start.11 = (bf16[128,384]{1,0:T(8,128)(2,1)S(1)}, bf16[128,384]{1,0:T(8,128)(2,1)S(1)}, u32[]{:S(2)}, u32[]{:S(2)}) collective-permute-start(bf16[128,384]{1,0:T(8,128)(2,1)S(1)} %get-tuple-element.86.refs_0_.refs_12_), channel_id=1, source_target_pairs={{0,6},{2,4},{4,2},{6,0},{8,14},{10,12},{12,10},{14,8},{1,7},{3,5},... | collective-permute-start | bytes 294920 | tf_op jit(solution)/shard_map/ppermute | solution.py:322
  46.1 2.1 %collective-permute-done.9.refs_1_.refs_13_ = bf16[128,384]{1,0:T(8,128)(2,1)S(1)} collective-permute-done((bf16[128,384]{1,0:T(8,128)(2,1)S(1)}, bf16[128,384]{1,0:T(8,128)(2,1)S(1)}, u32[]{:S(2)}, u32[]{:S(2)}) %collective-permute-start.9) | collective-permute-done | bytes 98336 | tf_op jit(solution)/shard_map/ppermute | solution.py:322
  48.2 0.9 collective-permute-start.19
  49.1 0.7 collective-permute-done.11.refs_3_.refs_15_
  49.9 1.6 %collective-permute-start.12 = (bf16[128,384]{1,0:T(8,128)(2,1)S(1)}, bf16[128,384]{1,0:T(8,128)(2,1)S(1)}, u32[]{:S(2)}, u32[]{:S(2)}) collective-permute-start(bf16[128,384]{1,0:T(8,128)(2,1)S(1)} %select_select_fusion.1), channel_id=1, source_target_pairs={{0,8},{2,10},{4,12},{6,14},{8,0},{10,2},{12,4},{14,6},{1,9},{3,11}... | collective-permute-start | bytes 294920 | tf_op jit(solution)/shard_map/ppermute | solution.py:341
  51.5 0.9 slice_bitcast_fusion.6
  52.5 0.9 slice_bitcast_fusion.5
  53.4 0.9 slice_bitcast_fusion.4
  54.5 6.0 %collective-permute-done.19.refs_2_ = bf16[2,2,128,384]{3,2,1,0:T(8,128)(2,1)S(1)} collective-permute-done((bf16[2,2,128,384]{3,2,1,0:T(8,128)(2,1)S(1)}, bf16[2,2,128,384]{3,2,1,0:T(8,128)(2,1)S(1)}, u32[]{:S(2)}, u32[]{:S(2)}) %collective-permute-start.19) | collective-permute-done | bytes 393248 | tf_op jit(solution)/shard_map/ppermute | solution.py:322
  60.4 0.5 collective-permute-start.16
  61.0 0.7 collective-permute-start.24
  61.7 0.4 collective-permute-start.21
  62.3 1.2 %collective-permute-done.17.refs_10_.refs_11_ = bf16[128,384]{1,0:T(8,128)(2,1)S(1)} collective-permute-done((bf16[128,384]{1,0:T(8,128)(2,1)S(1)}, bf16[128,384]{1,0:T(8,128)(2,1)S(1)}, u32[]{:S(2)}, u32[]{:S(2)}) %collective-permute-start.17) | collective-permute-done | bytes 98336 | tf_op jit(solution)/shard_map/ppermute | solution.py:319
  63.5 0.2 collective-permute-start.22
  63.8 0.3 collective-permute-start.23
  64.0 0.2 collective-permute-start.27
  64.3 1.8 %collective-permute-start.26 = (bf16[128,384]{1,0:T(8,128)(2,1)S(1)}, bf16[128,384]{1,0:T(8,128)(2,1)S(1)}, u32[]{:S(2)}, u32[]{:S(2)}) collective-permute-start(bf16[128,384]{1,0:T(8,128)(2,1)S(1)} %select_select_fusion), channel_id=1, source_target_pairs={{0,8},{2,10},{4,12},{6,14},{8,0},{10,2},{12,4},{14,6},{1,9},{3,11}... | collective-permute-start | bytes 294920 | tf_op jit(solution)/shard_map/ppermute | solution.py:341
  66.1 1.1 %mix_grad.1.rows_ref.grad_ref = bf16[2,4,128,384]{3,2,1,0:T(8,128)(2,1)S(1)} custom-call(s32[3]{0:T(128)S(1)} %pad_add_fusion.2.index_ref, f32[3,384]{1,0:T(4,128)S(1)} %copy-done.7, bf16[128,384]{1,0:T(8,128)(2,1)S(1)} %get-tuple-element.86.refs_0_.refs_12_, bf16[128,384]{1,0:T(8,128)(2,1)S(1)} %collective-permute-done.9.refs_1_.refs_13_, ...), custom_call_target="tpu_custom_call" | custom-call | tf_op jit(solution)/shard_map/mix_grad/pallas_call | solution.py:238
  67.3 0.5 collective-permute-start.29
  67.8 3.2 %contract_down.1 = (f32[384,384]{1,0:T(8,128)S(1)}, f32[1,384]{1,0:T(1,128)}, bf16[384,384]{1,0:T(8,128)(2,1)S(1)}) custom-call(s32[2]{0:T(128)S(1)} %pad_add_fusion.1.targets_ref, bf16[2,4,128,384]{3,2,1,0:T(8,128)(2,1)S(1)} %mix_grad.1.rows_ref.grad_ref, bf16[2,2,128,384]{3,2,1,0:T(8,128)(2,1)S(1)} %copy-done.6, ...), custom_call_target="tpu_custom_call" | custom-call | tf_op jit(solution)/shard_map/contract_down/pallas_call | solution.py:287
  70.9 4.1 %collective-permute-done.24.refs_3_ = bf16[2,2,128,384]{3,2,1,0:T(8,128)(2,1)S(1)} collective-permute-done((bf16[2,2,128,384]{3,2,1,0:T(8,128)(2,1)S(1)}, bf16[2,2,128,384]{3,2,1,0:T(8,128)(2,1)S(1)}, u32[]{:S(2)}, u32[]{:S(2)}) %collective-permute-start.24) | collective-permute-done | bytes 393248 | tf_op jit(solution)/shard_map/ppermute | solution.py:322
  75.1 0.3 collective-permute-start.25
  75.4 0.3 collective-permute-start.31
  75.7 0.3 collective-permute-start.32
  76.0 0.3 collective-permute-start.33
  76.3 0.1 collective-permute-done.30.refs_9_
  76.4 0.2 collective-permute-start.34
  76.5 0.1 collective-permute-done.31.refs_10_.refs_11_
  76.7 0.3 collective-permute-start.35
  77.0 2.9 %mix_conv.1 = (bf16[2,4,128,384]{3,2,1,0:T(8,128)(2,1)S(1)}, f32[8,384]{1,0:T(8,128)S(1)}) custom-call(s32[3]{0:T(128)S(1)} %pad_add_fusion.2.index_ref, f32[3,384]{1,0:T(4,128)S(1)} %copy-done.7, bf16[2,4,128,384]{3,2,1,0:T(8,128)(2,1)S(1)} %mix_grad.1.rows_ref.grad_ref, bf16[128,384]{1,0:T(8,128)(2,1)S(1)} %squeeze.44.refs_0_, ...), custom_call_target="tpu_custom_call" | custom-call | tf_op jit(solution)/shard_map/mix_conv/pallas_call | solution.py:238
  79.9 2.0 %contract_up.1 = (f32[384,384]{1,0:T(8,128)S(1)}, f32[1,384]{1,0:T(1,128)S(1)}, bf16[400,384]{1,0:T(8,128)(2,1)S(1)}) custom-call(s32[2]{0:T(128)S(1)} %pad_add_fusion.1.targets_ref, bf16[2,4,128,384]{3,2,1,0:T(8,128)(2,1)S(1)} %get-tuple-element.111.rows_ref, f32[8,384]{1,0:T(8,128)S(1)} %get-tuple-element.112.small_ref, ...), custom_call_target="tpu_custom_call" | custom-call | tf_op jit(solution)/shard_map/contract_up/pallas_call | solution.py:287
  81.9 2.6 %collective-permute-start.36 = (bf16[400,384]{1,0:T(8,128)(2,1)S(1)}, bf16[400,384]{1,0:T(8,128)(2,1)S(1)}, u32[]{:S(2)}, u32[]{:S(2)}) collective-permute-start(bf16[400,384]{1,0:T(8,128)(2,1)S(1)} %get-tuple-element.114), channel_id=1, source_target_pairs={{0,8},{2,10},{4,12},{6,14},{8,0},{10,2},{12,4},{14,6},{1,9},{3,11}... | collective-permute-start | bytes 921608 | tf_op jit(solution)/shard_map/ppermute | solution.py:341
  84.6 12.1 %collective-permute-done.25 = bf16[384,384]{1,0:T(8,128)(2,1)S(1)} collective-permute-done((bf16[384,384]{1,0:T(8,128)(2,1)S(1)}, bf16[384,384]{1,0:T(8,128)(2,1)S(1)}, u32[]{:S(2)}, u32[]{:S(2)}) %collective-permute-start.25) | collective-permute-done | bytes 294944 | tf_op jit(solution)/shard_map/ppermute | solution.py:341
  96.7 0.9 convert_add_fusion
  97.5 5.7 %collective-permute-done.36 = bf16[400,384]{1,0:T(8,128)(2,1)S(1)} collective-permute-done((bf16[400,384]{1,0:T(8,128)(2,1)S(1)}, bf16[400,384]{1,0:T(8,128)(2,1)S(1)}, u32[]{:S(2)}, u32[]{:S(2)}) %collective-permute-start.36) | collective-permute-done | bytes 307232 | tf_op jit(solution)/shard_map/ppermute | solution.py:341
  103.3 0.6 slice.83
  103.9 0.6 slice_reduce_fusion
  104.5 0.9 slice_add_fusion
  (67 shorter events, 1.1 us)
Async XLA Ops:
  0.6 9.4 %collective-permute-start = (bf16[3072,384]{1,0:T(8,128)(2,1)}, bf16[3072,384]{1,0:T(8,128)(2,1)}, u32[]{:S(2)}, u32[]{:S(2)}) collective-permute-start(bf16[3072,384]{1,0:T(8,128)(2,1)} %weight_ref.1), channel_id=1, source_target_pairs={{0,1},{1,0},{2,3},{3,2},{4,5},{5,4},{6,7},{7,6},{8,9},{9,8},{10,11... | collective-permute-start | bytes 7077896 | tf_op jit(solution)/shard_map/ppermute | solution.py:319
  1.1 28.6 %collective-permute-start.4 = (bf16[3072,384]{1,0:T(8,128)(2,1)}, bf16[3072,384]{1,0:T(8,128)(2,1)}, u32[]{:S(2)}, u32[]{:S(2)}) collective-permute-start(bf16[3072,384]{1,0:T(8,128)(2,1)} %own_ref.1), channel_id=1, source_target_pairs={{0,1},{1,0},{2,3},{3,2},{4,5},{5,4},{6,7},{7,6},{8,9},{9,8},{10,11... | collective-permute-start | bytes 7077896 | tf_op jit(solution)/shard_map/ppermute | solution.py:319
  1.3 1.4 %copy-start = (bf16[128,6144]{1,0:T(8,128)(2,1)S(1)}, bf16[128,6144]{1,0:T(8,128)(2,1)}, u32[]{:S(2)}) copy-start(bf16[128,6144]{1,0:T(8,128)(2,1)} %frames_ref.5) | copy-start | bytes 4718596
  2.7 4.5 %copy-start.1 = (bf16[128,6144]{1,0:T(8,128)(2,1)S(1)}, bf16[128,6144]{1,0:T(8,128)(2,1)}, u32[]{:S(2)}) copy-start(bf16[128,6144]{1,0:T(8,128)(2,1)} %frames_ref.5) | copy-start | bytes 4718596
  3.5 0.7 copy-start.5
  4.2 0.8 copy-start.10
  5.0 0.7 copy-start.11
  5.7 0.7 copy-start.12
  7.2 1.7 %copy-start.2 = (bf16[3072,384]{1,0:T(8,128)(2,1)S(1)}, bf16[3072,384]{1,0:T(8,128)(2,1)}, u32[]{:S(2)}) copy-start(bf16[3072,384]{1,0:T(8,128)(2,1)} %weight_ref.1) | copy-start | bytes 7077892
  10.0 18.8 %copy-start.7 = (f32[3,384]{1,0:T(4,128)S(1)}, f32[3,384]{1,0:T(4,128)}, u32[]{:S(2)}) copy-start(f32[3,384]{1,0:T(4,128)} %taps_ref.3) | copy-start | bytes 13828
  10.0 19.8 %copy-start.4 = (bf16[128,6144]{1,0:T(8,128)(2,1)S(1)}, bf16[128,6144]{1,0:T(8,128)(2,1)}, u32[]{:S(2)}) copy-start(bf16[128,6144]{1,0:T(8,128)(2,1)} %cotangent_ref.1) | copy-start | bytes 4718596
  12.4 7.4 %collective-permute-start.1 = (bf16[128,384]{1,0:T(8,128)(2,1)S(1)}, bf16[128,384]{1,0:T(8,128)(2,1)S(1)}, u32[]{:S(2)}, u32[]{:S(2)}) collective-permute-start(bf16[128,384]{1,0:T(8,128)(2,1)S(1)} %squeeze.44.refs_0_), channel_id=1, source_target_pairs={{0,2},{2,0},{4,6},{6,4},{8,10},{10,8},{12,14},{14,12},{1,3},{3,1},... | collective-permute-start | bytes 294920 | tf_op jit(solution)/shard_map/ppermute | solution.py:322
  15.4 8.1 %collective-permute-start.2 = (bf16[128,384]{1,0:T(8,128)(2,1)S(1)}, bf16[128,384]{1,0:T(8,128)(2,1)S(1)}, u32[]{:S(2)}, u32[]{:S(2)}) collective-permute-start(bf16[128,384]{1,0:T(8,128)(2,1)S(1)} %squeeze.44.refs_0_), channel_id=1, source_target_pairs={{0,6},{2,4},{4,2},{6,0},{8,14},{10,12},{12,10},{14,8},{1,7},{3,5},... | collective-permute-start | bytes 294920 | tf_op jit(solution)/shard_map/ppermute | solution.py:322
  16.9 8.0 %collective-permute-start.3 = (bf16[128,384]{1,0:T(8,128)(2,1)S(1)}, bf16[128,384]{1,0:T(8,128)(2,1)}, u32[]{:S(2)}, u32[]{:S(2)}) collective-permute-start(bf16[128,384]{1,0:T(8,128)(2,1)S(1)} %squeeze.44.refs_0_), channel_id=1, source_target_pairs={{6,8},{8,6},{7,9},{9,7},{22,24},{24,22},{23,25},{25,23}} | collective-permute-start | bytes 294920 | tf_op jit(solution)/shard_map/ppermute | solution.py:336
  18.2 6.7 %collective-permute-start.7 = (bf16[128,384]{1,0:T(8,128)(2,1)S(1)}, bf16[128,384]{1,0:T(8,128)(2,1)S(1)}, u32[]{:S(2)}, u32[]{:S(2)}) collective-permute-start(bf16[128,384]{1,0:T(8,128)(2,1)S(1)} %squeeze.44.refs_0_), channel_id=1, source_target_pairs={{0,4},{2,6},{4,0},{6,2},{8,12},{10,14},{12,8},{14,10},{1,5},{3,7},... | collective-permute-start | bytes 294920 | tf_op jit(solution)/shard_map/ppermute | solution.py:322
  19.8 22.7 %collective-permute-start.5 = (bf16[2,2,128,384]{3,2,1,0:T(8,128)(2,1)}, bf16[2,2,128,384]{3,2,1,0:T(8,128)(2,1)}, u32[]{:S(2)}, u32[]{:S(2)}) collective-permute-start(bf16[2,2,128,384]{3,2,1,0:T(8,128)(2,1)} %copy-done.12), channel_id=1, source_target_pairs={{0,2},{2,0},{4,6},{6,4},{8,10},{10,8},{12,14},{14,12},{1,3},{3,1},... | collective-permute-start | bytes 1179656 | tf_op jit(solution)/shard_map/ppermute | solution.py:322
  23.5 19.0 %collective-permute-start.6 = (bf16[2,2,128,384]{3,2,1,0:T(8,128)(2,1)}, bf16[2,2,128,384]{3,2,1,0:T(8,128)(2,1)}, u32[]{:S(2)}, u32[]{:S(2)}) collective-permute-start(bf16[2,2,128,384]{3,2,1,0:T(8,128)(2,1)} %copy-done.11), channel_id=1, source_target_pairs={{0,4},{2,6},{4,0},{6,2},{8,12},{10,14},{12,8},{14,10},{1,5},{3,7},... | collective-permute-start | bytes 1179656 | tf_op jit(solution)/shard_map/ppermute | solution.py:322
  24.9 17.6 %collective-permute-start.8 = (bf16[2,2,128,384]{3,2,1,0:T(8,128)(2,1)}, bf16[2,2,128,384]{3,2,1,0:T(8,128)(2,1)}, u32[]{:S(2)}, u32[]{:S(2)}) collective-permute-start(bf16[2,2,128,384]{3,2,1,0:T(8,128)(2,1)} %copy-done.10), channel_id=1, source_target_pairs={{0,6},{2,4},{4,2},{6,0},{8,14},{10,12},{12,10},{14,8},{1,7},{3,5},... | collective-permute-start | bytes 1179656 | tf_op jit(solution)/shard_map/ppermute | solution.py:322
  29.8 1.7 %copy-start.3 = (bf16[3072,384]{1,0:T(8,128)(2,1)S(1)}, bf16[3072,384]{1,0:T(8,128)(2,1)}, u32[]{:S(2)}) copy-start(bf16[3072,384]{1,0:T(8,128)(2,1)} %own_ref.1) | copy-start | bytes 7077892
  31.5 0.7 copy-start.8
  32.2 0.7 copy-start.9
  32.9 18.6 %copy-start.6 = (bf16[2,2,128,384]{3,2,1,0:T(8,128)(2,1)S(1)}, bf16[2,2,128,384]{3,2,1,0:T(8,128)(2,1)}, u32[]{:S(2)}) copy-start(bf16[2,2,128,384]{3,2,1,0:T(8,128)(2,1)} %copy-done.5) | copy-start | bytes 1179652
  42.5 5.7 %collective-permute-start.9 = (bf16[128,384]{1,0:T(8,128)(2,1)S(1)}, bf16[128,384]{1,0:T(8,128)(2,1)S(1)}, u32[]{:S(2)}, u32[]{:S(2)}) collective-permute-start(bf16[128,384]{1,0:T(8,128)(2,1)S(1)} %get-tuple-element.86.refs_0_.refs_12_), channel_id=1, source_target_pairs={{0,2},{2,0},{4,6},{6,4},{8,10},{10,8},{12,14},{14,12},{1,3},{3,1},... | collective-permute-start | bytes 294920 | tf_op jit(solution)/shard_map/ppermute | solution.py:322
  43.4 5.7 %collective-permute-start.10 = (bf16[128,384]{1,0:T(8,128)(2,1)S(1)}, bf16[128,384]{1,0:T(8,128)(2,1)S(1)}, u32[]{:S(2)}, u32[]{:S(2)}) collective-permute-start(bf16[128,384]{1,0:T(8,128)(2,1)S(1)} %get-tuple-element.86.refs_0_.refs_12_), channel_id=1, source_target_pairs={{0,4},{2,6},{4,0},{6,2},{8,12},{10,14},{12,8},{14,10},{1,5},{3,7},... | collective-permute-start | bytes 294920 | tf_op jit(solution)/shard_map/ppermute | solution.py:322
  43.8 6.0 %collective-permute-start.11 = (bf16[128,384]{1,0:T(8,128)(2,1)S(1)}, bf16[128,384]{1,0:T(8,128)(2,1)S(1)}, u32[]{:S(2)}, u32[]{:S(2)}) collective-permute-start(bf16[128,384]{1,0:T(8,128)(2,1)S(1)} %get-tuple-element.86.refs_0_.refs_12_), channel_id=1, source_target_pairs={{0,6},{2,4},{4,2},{6,0},{8,14},{10,12},{12,10},{14,8},{1,7},{3,5},... | collective-permute-start | bytes 294920 | tf_op jit(solution)/shard_map/ppermute | solution.py:322
  46.1 14.3 %collective-permute-start.13 = (bf16[128,384]{1,0:T(8,128)(2,1)S(1)}, bf16[128,384]{1,0:T(8,128)(2,1)S(1)}, u32[]{:S(2)}, u32[]{:S(2)}) collective-permute-start(bf16[128,384]{1,0:T(8,128)(2,1)S(1)} %get-tuple-element.86.refs_0_.refs_12_), channel_id=1, source_target_pairs={{0,1},{1,0},{2,3},{3,2},{4,5},{5,4},{6,7},{7,6},{8,9},{9,8},{10,11... | collective-permute-start | bytes 294920 | tf_op jit(solution)/shard_map/ppermute | solution.py:319
  48.2 12.2 %collective-permute-start.19 = (bf16[2,2,128,384]{3,2,1,0:T(8,128)(2,1)S(1)}, bf16[2,2,128,384]{3,2,1,0:T(8,128)(2,1)S(1)}, u32[]{:S(2)}, u32[]{:S(2)}) collective-permute-start(bf16[2,2,128,384]{3,2,1,0:T(8,128)(2,1)S(1)} %get-tuple-element.85), channel_id=1, source_target_pairs={{0,4},{2,6},{4,0},{6,2},{8,12},{10,14},{12,8},{14,10},{1,5},{3,7},... | collective-permute-start | bytes 1179656 | tf_op jit(solution)/shard_map/ppermute | solution.py:322
  49.1 15.2 %collective-permute-start.18 = (bf16[2,2,128,384]{3,2,1,0:T(8,128)(2,1)S(1)}, bf16[2,2,128,384]{3,2,1,0:T(8,128)(2,1)S(1)}, u32[]{:S(2)}, u32[]{:S(2)}) collective-permute-start(bf16[2,2,128,384]{3,2,1,0:T(8,128)(2,1)S(1)} %get-tuple-element.84), channel_id=1, source_target_pairs={{0,2},{2,0},{4,6},{6,4},{8,10},{10,8},{12,14},{14,12},{1,3},{3,1},... | collective-permute-start | bytes 1179656 | tf_op jit(solution)/shard_map/ppermute | solution.py:322
  49.9 11.1 %collective-permute-start.12 = (bf16[128,384]{1,0:T(8,128)(2,1)S(1)}, bf16[128,384]{1,0:T(8,128)(2,1)S(1)}, u32[]{:S(2)}, u32[]{:S(2)}) collective-permute-start(bf16[128,384]{1,0:T(8,128)(2,1)S(1)} %select_select_fusion.1), channel_id=1, source_target_pairs={{0,8},{2,10},{4,12},{6,14},{8,0},{10,2},{12,4},{14,6},{1,9},{3,11}... | collective-permute-start | bytes 294920 | tf_op jit(solution)/shard_map/ppermute | solution.py:341
  54.4 7.3 %collective-permute-start.14 = (bf16[128,384]{1,0:T(8,128)(2,1)S(1)}, bf16[128,384]{1,0:T(8,128)(2,1)S(1)}, u32[]{:S(2)}, u32[]{:S(2)}) collective-permute-start(bf16[128,384]{1,0:T(8,128)(2,1)S(1)} %collective-permute-done.9.refs_1_.refs_13_), channel_id=1, source_target_pairs={{0,1},{1,0},{2,3},{3,2},{4,5},{5,4},{6,7},{7,6},{8,9},{9,8},{10,11... | collective-permute-start | bytes 294920 | tf_op jit(solution)/shard_map/ppermute | solution.py:319
  60.4 1.3 %collective-permute-start.15 = (bf16[128,384]{1,0:T(8,128)(2,1)S(1)}, bf16[128,384]{1,0:T(8,128)(2,1)S(1)}, u32[]{:S(2)}, u32[]{:S(2)}) collective-permute-start(bf16[128,384]{1,0:T(8,128)(2,1)S(1)} %collective-permute-done.10.refs_2_.refs_14_), channel_id=1, source_target_pairs={{0,1},{1,0},{2,3},{3,2},{4,5},{5,4},{6,7},{7,6},{8,9},{9,8},{10,11... | collective-permute-start | bytes 294920 | tf_op jit(solution)/shard_map/ppermute | solution.py:319
  60.4 1.7 %collective-permute-start.16 = (bf16[128,384]{1,0:T(8,128)(2,1)S(1)}, bf16[128,384]{1,0:T(8,128)(2,1)S(1)}, u32[]{:S(2)}, u32[]{:S(2)}) collective-permute-start(bf16[128,384]{1,0:T(8,128)(2,1)S(1)} %collective-permute-done.11.refs_3_.refs_15_), channel_id=1, source_target_pairs={{0,1},{1,0},{2,3},{3,2},{4,5},{5,4},{6,7},{7,6},{8,9},{9,8},{10,11... | collective-permute-start | bytes 294920 | tf_op jit(solution)/shard_map/ppermute | solution.py:319
  61.0 14.1 %collective-permute-start.24 = (bf16[2,2,128,384]{3,2,1,0:T(8,128)(2,1)S(1)}, bf16[2,2,128,384]{3,2,1,0:T(8,128)(2,1)S(1)}, u32[]{:S(2)}, u32[]{:S(2)}) collective-permute-start(bf16[2,2,128,384]{3,2,1,0:T(8,128)(2,1)S(1)} %get-tuple-element.105), channel_id=1, source_target_pairs={{0,6},{2,4},{4,2},{6,0},{8,14},{10,12},{12,10},{14,8},{1,7},{3,5},... | collective-permute-start | bytes 1179656 | tf_op jit(solution)/shard_map/ppermute | solution.py:322
  61.6 2.1 %collective-permute-start.20 = (bf16[2,128,384]{2,1,0:T(8,128)(2,1)S(1)}, bf16[2,128,384]{2,1,0:T(8,128)(2,1)S(1)}, u32[]{:S(2)}, u32[]{:S(2)}) collective-permute-start(bf16[2,128,384]{2,1,0:T(8,128)(2,1)S(1)} %slice_bitcast_fusion.7), channel_id=1, source_target_pairs={{0,1},{1,0},{2,3},{3,2},{4,5},{5,4},{6,7},{7,6},{8,9},{9,8},{10,11... | collective-permute-start | bytes 589832 | tf_op jit(solution)/shard_map/ppermute | solution.py:319
  61.7 2.3 %collective-permute-start.21 = (bf16[2,128,384]{2,1,0:T(8,128)(2,1)S(1)}, bf16[2,128,384]{2,1,0:T(8,128)(2,1)S(1)}, u32[]{:S(2)}, u32[]{:S(2)}) collective-permute-start(bf16[2,128,384]{2,1,0:T(8,128)(2,1)S(1)} %slice_bitcast_fusion.6), channel_id=1, source_target_pairs={{0,1},{1,0},{2,3},{3,2},{4,5},{5,4},{6,7},{7,6},{8,9},{9,8},{10,11... | collective-permute-start | bytes 589832 | tf_op jit(solution)/shard_map/ppermute | solution.py:319
  62.2 1.3 %collective-permute-start.17 = (bf16[128,384]{1,0:T(8,128)(2,1)S(1)}, bf16[128,384]{1,0:T(8,128)(2,1)S(1)}, u32[]{:S(2)}, u32[]{:S(2)}) collective-permute-start(bf16[128,384]{1,0:T(8,128)(2,1)S(1)} %collective-permute-done.12.refs_4_.refs_5_), channel_id=1, source_target_pairs={{0,1},{1,0},{2,3},{3,2},{4,5},{5,4},{6,7},{7,6},{8,9},{9,8},{10,11... | collective-permute-start | bytes 294920 | tf_op jit(solution)/shard_map/ppermute | solution.py:319
  63.5 3.7 %collective-permute-start.22 = (bf16[2,128,384]{2,1,0:T(8,128)(2,1)S(1)}, bf16[2,128,384]{2,1,0:T(8,128)(2,1)S(1)}, u32[]{:S(2)}, u32[]{:S(2)}) collective-permute-start(bf16[2,128,384]{2,1,0:T(8,128)(2,1)S(1)} %slice_bitcast_fusion.5), channel_id=1, source_target_pairs={{0,1},{1,0},{2,3},{3,2},{4,5},{5,4},{6,7},{7,6},{8,9},{9,8},{10,11... | collective-permute-start | bytes 589832 | tf_op jit(solution)/shard_map/ppermute | solution.py:319
  63.8 3.5 %collective-permute-start.23 = (bf16[2,128,384]{2,1,0:T(8,128)(2,1)S(1)}, bf16[2,128,384]{2,1,0:T(8,128)(2,1)S(1)}, u32[]{:S(2)}, u32[]{:S(2)}) collective-permute-start(bf16[2,128,384]{2,1,0:T(8,128)(2,1)S(1)} %slice_bitcast_fusion.4), channel_id=1, source_target_pairs={{0,1},{1,0},{2,3},{3,2},{4,5},{5,4},{6,7},{7,6},{8,9},{9,8},{10,11... | collective-permute-start | bytes 589832 | tf_op jit(solution)/shard_map/ppermute | solution.py:319
  64.0 11.3 %collective-permute-start.27 = (bf16[128,384]{1,0:T(8,128)(2,1)S(1)}, bf16[128,384]{1,0:T(8,128)(2,1)S(1)}, u32[]{:S(2)}, u32[]{:S(2)}) collective-permute-start(bf16[128,384]{1,0:T(8,128)(2,1)S(1)} %squeeze.44.refs_0_), channel_id=1, source_target_pairs={{0,1},{1,0},{2,3},{3,2},{4,5},{5,4},{6,7},{7,6},{8,9},{9,8},{10,11... | collective-permute-start | bytes 294920 | tf_op jit(solution)/shard_map/ppermute | solution.py:319
  64.3 10.8 %collective-permute-start.26 = (bf16[128,384]{1,0:T(8,128)(2,1)S(1)}, bf16[128,384]{1,0:T(8,128)(2,1)S(1)}, u32[]{:S(2)}, u32[]{:S(2)}) collective-permute-start(bf16[128,384]{1,0:T(8,128)(2,1)S(1)} %select_select_fusion), channel_id=1, source_target_pairs={{0,8},{2,10},{4,12},{6,14},{8,0},{10,2},{12,4},{14,6},{1,9},{3,11}... | collective-permute-start | bytes 294920 | tf_op jit(solution)/shard_map/ppermute | solution.py:341
  67.2 8.5 %collective-permute-start.28 = (bf16[128,384]{1,0:T(8,128)(2,1)S(1)}, bf16[128,384]{1,0:T(8,128)(2,1)S(1)}, u32[]{:S(2)}, u32[]{:S(2)}) collective-permute-start(bf16[128,384]{1,0:T(8,128)(2,1)S(1)} %collective-permute-done.1.refs_1_), channel_id=1, source_target_pairs={{0,1},{1,0},{2,3},{3,2},{4,5},{5,4},{6,7},{7,6},{8,9},{9,8},{10,11... | collective-permute-start | bytes 294920 | tf_op jit(solution)/shard_map/ppermute | solution.py:319
  67.3 8.7 %collective-permute-start.29 = (bf16[128,384]{1,0:T(8,128)(2,1)S(1)}, bf16[128,384]{1,0:T(8,128)(2,1)S(1)}, u32[]{:S(2)}, u32[]{:S(2)}) collective-permute-start(bf16[128,384]{1,0:T(8,128)(2,1)S(1)} %collective-permute-done.7.refs_2_), channel_id=1, source_target_pairs={{0,1},{1,0},{2,3},{3,2},{4,5},{5,4},{6,7},{7,6},{8,9},{9,8},{10,11... | collective-permute-start | bytes 294920 | tf_op jit(solution)/shard_map/ppermute | solution.py:319
  75.1 1.3 %collective-permute-start.30 = (bf16[128,384]{1,0:T(8,128)(2,1)S(1)}, bf16[128,384]{1,0:T(8,128)(2,1)S(1)}, u32[]{:S(2)}, u32[]{:S(2)}) collective-permute-start(bf16[128,384]{1,0:T(8,128)(2,1)S(1)} %collective-permute-done.2.refs_3_), channel_id=1, source_target_pairs={{0,1},{1,0},{2,3},{3,2},{4,5},{5,4},{6,7},{7,6},{8,9},{9,8},{10,11... | collective-permute-start | bytes 294920 | tf_op jit(solution)/shard_map/ppermute | solution.py:319
  75.1 21.6 %collective-permute-start.25 = (bf16[384,384]{1,0:T(8,128)(2,1)S(1)}, bf16[384,384]{1,0:T(8,128)(2,1)S(1)}, u32[]{:S(2)}, u32[]{:S(2)}) collective-permute-start(bf16[384,384]{1,0:T(8,128)(2,1)S(1)} %get-tuple-element.106), channel_id=1, source_target_pairs={{0,8},{2,10},{4,12},{6,14},{8,0},{10,2},{12,4},{14,6},{1,9},{3,11}... | collective-permute-start | bytes 884744 | tf_op jit(solution)/shard_map/ppermute | solution.py:341
  75.4 1.3 %collective-permute-start.31 = (bf16[128,384]{1,0:T(8,128)(2,1)S(1)}, bf16[128,384]{1,0:T(8,128)(2,1)S(1)}, u32[]{:S(2)}, u32[]{:S(2)}) collective-permute-start(bf16[128,384]{1,0:T(8,128)(2,1)S(1)} %collective-permute-done.26.refs_4_.refs_5_), channel_id=1, source_target_pairs={{0,1},{1,0},{2,3},{3,2},{4,5},{5,4},{6,7},{7,6},{8,9},{9,8},{10,11... | collective-permute-start | bytes 294920 | tf_op jit(solution)/shard_map/ppermute | solution.py:319
  75.7 4.2 %collective-permute-start.32 = (bf16[2,128,384]{2,1,0:T(8,128)(2,1)S(1)}, bf16[2,128,384]{2,1,0:T(8,128)(2,1)S(1)}, u32[]{:S(2)}, u32[]{:S(2)}) collective-permute-start(bf16[2,128,384]{2,1,0:T(8,128)(2,1)S(1)} %slice_bitcast_fusion.3), channel_id=1, source_target_pairs={{0,1},{1,0},{2,3},{3,2},{4,5},{5,4},{6,7},{7,6},{8,9},{9,8},{10,11... | collective-permute-start | bytes 589832 | tf_op jit(solution)/shard_map/ppermute | solution.py:319
  76.0 3.9 %collective-permute-start.33 = (bf16[2,128,384]{2,1,0:T(8,128)(2,1)S(1)}, bf16[2,128,384]{2,1,0:T(8,128)(2,1)S(1)}, u32[]{:S(2)}, u32[]{:S(2)}) collective-permute-start(bf16[2,128,384]{2,1,0:T(8,128)(2,1)S(1)} %slice_bitcast_fusion.2), channel_id=1, source_target_pairs={{0,1},{1,0},{2,3},{3,2},{4,5},{5,4},{6,7},{7,6},{8,9},{9,8},{10,11... | collective-permute-start | bytes 589832 | tf_op jit(solution)/shard_map/ppermute | solution.py:319
  76.4 3.5 %collective-permute-start.34 = (bf16[2,128,384]{2,1,0:T(8,128)(2,1)S(1)}, bf16[2,128,384]{2,1,0:T(8,128)(2,1)S(1)}, u32[]{:S(2)}, u32[]{:S(2)}) collective-permute-start(bf16[2,128,384]{2,1,0:T(8,128)(2,1)S(1)} %slice_bitcast_fusion.1), channel_id=1, source_target_pairs={{0,1},{1,0},{2,3},{3,2},{4,5},{5,4},{6,7},{7,6},{8,9},{9,8},{10,11... | collective-permute-start | bytes 589832 | tf_op jit(solution)/shard_map/ppermute | solution.py:319
  76.7 3.3 %collective-permute-start.35 = (bf16[2,128,384]{2,1,0:T(8,128)(2,1)S(1)}, bf16[2,128,384]{2,1,0:T(8,128)(2,1)S(1)}, u32[]{:S(2)}, u32[]{:S(2)}) collective-permute-start(bf16[2,128,384]{2,1,0:T(8,128)(2,1)S(1)} %slice_bitcast_fusion), channel_id=1, source_target_pairs={{0,1},{1,0},{2,3},{3,2},{4,5},{5,4},{6,7},{7,6},{8,9},{9,8},{10,11... | collective-permute-start | bytes 589832 | tf_op jit(solution)/shard_map/ppermute | solution.py:319
  81.9 21.3 %collective-permute-start.36 = (bf16[400,384]{1,0:T(8,128)(2,1)S(1)}, bf16[400,384]{1,0:T(8,128)(2,1)S(1)}, u32[]{:S(2)}, u32[]{:S(2)}) collective-permute-start(bf16[400,384]{1,0:T(8,128)(2,1)S(1)} %get-tuple-element.114), channel_id=1, source_target_pairs={{0,8},{2,10},{4,12},{6,14},{8,0},{10,2},{12,4},{14,6},{1,9},{3,11}... | collective-permute-start | bytes 921608 | tf_op jit(solution)/shard_map/ppermute | solution.py:341

commit v3 on v2

--- a/solution.py
+++ b/solution.py
@@ -36,46 +36,76 @@
 
 def lift_kernel(
     index_ref,
-    frames_ref,
-    cotangent_ref,
+    frames_hbm,
+    cotangent_hbm,
     conv_ref,
-    own_ref,
-    other_ref,
-    bias_ref,
-    gain_ref,
-    out_ref,
-    *other_refs,
+    own_hbm,
+    other_hbm,
+    vectors_ref,
+    out_hbm,
+    *refs,
 ):
-    *sent_refs, grad_conv_ref, lifted_ref = other_refs
+    sent_hbm, grad_conv_ref = refs[:block_frames], refs[block_frames]
+    (
+        frames_ref,
+        lifted_ref,
+        cotangent_ref,
+        own_ref,
+        other_ref,
+        out_ref,
+        sent_ref,
+        in_sems,
+        out_sems,
+    ) = refs[block_frames + 1 :]
     tokens, features = frames_ref.shape
     half = features // cores
-    share, half_blocks = sent_refs[0].shape[-1], sent_refs[0].shape[1] // cores
+    share, half_blocks = sent_ref.shape[-1], sent_ref.shape[2] // cores
     core, place = index_ref[0], index_ref[1]
     conv = conv_ref[...]
-    pieces = []
-    for weight_ref, side in ((own_ref, core), (other_ref, 1 - core)):
-        for start in range(0, half, chunk):
-            pieces.append((weight_ref, start, side))
-
     def columns(start, side):
         return pl.ds(pl.multiple_of(side * half + start, lanes), chunk)
 
+    pieces, loads = [], []
+    for weight_hbm, weight_ref, side in (
+        (other_hbm, other_ref, 1 - core),
+        (own_hbm, own_ref, core),
+    ):
+        for start in range(0, half, chunk):
+            where, rows, slot = columns(start, side), pl.ds(start, chunk), 2 * len(pieces)
+            pieces.append((weight_ref, start, side))
+            pair = (
+                pltpu.make_async_copy(
+                    weight_hbm.at[rows, :], weight_ref.at[rows, :], in_sems.at[slot]
+                ),
+                pltpu.make_async_copy(
+                    frames_hbm.at[:, where], frames_ref.at[:, where], in_sems.at[slot + 1]
+                ),
+            )
+            loads.append(pair)
+            for copy in pair:
+                copy.start()
+    load = pltpu.make_async_copy(cotangent_hbm, cotangent_ref, in_sems.at[2 * len(pieces)])
+    load.start()
+
     total = jnp.zeros((tokens, lanes), wide)
-    for weight_ref, start, side in pieces:
+    for number, (weight_ref, start, side) in enumerate(pieces):
+        for copy in loads[number]:
+            copy.wait()
         where = columns(start, side)
         raised = outer_rows(conv, weight_ref[start : start + chunk, :])
-        lifted = (frames_ref[:, where].astype(wide) + raised + bias_ref[:, where]).astype(narrow)
+        lifted = (frames_ref[:, where].astype(wide) + raised + vectors_ref[0:1, where]).astype(narrow)
         lifted_ref[:, where] = lifted
         total = total + folded(lifted.astype(wide))
     center = jnp.sum(total, axis=1, keepdims=True) / features
 
+    load.wait()
     squares = jnp.zeros((tokens, lanes), wide)
     plain = jnp.zeros((tokens, lanes), wide)
     crossed = jnp.zeros((tokens, lanes), wide)
     for weight_ref, start, side in pieces:
         where = columns(start, side)
         shifted = lifted_ref[:, where].astype(wide) - center
-        scaled = cotangent_ref[:, where].astype(wide) * gain_ref[:, where]
+        scaled = cotangent_ref[:, where].astype(wide) * vectors_ref[1:2, where]
         squares = squares + folded(shifted * shifted)
         plain = plain + folded(scaled)
         crossed = crossed + folded(scaled * shifted)
@@ -84,34 +114,44 @@
     mean_crossed = inverse * jnp.sum(crossed, axis=1, keepdims=True) / features
 
     grad_conv = jnp.zeros(grad_conv_ref.shape, wide)
-    for weight_ref, start, side in pieces:
+    stores = []
+    for number, (weight_ref, start, side) in enumerate(pieces):
         where = columns(start, side)
         unit = (lifted_ref[:, where].astype(wide) - center) * inverse
-        gain = gain_ref[:, where]
+        gain = vectors_ref[1:2, where]
         out_ref[:, where] = (unit * gain).astype(narrow)
+        stores.append(
+            pltpu.make_async_copy(
+                out_ref.at[:, where], out_hbm.at[:, where], out_sems.at[block_frames + number]
+            )
+        )
+        stores[-1].start()
         scaled = cotangent_ref[:, where].astype(wide) * gain
         grad = (inverse * (scaled - mean_plain - unit * mean_crossed)).astype(narrow)
         for piece in range(chunk // share):
             slot = start // share + piece
             member, block = slot % members // cores, side * half_blocks + slot // members
-            for step, sent_ref in enumerate(sent_refs):
-
-                @pl.when((place ^ step) == member)
-                def _():
-                    sent_ref[core ^ (slot % cores), block] = grad[
-                        :, piece * share : (piece + 1) * share
-                    ]
-
+            sent_ref[place ^ member, core ^ (slot % cores), block] = grad[
+                :, piece * share : (piece + 1) * share
+            ]
         grad_conv = grad_conv + jnp.dot(
             grad, weight_ref[start : start + chunk, :], preferred_element_type=wide
         )
+    for step in range(block_frames):
+        stores.append(
+            pltpu.make_async_copy(sent_ref.at[step], sent_hbm[step], out_sems.at[step])
+        )
+        stores[-1].start()
     grad_conv_ref[...] = grad_conv.astype(narrow)
+    for copy in stores:
+        copy.wait()
 
 
 def lift(index, frames_in, cotangent, conv, own, other, bias, gain, blocks, share):
     tokens, features = frames_in.shape
     channels = conv.shape[1]
     vmem = pl.BlockSpec(memory_space=pltpu.VMEM)
+    hbm = pl.BlockSpec(memory_space=pltpu.HBM)
     return pl.pallas_call(
         lift_kernel,
         out_shape=(
@@ -119,17 +159,27 @@
             *[jax.ShapeDtypeStruct((cores, blocks, tokens, share), narrow)] * block_frames,
             jax.ShapeDtypeStruct((tokens, channels), narrow),
         ),
-        in_specs=[pl.BlockSpec(memory_space=pltpu.SMEM)] + [vmem] * 7,
-        out_specs=(vmem,) * (2 + block_frames),
-        scratch_shapes=[pltpu.VMEM((tokens, features), narrow)],
-        compiler_params=pltpu.CompilerParams(vmem_limit_bytes=32 * 1024 * 1024),
+        in_specs=[pl.BlockSpec(memory_space=pltpu.SMEM), hbm, hbm, vmem, hbm, hbm, vmem],
+        out_specs=(hbm,) * (1 + block_frames) + (vmem,),
+        scratch_shapes=[
+            pltpu.VMEM((tokens, features), narrow),
+            pltpu.VMEM((tokens, features), narrow),
+            pltpu.VMEM((tokens, features), narrow),
+            pltpu.VMEM(own.shape, narrow),
+            pltpu.VMEM(own.shape, narrow),
+            pltpu.VMEM((tokens, features), narrow),
+            pltpu.VMEM((block_frames, cores, blocks, tokens, share), narrow),
+            pltpu.SemaphoreType.DMA((1 + 2 * (features // chunk),)),
+            pltpu.SemaphoreType.DMA((block_frames + features // chunk,)),
+        ],
+        compiler_params=pltpu.CompilerParams(vmem_limit_bytes=60 * 1024 * 1024),
         cost_estimate=pl.CostEstimate(
             flops=0,
             bytes_accessed=0,
             transcendentals=0,
         ),
         name="lift",
-    )(index, frames_in, cotangent, conv, own, other, bias[None], gain[None])
+    )(index, frames_in, cotangent, conv, own, other, jnp.stack([bias, gain]))
 
 
 def split_kernel(index_ref, value_ref, *out_refs):
@@ -362,11 +412,17 @@
         frames_parts[step] = block_swap(frames_parts[step], step)
     bottle = squeeze(index_after, frames_in, down_weight, down_bias[None], 0, wide)
     bottle = squeeze(index, frames_in, down_other, bottle, 1, narrow)
+    bottle = after([bottle], frames_parts[1:3])[0]
     up_other = core_swap(up_weight)
-    bottle_parts = [bottle] + [block_swap(bottle, step) for step in range(1, block_frames)]
     bottle_edge = edge_swap(bottle)
+    bottle_parts = [
+        bottle,
+        block_swap(bottle, 1),
+        block_swap(after([bottle], bottle_edge)[0], 2),
+        block_swap(bottle, 3),
+    ]
     frames_parts[3] = block_swap(
-        after([frames_parts[3]], (bottle_parts[1:], bottle_edge))[0], 3
+        after([frames_parts[3]], (bottle_parts[1], bottle_parts[3], bottle_edge))[0], 3
     )
 
     def pick(value, *places):
@@ -405,7 +461,7 @@
 
     frames_got = by_core(after(frames_parts, grad_parts[1]))
 
-    def whole_block(parts):
+    def whole_block(parts, late):
         if blocks == 2:
             beside = across(
                 lax.select_n(jnp.where(block == 0, block_frames - 1, 0) ^ place, *parts), 1
@@ -414,24 +470,27 @@
         else:
             frames = ordered(parts)
             sides = [shifted(frames[-1], 1), shifted(frames[0], -1)]
+        if late is not None:
+            sides = after(sides, late)
         own = list(parts) + sides[: 1 if blocks == 2 else 2]
         other = [core_swap(value) for value in own]
         return own[:block_frames] + sides, other[:block_frames] + [other[block_frames], other[-1]]
 
-    grad_own, grad_other = whole_block(grad_parts)
+    grad_own, grad_other = whole_block(grad_parts, None)
     ends = jnp.stack([place, block, blocks - 1 - block]).astype(jnp.int32)
     grad_bottle = mix(ends, conv_kernel, after(grad_own + grad_other, lifted_parts[1:3]))
     targets = jnp.stack([(block + step) % blocks for step in range(blocks)]).astype(jnp.int32)
     grad_down, _, *down_sent = contract(targets, grad_bottle, None, frames_got)
-    down_sent = after(down_sent, lifted_parts[3])
-    down_got = [across(value, step + 1) for step, value in enumerate(down_sent)]
-    bottle_own, bottle_other = whole_block(after(bottle_parts, lifted_parts[2]))
+    bottle_own, bottle_other = whole_block(
+        after(bottle_parts, grad_parts[3]), lifted_parts[2]
+    )
     conv_rows, small = mix(
         ends,
         conv_kernel,
         bottle_own + bottle_other + grad_own[:block_frames] + grad_other[:block_frames],
         grad_bottle,
     )
+    down_got = [across(value, step + 1) for step, value in enumerate(down_sent)]
     grad_up, grad_up_bias, *up_sent = contract(targets, conv_rows, small, by_core(lifted_parts))
     up_got = [across(value, step + 1) for step, value in enumerate(up_sent)]
     down_got = after(down_got, up_sent[0])

time: 106 us -> 103 us (0.972)
  local copies, waits for them, and re-layouts: 14.1 us -> 6.11 us
  starting transfers between devices: 30.6 us -> 35.6 us
    ppermute x4, waiting for transfers between devices: 17.7 us -> 24.4 us  [across(): lax.ppermute(value, 'tm', [(i, (i + step * block_frames) % count) for i i...]
    ppermute x12, waiting for transfers between devices: 14.4 us -> 7.77 us  [block_swap(): return lax.ppermute(value, 'tm', [(i, i ^ step) for i in range(count)])]
    unnamed x26 -> x20, local copies, waits for them, and re-layouts: 9.22 us -> 3.11 us
    ppermute x12, starting transfers between devices: 18.6 us -> 23.5 us  [block_swap(): return lax.ppermute(value, 'tm', [(i, i ^ step) for i in range(count)])]
    squeeze x8, local copies, waits for them, and re-layouts: 2.95 us -> 1.09 us  [by_core(): return list(parts) + [core_swap(v[1]) for v in parts]]
  transfers between devices with their start and end apart: 37 -> 37, of which waited for: 11 -> 10; matrix products, arithmetic and copies ran while one was open for 6% -> 4% of each run, Pallas kernels for 22% -> 23%
where the time goes in v3:
time: 103 us
  starting transfers between devices  35.6 us (35%)
  waiting for transfers between devices  33.2 us (32%)
  Pallas kernels  23.1 us (22%)
  local copies, waits for them, and re-layouts  6.11 us (6%)
  other arithmetic  3.49 us (3%)
    ppermute x4, waiting for transfers between devices, across(): lax.ppermute(value, 'tm', [(i, (i + step * block_frames) % count) for i i...  24.4 us
    ppermute x12, starting transfers between devices, block_swap(): return lax.ppermute(value, 'tm', [(i, i ^ step) for i in range(count)])  23.5 us
    pallas_call x1, Pallas kernels, lift(): pl.pallas_call(lift_kernel, out_shape=(jax.ShapeDtypeStruct((tokens, feat...  10.5 us
    ppermute x12, waiting for transfers between devices, block_swap(): return lax.ppermute(value, 'tm', [(i, i ^ step) for i in range(count)])  7.77 us
    ppermute x4, starting transfers between devices, across(): lax.ppermute(value, 'tm', [(i, (i + step * block_frames) % count) for i i...  6.32 us
    ppermute x20, starting transfers between devices, core_swap(): return lax.ppermute(value, 'tensor', [(0, 1), (1, 0)])  4.92 us
    pallas_call x2, Pallas kernels, contract(): pl.pallas_call(body, out_shape=(jax.ShapeDtypeStruct((share, channels), w...  4.42 us
    pallas_call x2, Pallas kernels, mix(): pl.pallas_call(mix_grad_kernel if last else mix_conv_kernel, out_shape=ro...  4 us
  transfers between devices with their start and end apart: 37, of which 10 were waited for; matrix products, arithmetic and copies ran while one was open for 4% of the time, Pallas kernels for 23%

profile of v3, /device:TPU:0, one launch (start us, length us, event | category | flops | bytes accessed | tf_op | source)
XLA Modules:
  0.0 102.5 jit_solution(15998772759899810276)
XLA Ops:
  0.6 0.5 collective-permute-start
  1.1 0.1 collective-permute-start.6
  1.2 0.1 pad_add_fusion.index_ref
  1.3 1.4 %copy-done = bf16[128,6144]{1,0:T(8,128)(2,1)S(1)} copy-done((bf16[128,6144]{1,0:T(8,128)(2,1)S(1)}, bf16[128,6144]{1,0:T(8,128)(2,1)}, u32[]{:S(2)}) %copy-start) | copy-done | bytes 1572888
  2.7 0.8 split.1
  3.5 3.0 %collective-permute-start.1 = (bf16[2,2,128,384]{3,2,1,0:T(8,128)(2,1)S(1)}, bf16[2,2,128,384]{3,2,1,0:T(8,128)(2,1)S(1)}, u32[]{:S(2)}, u32[]{:S(2)}) collective-permute-start(bf16[2,2,128,384]{3,2,1,0:T(8,128)(2,1)S(1)} %get-tuple-element.73), channel_id=1, source_target_pairs={{0,2},{2,0},{4,6},{6,4},{8,10},{10,8},{12,14},{14,12},{1,3},{3,1},... | collective-permute-start | bytes 1179656 | tf_op jit(solution)/shard_map/ppermute | solution.py:372
  6.5 1.6 %collective-permute-start.2 = (bf16[2,2,128,384]{3,2,1,0:T(8,128)(2,1)S(1)}, bf16[2,2,128,384]{3,2,1,0:T(8,128)(2,1)S(1)}, u32[]{:S(2)}, u32[]{:S(2)}) collective-permute-start(bf16[2,2,128,384]{3,2,1,0:T(8,128)(2,1)S(1)} %get-tuple-element.74), channel_id=1, source_target_pairs={{0,4},{2,6},{4,0},{6,2},{8,12},{10,14},{12,8},{14,10},{1,5},{3,7},... | collective-permute-start | bytes 1179656 | tf_op jit(solution)/shard_map/ppermute | solution.py:372
  8.1 0.7 broadcast_in_dim.13.start_ref
  8.8 1.7 %copy-done.2 = bf16[3072,384]{1,0:T(8,128)(2,1)S(1)} copy-done((bf16[3072,384]{1,0:T(8,128)(2,1)S(1)}, bf16[3072,384]{1,0:T(8,128)(2,1)}, u32[]{:S(2)}) %copy-start.2) | copy-done | bytes 2359320
  10.4 1.1 %squeeze.43.start_ref = f32[128,384]{1,0:T(8,128)S(1)} custom-call(s32[2]{0:T(128)S(1)} %pad_add_fusion.index_ref, bf16[128,6144]{1,0:T(8,128)(2,1)S(1)} %copy-done.1, bf16[3072,384]{1,0:T(8,128)(2,1)S(1)} %copy-done.2, f32[1,384]{1,0:T(1,128)S(1)} %broadcast_in_dim.13.start_ref), custom_call_target="tpu_custom_call" | custom-call | tf_op jit(solution)/shard_map/squeeze/pallas_call | solution.py:223
  11.6 2.2 %squeeze.44.refs_0_ = bf16[128,384]{1,0:T(8,128)(2,1)S(1)} custom-call(s32[2]{0:T(128)S(1)} %pad_add_fusion.index_ref, bf16[128,6144]{1,0:T(8,128)(2,1)S(1)} %copy-done.1, bf16[3072,384]{1,0:T(8,128)(2,1)} %collective-permute-done.weight_ref, f32[128,384]{1,0:T(8,128)S(1)} %squeeze.43.start_ref), custom_call_target="tpu_custom_call" | custom-call | tf_op jit(solution)/shard_map/squeeze/pallas_call | solution.py:223
  13.8 2.0 %collective-permute-done.1.refs_1_ = bf16[2,2,128,384]{3,2,1,0:T(8,128)(2,1)S(1)} collective-permute-done((bf16[2,2,128,384]{3,2,1,0:T(8,128)(2,1)S(1)}, bf16[2,2,128,384]{3,2,1,0:T(8,128)(2,1)S(1)}, u32[]{:S(2)}, u32[]{:S(2)}) %collective-permute-start.1) | collective-permute-done | bytes 393248 | tf_op jit(solution)/shard_map/ppermute | solution.py:372
  15.8 1.5 %collective-permute-done.2.refs_2_ = bf16[2,2,128,384]{3,2,1,0:T(8,128)(2,1)S(1)} collective-permute-done((bf16[2,2,128,384]{3,2,1,0:T(8,128)(2,1)S(1)}, bf16[2,2,128,384]{3,2,1,0:T(8,128)(2,1)S(1)}, u32[]{:S(2)}, u32[]{:S(2)}) %collective-permute-start.2) | collective-permute-done | bytes 393248 | tf_op jit(solution)/shard_map/ppermute | solution.py:372
  17.3 0.4 collective-permute-start.3
  17.7 2.7 %collective-permute-start.4 = (bf16[128,384]{1,0:T(8,128)(2,1)S(1)}, bf16[128,384]{1,0:T(8,128)(2,1)S(1)}, u32[]{:S(2)}, u32[]{:S(2)}) collective-permute-start(bf16[128,384]{1,0:T(8,128)(2,1)S(1)} %squeeze.44.refs_0_), channel_id=1, source_target_pairs={{0,6},{2,4},{4,2},{6,0},{8,14},{10,12},{12,10},{14,8},{1,7},{3,5},... | collective-permute-start | bytes 294920 | tf_op jit(solution)/shard_map/ppermute | solution.py:372
  20.3 0.8 collective-permute-start.5
  21.2 0.7 pad_maximum_fusion.vectors_ref
  21.9 0.4 collective-permute-done.3.refs_1_
  22.2 1.0 %collective-permute-done.4.refs_3_ = bf16[128,384]{1,0:T(8,128)(2,1)S(1)} collective-permute-done((bf16[128,384]{1,0:T(8,128)(2,1)S(1)}, bf16[128,384]{1,0:T(8,128)(2,1)S(1)}, u32[]{:S(2)}, u32[]{:S(2)}) %collective-permute-start.4) | collective-permute-done | bytes 98336 | tf_op jit(solution)/shard_map/ppermute | solution.py:372
  23.3 5.6 %collective-permute-start.7 = (bf16[2,2,128,384]{3,2,1,0:T(8,128)(2,1)S(1)}, bf16[2,2,128,384]{3,2,1,0:T(8,128)(2,1)S(1)}, u32[]{:S(2)}, u32[]{:S(2)}) collective-permute-start(bf16[2,2,128,384]{3,2,1,0:T(8,128)(2,1)S(1)} %get-tuple-element.82), channel_id=1, source_target_pairs={{0,6},{2,4},{4,2},{6,0},{8,14},{10,12},{12,10},{14,8},{1,7},{3,5},... | collective-permute-start | bytes 1179656 | tf_op jit(solution)/shard_map/ppermute | solution.py:372
  28.9 0.1 pad_add_fusion.2.index_ref
  29.0 0.1 collective-permute-start.24
  29.1 0.7 add_convert_fusion.conv_ref
  29.8 10.5 %lift.1 = (bf16[128,6144]{1,0:T(8,128)(2,1)}, bf16[2,2,128,384]{3,2,1,0:T(8,128)(2,1)}, bf16[2,2,128,384]{3,2,1,0:T(8,128)(2,1)}, bf16[2,2,128,384]{3,2,1,0:T(8,...) custom-call(s32[2]{0:T(128)} %copy-done.6, bf16[128,6144]{1,0:T(8,128)(2,1)} %frames_hbm.1, ...), custom_call_target="tpu_custom_call" | custom-call | tf_op jit(solution)/shard_map/lift/pallas_call | solution.py:155
  40.4 0.1 collective-permute-start.10
  40.5 0.1 pad_add_fusion.1.targets_ref
  40.5 3.5 %collective-permute-start.8 = (bf16[128,384]{1,0:T(8,128)(2,1)}, bf16[128,384]{1,0:T(8,128)(2,1)S(1)}, u32[]{:S(2)}, u32[]{:S(2)}) collective-permute-start(bf16[128,384]{1,0:T(8,128)(2,1)} %get-tuple-element.90.refs_0_.refs_12_), channel_id=1, source_target_pairs={{0,2},{2,0},{4,6},{6,4},{8,10},{10,8},{12,14},{14,12},{1,3},{3,1},... | collective-permute-start | bytes 294920 | tf_op jit(solution)/shard_map/ppermute | solution.py:372
  44.0 2.2 %collective-permute-done.10.refs_3_.refs_15_ = bf16[128,384]{1,0:T(8,128)(2,1)S(1)} collective-permute-done((bf16[128,384]{1,0:T(8,128)(2,1)}, bf16[128,384]{1,0:T(8,128)(2,1)S(1)}, u32[]{:S(2)}, u32[]{:S(2)}) %collective-permute-start.10) | collective-permute-done | bytes 98336 | tf_op jit(solution)/shard_map/ppermute | solution.py:372
  46.3 1.5 %collective-permute-start.25 = (bf16[128,384]{1,0:T(8,128)(2,1)S(1)}, bf16[128,384]{1,0:T(8,128)(2,1)S(1)}, u32[]{:S(2)}, u32[]{:S(2)}) collective-permute-start(bf16[128,384]{1,0:T(8,128)(2,1)S(1)} %select_select_fusion), channel_id=1, source_target_pairs={{0,8},{2,10},{4,12},{6,14},{8,0},{10,2},{12,4},{14,6},{1,9},{3,11}... | collective-permute-start | bytes 294920 | tf_op jit(solution)/shard_map/ppermute | solution.py:391
  47.8 2.0 %collective-permute-start.18 = (bf16[2,2,128,384]{3,2,1,0:T(8,128)(2,1)}, bf16[2,2,128,384]{3,2,1,0:T(8,128)(2,1)S(1)}, u32[]{:S(2)}, u32[]{:S(2)}) collective-permute-start(bf16[2,2,128,384]{3,2,1,0:T(8,128)(2,1)} %get-tuple-element.89), channel_id=1, source_target_pairs={{0,4},{2,6},{4,0},{6,2},{8,12},{10,14},{12,8},{14,10},{1,5},{3,7},... | collective-permute-start | bytes 1179656 | tf_op jit(solution)/shard_map/ppermute | solution.py:372
  49.7 1.6 %collective-permute-start.17 = (bf16[2,2,128,384]{3,2,1,0:T(8,128)(2,1)}, bf16[2,2,128,384]{3,2,1,0:T(8,128)(2,1)S(1)}, u32[]{:S(2)}, u32[]{:S(2)}) collective-permute-start(bf16[2,2,128,384]{3,2,1,0:T(8,128)(2,1)} %get-tuple-element.88), channel_id=1, source_target_pairs={{0,2},{2,0},{4,6},{6,4},{8,10},{10,8},{12,14},{14,12},{1,3},{3,1},... | collective-permute-start | bytes 1179656 | tf_op jit(solution)/shard_map/ppermute | solution.py:372
  51.4 1.8 %collective-permute-start.11 = (bf16[128,384]{1,0:T(8,128)(2,1)S(1)}, bf16[128,384]{1,0:T(8,128)(2,1)S(1)}, u32[]{:S(2)}, u32[]{:S(2)}) collective-permute-start(bf16[128,384]{1,0:T(8,128)(2,1)S(1)} %select_select_fusion.1), channel_id=1, source_target_pairs={{0,8},{2,10},{4,12},{6,14},{8,0},{10,2},{12,4},{14,6},{1,9},{3,11}... | collective-permute-start | bytes 294920 | tf_op jit(solution)/shard_map/ppermute | solution.py:391
  53.2 0.9 slice_bitcast_fusion.3
  54.2 0.1 collective-permute-start.13
  54.3 0.5 collective-permute-start.14
  54.8 5.6 %collective-permute-done.11.refs_4_.refs_5_ = bf16[128,384]{1,0:T(8,128)(2,1)S(1)} collective-permute-done((bf16[128,384]{1,0:T(8,128)(2,1)S(1)}, bf16[128,384]{1,0:T(8,128)(2,1)S(1)}, u32[]{:S(2)}, u32[]{:S(2)}) %collective-permute-start.11) | collective-permute-done | bytes 98336 | tf_op jit(solution)/shard_map/ppermute | solution.py:391
  60.4 3.2 %collective-permute-start.31 = (bf16[2,2,128,384]{3,2,1,0:T(8,128)(2,1)S(1)}, bf16[2,2,128,384]{3,2,1,0:T(8,128)(2,1)S(1)}, u32[]{:S(2)}, u32[]{:S(2)}) collective-permute-start(bf16[2,2,128,384]{3,2,1,0:T(8,128)(2,1)S(1)} %copy-done.9), channel_id=1, source_target_pairs={{0,6},{2,4},{4,2},{6,0},{8,14},{10,12},{12,10},{14,8},{1,7},{3,5},... | collective-permute-start | bytes 1179656 | tf_op jit(solution)/shard_map/ppermute | solution.py:372
  63.6 0.5 collective-permute-start.15
  64.2 1.0 collective-permute-done.15.refs_9_.refs_19_
  65.1 0.2 collective-permute-start.26
  65.4 0.3 collective-permute-start.20
  65.7 0.2 collective-permute-start.21
  65.9 0.3 collective-permute-start.22
  66.2 1.1 %mix_grad.1.rows_ref.grad_ref = bf16[2,4,128,384]{3,2,1,0:T(8,128)(2,1)S(1)} custom-call(s32[3]{0:T(128)S(1)} %pad_add_fusion.2.index_ref, f32[3,384]{1,0:T(4,128)S(1)} %copy-done.5, bf16[128,384]{1,0:T(8,128)(2,1)S(1)} %copy-done.3, bf16[128,384]{1,0:T(8,128)(2,1)S(1)} %collective-permute-done.8.refs_1_.refs_13_, ...), custom_call_target="tpu_custom_call" | custom-call | tf_op jit(solution)/shard_map/mix_grad/pallas_call | solution.py:288
  67.3 0.3 collective-permute-start.27
  67.6 0.3 collective-permute-start.28
  67.9 0.2 collective-permute-start.29
  68.1 2.5 %contract_down.1 = (f32[384,384]{1,0:T(8,128)S(1)}, f32[1,384]{1,0:T(1,128)}, bf16[384,384]{1,0:T(8,128)(2,1)S(1)}) custom-call(s32[2]{0:T(128)S(1)} %pad_add_fusion.1.targets_ref, bf16[2,4,128,384]{3,2,1,0:T(8,128)(2,1)S(1)} %mix_grad.1.rows_ref.grad_ref, bf16[2,2,128,384]{3,2,1,0:T(8,128)(2,1)S(1)} %get-tuple-element.103.refs_0_, ...), custom_call_target="tpu_custom_call" | custom-call | tf_op jit(solution)/shard_map/contract_down/pallas_call | solution.py:337
  70.6 0.3 collective-permute-start.30
  70.9 0.7 collective-permute-done.31.refs_3_
  71.5 2.7 %collective-permute-start.23 = (bf16[384,384]{1,0:T(8,128)(2,1)S(1)}, bf16[384,384]{1,0:T(8,128)(2,1)S(1)}, u32[]{:S(2)}, u32[]{:S(2)}) collective-permute-start(bf16[384,384]{1,0:T(8,128)(2,1)S(1)} %get-tuple-element.108), channel_id=1, source_target_pairs={{0,8},{2,10},{4,12},{6,14},{8,0},{10,2},{12,4},{14,6},{1,9},{3,11}... | collective-permute-start | bytes 884744 | tf_op jit(solution)/shard_map/ppermute | solution.py:391
  74.3 0.1 collective-permute-start.32
  74.4 0.5 collective-permute-start.33
  74.9 0.1 collective-permute-start.34
  75.0 0.4 collective-permute-start.35
  75.4 2.9 %mix_conv.1 = (bf16[2,4,128,384]{3,2,1,0:T(8,128)(2,1)S(1)}, f32[8,384]{1,0:T(8,128)S(1)}) custom-call(s32[3]{0:T(128)S(1)} %pad_add_fusion.2.index_ref, f32[3,384]{1,0:T(4,128)S(1)} %copy-done.5, bf16[2,4,128,384]{3,2,1,0:T(8,128)(2,1)S(1)} %mix_grad.1.rows_ref.grad_ref, bf16[128,384]{1,0:T(8,128)(2,1)S(1)} %squeeze.44.refs_0_, ...), custom_call_target="tpu_custom_call" | custom-call | tf_op jit(solution)/shard_map/mix_conv/pallas_call | solution.py:288
  78.4 2.0 %contract_up.1 = (f32[384,384]{1,0:T(8,128)S(1)}, f32[1,384]{1,0:T(1,128)S(1)}, bf16[400,384]{1,0:T(8,128)(2,1)S(1)}) custom-call(s32[2]{0:T(128)S(1)} %pad_add_fusion.1.targets_ref, bf16[2,4,128,384]{3,2,1,0:T(8,128)(2,1)S(1)} %get-tuple-element.116.rows_ref, f32[8,384]{1,0:T(8,128)S(1)} %get-tuple-element.117.small_ref, ...), custom_call_target="tpu_custom_call" | custom-call | tf_op jit(solution)/shard_map/contract_up/pallas_call | solution.py:337
  80.4 0.2 collective-permute-start.36
  80.7 13.7 %collective-permute-done.23 = bf16[384,384]{1,0:T(8,128)(2,1)S(1)} collective-permute-done((bf16[384,384]{1,0:T(8,128)(2,1)S(1)}, bf16[384,384]{1,0:T(8,128)(2,1)S(1)}, u32[]{:S(2)}, u32[]{:S(2)}) %collective-permute-start.23) | collective-permute-done | bytes 294944 | tf_op jit(solution)/shard_map/ppermute | solution.py:391
  94.4 0.9 convert_add_fusion
  95.2 5.2 %collective-permute-done.36 = bf16[400,384]{1,0:T(8,128)(2,1)S(1)} collective-permute-done((bf16[400,384]{1,0:T(8,128)(2,1)S(1)}, bf16[400,384]{1,0:T(8,128)(2,1)S(1)}, u32[]{:S(2)}, u32[]{:S(2)}) %collective-permute-start.36) | collective-permute-done | bytes 307232 | tf_op jit(solution)/shard_map/ppermute | solution.py:391
  100.5 0.6 slice.83
  101.1 0.6 slice_reduce_fusion
  101.7 0.9 slice_add_fusion
  (62 shorter events, 0.5 us)
Async XLA Ops:
  0.6 10.9 %collective-permute-start = (bf16[3072,384]{1,0:T(8,128)(2,1)}, bf16[3072,384]{1,0:T(8,128)(2,1)}, u32[]{:S(2)}, u32[]{:S(2)}) collective-permute-start(bf16[3072,384]{1,0:T(8,128)(2,1)} %weight_ref.1), channel_id=1, source_target_pairs={{0,1},{1,0},{2,3},{3,2},{4,5},{5,4},{6,7},{7,6},{8,9},{9,8},{10,11... | collective-permute-start | bytes 7077896 | tf_op jit(solution)/shard_map/ppermute | solution.py:369
  1.1 28.7 %collective-permute-start.6 = (bf16[3072,384]{1,0:T(8,128)(2,1)}, bf16[3072,384]{1,0:T(8,128)(2,1)}, u32[]{:S(2)}, u32[]{:S(2)}) collective-permute-start(bf16[3072,384]{1,0:T(8,128)(2,1)} %own_hbm.1), channel_id=1, source_target_pairs={{0,1},{1,0},{2,3},{3,2},{4,5},{5,4},{6,7},{7,6},{8,9},{9,8},{10,11... | collective-permute-start | bytes 7077896 | tf_op jit(solution)/shard_map/ppermute | solution.py:369
  1.3 1.4 %copy-start = (bf16[128,6144]{1,0:T(8,128)(2,1)S(1)}, bf16[128,6144]{1,0:T(8,128)(2,1)}, u32[]{:S(2)}) copy-start(bf16[128,6144]{1,0:T(8,128)(2,1)} %frames_hbm.1) | copy-start | bytes 4718596
  2.7 8.9 %copy-start.6 = (s32[2]{0:T(128)}, s32[2]{0:T(128)S(1)}, u32[]{:S(2)}) copy-start(s32[2]{0:T(128)S(1)} %pad_add_fusion.index_ref) | copy-start | bytes 28
  2.7 6.0 %copy-start.1 = (bf16[128,6144]{1,0:T(8,128)(2,1)S(1)}, bf16[128,6144]{1,0:T(8,128)(2,1)}, u32[]{:S(2)}) copy-start(bf16[128,6144]{1,0:T(8,128)(2,1)} %frames_hbm.1) | copy-start | bytes 4718596
  3.5 12.4 %collective-permute-start.1 = (bf16[2,2,128,384]{3,2,1,0:T(8,128)(2,1)S(1)}, bf16[2,2,128,384]{3,2,1,0:T(8,128)(2,1)S(1)}, u32[]{:S(2)}, u32[]{:S(2)}) collective-permute-start(bf16[2,2,128,384]{3,2,1,0:T(8,128)(2,1)S(1)} %get-tuple-element.73), channel_id=1, source_target_pairs={{0,2},{2,0},{4,6},{6,4},{8,10},{10,8},{12,14},{14,12},{1,3},{3,1},... | collective-permute-start | bytes 1179656 | tf_op jit(solution)/shard_map/ppermute | solution.py:372
  6.5 10.8 %collective-permute-start.2 = (bf16[2,2,128,384]{3,2,1,0:T(8,128)(2,1)S(1)}, bf16[2,2,128,384]{3,2,1,0:T(8,128)(2,1)S(1)}, u32[]{:S(2)}, u32[]{:S(2)}) collective-permute-start(bf16[2,2,128,384]{3,2,1,0:T(8,128)(2,1)S(1)} %get-tuple-element.74), channel_id=1, source_target_pairs={{0,4},{2,6},{4,0},{6,2},{8,12},{10,14},{12,8},{14,10},{1,5},{3,7},... | collective-permute-start | bytes 1179656 | tf_op jit(solution)/shard_map/ppermute | solution.py:372
  8.8 1.7 %copy-start.2 = (bf16[3072,384]{1,0:T(8,128)(2,1)S(1)}, bf16[3072,384]{1,0:T(8,128)(2,1)}, u32[]{:S(2)}) copy-start(bf16[3072,384]{1,0:T(8,128)(2,1)} %weight_ref.1) | copy-start | bytes 7077892
  11.5 9.7 %copy-start.7 = (f32[6144]{0:T(1024)S(1)}, f32[6144]{0:T(1024)}, u32[]{:S(2)}) copy-start(f32[6144]{0:T(1024)} %param.17) | copy-start | bytes 73732
  11.5 9.7 %copy-start.8 = (f32[6144]{0:T(1024)S(1)}, f32[6144]{0:T(1024)}, u32[]{:S(2)}) copy-start(f32[6144]{0:T(1024)} %param.16) | copy-start | bytes 73732
  11.6 17.4 %copy-start.5 = (f32[3,384]{1,0:T(4,128)S(1)}, f32[3,384]{1,0:T(4,128)}, u32[]{:S(2)}) copy-start(f32[3,384]{1,0:T(4,128)} %taps_ref.3) | copy-start | bytes 13828
  17.3 4.9 %collective-permute-start.3 = (bf16[128,384]{1,0:T(8,128)(2,1)S(1)}, bf16[128,384]{1,0:T(8,128)(2,1)S(1)}, u32[]{:S(2)}, u32[]{:S(2)}) collective-permute-start(bf16[128,384]{1,0:T(8,128)(2,1)S(1)} %squeeze.44.refs_0_), channel_id=1, source_target_pairs={{0,2},{2,0},{4,6},{6,4},{8,10},{10,8},{12,14},{14,12},{1,3},{3,1},... | collective-permute-start | bytes 294920 | tf_op jit(solution)/shard_map/ppermute | solution.py:372
  17.7 5.6 %collective-permute-start.4 = (bf16[128,384]{1,0:T(8,128)(2,1)S(1)}, bf16[128,384]{1,0:T(8,128)(2,1)S(1)}, u32[]{:S(2)}, u32[]{:S(2)}) collective-permute-start(bf16[128,384]{1,0:T(8,128)(2,1)S(1)} %squeeze.44.refs_0_), channel_id=1, source_target_pairs={{0,6},{2,4},{4,2},{6,0},{8,14},{10,12},{12,10},{14,8},{1,7},{3,5},... | collective-permute-start | bytes 294920 | tf_op jit(solution)/shard_map/ppermute | solution.py:372
  20.3 2.9 %collective-permute-start.5 = (bf16[128,384]{1,0:T(8,128)(2,1)S(1)}, bf16[128,384]{1,0:T(8,128)(2,1)S(1)}, u32[]{:S(2)}, u32[]{:S(2)}) collective-permute-start(bf16[128,384]{1,0:T(8,128)(2,1)S(1)} %squeeze.44.refs_0_), channel_id=1, source_target_pairs={{6,8},{8,6},{7,9},{9,7},{22,24},{24,22},{23,25},{25,23}} | collective-permute-start | bytes 294920 | tf_op jit(solution)/shard_map/ppermute | solution.py:386
  23.3 17.1 %collective-permute-start.7 = (bf16[2,2,128,384]{3,2,1,0:T(8,128)(2,1)S(1)}, bf16[2,2,128,384]{3,2,1,0:T(8,128)(2,1)S(1)}, u32[]{:S(2)}, u32[]{:S(2)}) collective-permute-start(bf16[2,2,128,384]{3,2,1,0:T(8,128)(2,1)S(1)} %get-tuple-element.82), channel_id=1, source_target_pairs={{0,6},{2,4},{4,2},{6,0},{8,14},{10,12},{12,10},{14,8},{1,7},{3,5},... | collective-permute-start | bytes 1179656 | tf_op jit(solution)/shard_map/ppermute | solution.py:372
  29.0 15.0 %collective-permute-start.24 = (bf16[128,384]{1,0:T(8,128)(2,1)S(1)}, bf16[128,384]{1,0:T(8,128)(2,1)S(1)}, u32[]{:S(2)}, u32[]{:S(2)}) collective-permute-start(bf16[128,384]{1,0:T(8,128)(2,1)S(1)} %squeeze.44.refs_0_), channel_id=1, source_target_pairs={{0,4},{2,6},{4,0},{6,2},{8,12},{10,14},{12,8},{14,10},{1,5},{3,7},... | collective-permute-start | bytes 294920 | tf_op jit(solution)/shard_map/ppermute | solution.py:372
  40.4 20.0 %copy-start.9 = (bf16[2,2,128,384]{3,2,1,0:T(8,128)(2,1)S(1)}, bf16[2,2,128,384]{3,2,1,0:T(8,128)(2,1)}, u32[]{:S(2)}) copy-start(bf16[2,2,128,384]{3,2,1,0:T(8,128)(2,1)} %get-tuple-element.119) | copy-start | bytes 1179652
  40.4 25.8 %copy-start.3 = (bf16[128,384]{1,0:T(8,128)(2,1)S(1)}, bf16[128,384]{1,0:T(8,128)(2,1)}, u32[]{:S(2)}) copy-start(bf16[128,384]{1,0:T(8,128)(2,1)} %get-tuple-element.90.refs_0_.refs_12_) | copy-start | bytes 294916
  40.4 5.8 %collective-permute-start.10 = (bf16[128,384]{1,0:T(8,128)(2,1)}, bf16[128,384]{1,0:T(8,128)(2,1)S(1)}, u32[]{:S(2)}, u32[]{:S(2)}) collective-permute-start(bf16[128,384]{1,0:T(8,128)(2,1)} %get-tuple-element.90.refs_0_.refs_12_), channel_id=1, source_target_pairs={{0,6},{2,4},{4,2},{6,0},{8,14},{10,12},{12,10},{14,8},{1,7},{3,5},... | collective-permute-start | bytes 294920 | tf_op jit(solution)/shard_map/ppermute | solution.py:372
  40.5 7.2 %collective-permute-start.8 = (bf16[128,384]{1,0:T(8,128)(2,1)}, bf16[128,384]{1,0:T(8,128)(2,1)S(1)}, u32[]{:S(2)}, u32[]{:S(2)}) collective-permute-start(bf16[128,384]{1,0:T(8,128)(2,1)} %get-tuple-element.90.refs_0_.refs_12_), channel_id=1, source_target_pairs={{0,2},{2,0},{4,6},{6,4},{8,10},{10,8},{12,14},{14,12},{1,3},{3,1},... | collective-permute-start | bytes 294920 | tf_op jit(solution)/shard_map/ppermute | solution.py:372
  44.0 7.3 %collective-permute-start.9 = (bf16[128,384]{1,0:T(8,128)(2,1)}, bf16[128,384]{1,0:T(8,128)(2,1)S(1)}, u32[]{:S(2)}, u32[]{:S(2)}) collective-permute-start(bf16[128,384]{1,0:T(8,128)(2,1)} %get-tuple-element.90.refs_0_.refs_12_), channel_id=1, source_target_pairs={{0,4},{2,6},{4,0},{6,2},{8,12},{10,14},{12,8},{14,10},{1,5},{3,7},... | collective-permute-start | bytes 294920 | tf_op jit(solution)/shard_map/ppermute | solution.py:372
  44.0 10.2 %collective-permute-start.12 = (bf16[128,384]{1,0:T(8,128)(2,1)}, bf16[128,384]{1,0:T(8,128)(2,1)S(1)}, u32[]{:S(2)}, u32[]{:S(2)}) collective-permute-start(bf16[128,384]{1,0:T(8,128)(2,1)} %get-tuple-element.90.refs_0_.refs_12_), channel_id=1, source_target_pairs={{0,1},{1,0},{2,3},{3,2},{4,5},{5,4},{6,7},{7,6},{8,9},{9,8},{10,11... | collective-permute-start | bytes 294920 | tf_op jit(solution)/shard_map/ppermute | solution.py:369
  46.3 8.1 %collective-permute-start.25 = (bf16[128,384]{1,0:T(8,128)(2,1)S(1)}, bf16[128,384]{1,0:T(8,128)(2,1)S(1)}, u32[]{:S(2)}, u32[]{:S(2)}) collective-permute-start(bf16[128,384]{1,0:T(8,128)(2,1)S(1)} %select_select_fusion), channel_id=1, source_target_pairs={{0,8},{2,10},{4,12},{6,14},{8,0},{10,2},{12,4},{14,6},{1,9},{3,11}... | collective-permute-start | bytes 294920 | tf_op jit(solution)/shard_map/ppermute | solution.py:391
  47.8 18.1 %collective-permute-start.18 = (bf16[2,2,128,384]{3,2,1,0:T(8,128)(2,1)}, bf16[2,2,128,384]{3,2,1,0:T(8,128)(2,1)S(1)}, u32[]{:S(2)}, u32[]{:S(2)}) collective-permute-start(bf16[2,2,128,384]{3,2,1,0:T(8,128)(2,1)} %get-tuple-element.89), channel_id=1, source_target_pairs={{0,4},{2,6},{4,0},{6,2},{8,12},{10,14},{12,8},{14,10},{1,5},{3,7},... | collective-permute-start | bytes 1179656 | tf_op jit(solution)/shard_map/ppermute | solution.py:372
  49.7 14.3 %collective-permute-start.17 = (bf16[2,2,128,384]{3,2,1,0:T(8,128)(2,1)}, bf16[2,2,128,384]{3,2,1,0:T(8,128)(2,1)S(1)}, u32[]{:S(2)}, u32[]{:S(2)}) collective-permute-start(bf16[2,2,128,384]{3,2,1,0:T(8,128)(2,1)} %get-tuple-element.88), channel_id=1, source_target_pairs={{0,2},{2,0},{4,6},{6,4},{8,10},{10,8},{12,14},{14,12},{1,3},{3,1},... | collective-permute-start | bytes 1179656 | tf_op jit(solution)/shard_map/ppermute | solution.py:372
  51.4 9.1 %collective-permute-start.11 = (bf16[128,384]{1,0:T(8,128)(2,1)S(1)}, bf16[128,384]{1,0:T(8,128)(2,1)S(1)}, u32[]{:S(2)}, u32[]{:S(2)}) collective-permute-start(bf16[128,384]{1,0:T(8,128)(2,1)S(1)} %select_select_fusion.1), channel_id=1, source_target_pairs={{0,8},{2,10},{4,12},{6,14},{8,0},{10,2},{12,4},{14,6},{1,9},{3,11}... | collective-permute-start | bytes 294920 | tf_op jit(solution)/shard_map/ppermute | solution.py:391
  54.2 9.3 %collective-permute-start.13 = (bf16[128,384]{1,0:T(8,128)(2,1)S(1)}, bf16[128,384]{1,0:T(8,128)(2,1)S(1)}, u32[]{:S(2)}, u32[]{:S(2)}) collective-permute-start(bf16[128,384]{1,0:T(8,128)(2,1)S(1)} %collective-permute-done.8.refs_1_.refs_13_), channel_id=1, source_target_pairs={{0,1},{1,0},{2,3},{3,2},{4,5},{5,4},{6,7},{7,6},{8,9},{9,8},{10,11... | collective-permute-start | bytes 294920 | tf_op jit(solution)/shard_map/ppermute | solution.py:369
  54.3 9.3 %collective-permute-start.14 = (bf16[128,384]{1,0:T(8,128)(2,1)S(1)}, bf16[128,384]{1,0:T(8,128)(2,1)S(1)}, u32[]{:S(2)}, u32[]{:S(2)}) collective-permute-start(bf16[128,384]{1,0:T(8,128)(2,1)S(1)} %collective-permute-done.9.refs_2_.refs_14_), channel_id=1, source_target_pairs={{0,1},{1,0},{2,3},{3,2},{4,5},{5,4},{6,7},{7,6},{8,9},{9,8},{10,11... | collective-permute-start | bytes 294920 | tf_op jit(solution)/shard_map/ppermute | solution.py:369
  60.4 11.1 %collective-permute-start.31 = (bf16[2,2,128,384]{3,2,1,0:T(8,128)(2,1)S(1)}, bf16[2,2,128,384]{3,2,1,0:T(8,128)(2,1)S(1)}, u32[]{:S(2)}, u32[]{:S(2)}) collective-permute-start(bf16[2,2,128,384]{3,2,1,0:T(8,128)(2,1)S(1)} %copy-done.9), channel_id=1, source_target_pairs={{0,6},{2,4},{4,2},{6,0},{8,14},{10,12},{12,10},{14,8},{1,7},{3,5},... | collective-permute-start | bytes 1179656 | tf_op jit(solution)/shard_map/ppermute | solution.py:372
  63.6 2.1 %collective-permute-start.19 = (bf16[2,128,384]{2,1,0:T(8,128)(2,1)S(1)}, bf16[2,128,384]{2,1,0:T(8,128)(2,1)S(1)}, u32[]{:S(2)}, u32[]{:S(2)}) collective-permute-start(bf16[2,128,384]{2,1,0:T(8,128)(2,1)S(1)} %slice_bitcast_fusion.7), channel_id=1, source_target_pairs={{0,1},{1,0},{2,3},{3,2},{4,5},{5,4},{6,7},{7,6},{8,9},{9,8},{10,11... | collective-permute-start | bytes 589832 | tf_op jit(solution)/shard_map/ppermute | solution.py:369
  63.6 1.6 %collective-permute-start.15 = (bf16[128,384]{1,0:T(8,128)(2,1)S(1)}, bf16[128,384]{1,0:T(8,128)(2,1)S(1)}, u32[]{:S(2)}, u32[]{:S(2)}) collective-permute-start(bf16[128,384]{1,0:T(8,128)(2,1)S(1)} %collective-permute-done.10.refs_3_.refs_15_), channel_id=1, source_target_pairs={{0,1},{1,0},{2,3},{3,2},{4,5},{5,4},{6,7},{7,6},{8,9},{9,8},{10,11... | collective-permute-start | bytes 294920 | tf_op jit(solution)/shard_map/ppermute | solution.py:369
  64.1 1.3 %collective-permute-start.16 = (bf16[128,384]{1,0:T(8,128)(2,1)S(1)}, bf16[128,384]{1,0:T(8,128)(2,1)S(1)}, u32[]{:S(2)}, u32[]{:S(2)}) collective-permute-start(bf16[128,384]{1,0:T(8,128)(2,1)S(1)} %collective-permute-done.11.refs_4_.refs_5_), channel_id=1, source_target_pairs={{0,1},{1,0},{2,3},{3,2},{4,5},{5,4},{6,7},{7,6},{8,9},{9,8},{10,11... | collective-permute-start | bytes 294920 | tf_op jit(solution)/shard_map/ppermute | solution.py:369
  65.1 5.4 %collective-permute-start.26 = (bf16[128,384]{1,0:T(8,128)(2,1)S(1)}, bf16[128,384]{1,0:T(8,128)(2,1)S(1)}, u32[]{:S(2)}, u32[]{:S(2)}) collective-permute-start(bf16[128,384]{1,0:T(8,128)(2,1)S(1)} %squeeze.44.refs_0_), channel_id=1, source_target_pairs={{0,1},{1,0},{2,3},{3,2},{4,5},{5,4},{6,7},{7,6},{8,9},{9,8},{10,11... | collective-permute-start | bytes 294920 | tf_op jit(solution)/shard_map/ppermute | solution.py:369
  65.4 1.9 %collective-permute-start.20 = (bf16[2,128,384]{2,1,0:T(8,128)(2,1)S(1)}, bf16[2,128,384]{2,1,0:T(8,128)(2,1)S(1)}, u32[]{:S(2)}, u32[]{:S(2)}) collective-permute-start(bf16[2,128,384]{2,1,0:T(8,128)(2,1)S(1)} %slice_bitcast_fusion.6), channel_id=1, source_target_pairs={{0,1},{1,0},{2,3},{3,2},{4,5},{5,4},{6,7},{7,6},{8,9},{9,8},{10,11... | collective-permute-start | bytes 589832 | tf_op jit(solution)/shard_map/ppermute | solution.py:369
  65.7 1.9 %collective-permute-start.21 = (bf16[2,128,384]{2,1,0:T(8,128)(2,1)S(1)}, bf16[2,128,384]{2,1,0:T(8,128)(2,1)S(1)}, u32[]{:S(2)}, u32[]{:S(2)}) collective-permute-start(bf16[2,128,384]{2,1,0:T(8,128)(2,1)S(1)} %slice_bitcast_fusion.5), channel_id=1, source_target_pairs={{0,1},{1,0},{2,3},{3,2},{4,5},{5,4},{6,7},{7,6},{8,9},{9,8},{10,11... | collective-permute-start | bytes 589832 | tf_op jit(solution)/shard_map/ppermute | solution.py:369
  65.9 2.0 %collective-permute-start.22 = (bf16[2,128,384]{2,1,0:T(8,128)(2,1)S(1)}, bf16[2,128,384]{2,1,0:T(8,128)(2,1)S(1)}, u32[]{:S(2)}, u32[]{:S(2)}) collective-permute-start(bf16[2,128,384]{2,1,0:T(8,128)(2,1)S(1)} %slice_bitcast_fusion.4), channel_id=1, source_target_pairs={{0,1},{1,0},{2,3},{3,2},{4,5},{5,4},{6,7},{7,6},{8,9},{9,8},{10,11... | collective-permute-start | bytes 589832 | tf_op jit(solution)/shard_map/ppermute | solution.py:369
  67.3 7.0 %collective-permute-start.27 = (bf16[128,384]{1,0:T(8,128)(2,1)S(1)}, bf16[128,384]{1,0:T(8,128)(2,1)S(1)}, u32[]{:S(2)}, u32[]{:S(2)}) collective-permute-start(bf16[128,384]{1,0:T(8,128)(2,1)S(1)} %collective-permute-done.3.refs_1_), channel_id=1, source_target_pairs={{0,1},{1,0},{2,3},{3,2},{4,5},{5,4},{6,7},{7,6},{8,9},{9,8},{10,11... | collective-permute-start | bytes 294920 | tf_op jit(solution)/shard_map/ppermute | solution.py:369
  67.6 6.8 %collective-permute-start.28 = (bf16[128,384]{1,0:T(8,128)(2,1)S(1)}, bf16[128,384]{1,0:T(8,128)(2,1)S(1)}, u32[]{:S(2)}, u32[]{:S(2)}) collective-permute-start(bf16[128,384]{1,0:T(8,128)(2,1)S(1)} %collective-permute-done.24.refs_2_), channel_id=1, source_target_pairs={{0,1},{1,0},{2,3},{3,2},{4,5},{5,4},{6,7},{7,6},{8,9},{9,8},{10,11... | collective-permute-start | bytes 294920 | tf_op jit(solution)/shard_map/ppermute | solution.py:369
  67.9 7.0 %collective-permute-start.29 = (bf16[128,384]{1,0:T(8,128)(2,1)S(1)}, bf16[128,384]{1,0:T(8,128)(2,1)S(1)}, u32[]{:S(2)}, u32[]{:S(2)}) collective-permute-start(bf16[128,384]{1,0:T(8,128)(2,1)S(1)} %collective-permute-done.4.refs_3_), channel_id=1, source_target_pairs={{0,1},{1,0},{2,3},{3,2},{4,5},{5,4},{6,7},{7,6},{8,9},{9,8},{10,11... | collective-permute-start | bytes 294920 | tf_op jit(solution)/shard_map/ppermute | solution.py:369
  70.6 7.8 %copy-start.4 = (bf16[2,2,128,384]{3,2,1,0:T(8,128)(2,1)S(1)}, bf16[2,2,128,384]{3,2,1,0:T(8,128)(2,1)}, u32[]{:S(2)}) copy-start(bf16[2,2,128,384]{3,2,1,0:T(8,128)(2,1)} %get-tuple-element.118.refs_0_) | copy-start | bytes 1179652
  70.6 4.4 %collective-permute-start.30 = (bf16[128,384]{1,0:T(8,128)(2,1)S(1)}, bf16[128,384]{1,0:T(8,128)(2,1)S(1)}, u32[]{:S(2)}, u32[]{:S(2)}) collective-permute-start(bf16[128,384]{1,0:T(8,128)(2,1)S(1)} %collective-permute-done.25.refs_4_.refs_5_), channel_id=1, source_target_pairs={{0,1},{1,0},{2,3},{3,2},{4,5},{5,4},{6,7},{7,6},{8,9},{9,8},{10,11... | collective-permute-start | bytes 294920 | tf_op jit(solution)/shard_map/ppermute | solution.py:369
  71.5 22.8 %collective-permute-start.23 = (bf16[384,384]{1,0:T(8,128)(2,1)S(1)}, bf16[384,384]{1,0:T(8,128)(2,1)S(1)}, u32[]{:S(2)}, u32[]{:S(2)}) collective-permute-start(bf16[384,384]{1,0:T(8,128)(2,1)S(1)} %get-tuple-element.108), channel_id=1, source_target_pairs={{0,8},{2,10},{4,12},{6,14},{8,0},{10,2},{12,4},{14,6},{1,9},{3,11}... | collective-permute-start | bytes 884744 | tf_op jit(solution)/shard_map/ppermute | solution.py:391
  74.3 4.0 %collective-permute-start.32 = (bf16[2,128,384]{2,1,0:T(8,128)(2,1)S(1)}, bf16[2,128,384]{2,1,0:T(8,128)(2,1)S(1)}, u32[]{:S(2)}, u32[]{:S(2)}) collective-permute-start(bf16[2,128,384]{2,1,0:T(8,128)(2,1)S(1)} %slice_bitcast_fusion.3), channel_id=1, source_target_pairs={{0,1},{1,0},{2,3},{3,2},{4,5},{5,4},{6,7},{7,6},{8,9},{9,8},{10,11... | collective-permute-start | bytes 589832 | tf_op jit(solution)/shard_map/ppermute | solution.py:369
  74.4 3.9 %collective-permute-start.33 = (bf16[2,128,384]{2,1,0:T(8,128)(2,1)S(1)}, bf16[2,128,384]{2,1,0:T(8,128)(2,1)S(1)}, u32[]{:S(2)}, u32[]{:S(2)}) collective-permute-start(bf16[2,128,384]{2,1,0:T(8,128)(2,1)S(1)} %slice_bitcast_fusion.2), channel_id=1, source_target_pairs={{0,1},{1,0},{2,3},{3,2},{4,5},{5,4},{6,7},{7,6},{8,9},{9,8},{10,11... | collective-permute-start | bytes 589832 | tf_op jit(solution)/shard_map/ppermute | solution.py:369
  74.9 3.5 %collective-permute-start.34 = (bf16[2,128,384]{2,1,0:T(8,128)(2,1)S(1)}, bf16[2,128,384]{2,1,0:T(8,128)(2,1)S(1)}, u32[]{:S(2)}, u32[]{:S(2)}) collective-permute-start(bf16[2,128,384]{2,1,0:T(8,128)(2,1)S(1)} %slice_bitcast_fusion.1), channel_id=1, source_target_pairs={{0,1},{1,0},{2,3},{3,2},{4,5},{5,4},{6,7},{7,6},{8,9},{9,8},{10,11... | collective-permute-start | bytes 589832 | tf_op jit(solution)/shard_map/ppermute | solution.py:369
  75.0 3.4 %collective-permute-start.35 = (bf16[2,128,384]{2,1,0:T(8,128)(2,1)S(1)}, bf16[2,128,384]{2,1,0:T(8,128)(2,1)S(1)}, u32[]{:S(2)}, u32[]{:S(2)}) collective-permute-start(bf16[2,128,384]{2,1,0:T(8,128)(2,1)S(1)} %slice_bitcast_fusion), channel_id=1, source_target_pairs={{0,1},{1,0},{2,3},{3,2},{4,5},{5,4},{6,7},{7,6},{8,9},{9,8},{10,11... | collective-permute-start | bytes 589832 | tf_op jit(solution)/shard_map/ppermute | solution.py:369
  80.4 20.0 %collective-permute-start.36 = (bf16[400,384]{1,0:T(8,128)(2,1)S(1)}, bf16[400,384]{1,0:T(8,128)(2,1)S(1)}, u32[]{:S(2)}, u32[]{:S(2)}) collective-permute-start(bf16[400,384]{1,0:T(8,128)(2,1)S(1)} %get-tuple-element.120), channel_id=1, source_target_pairs={{0,8},{2,10},{4,12},{6,14},{8,0},{10,2},{12,4},{14,6},{1,9},{3,11}... | collective-permute-start | bytes 921608 | tf_op jit(solution)/shard_map/ppermute | solution.py:391

commit v4 on v3

--- a/solution.py
+++ b/solution.py
@@ -12,7 +12,7 @@
 block_frames = 4
 members = cores * block_frames
 lanes = 128
-chunk = 768
+chunk = 1536
 narrow, wide = jnp.bfloat16, jnp.float32
 
 

time: 103 us -> 102 us (level)
  transfers between devices with their start and end apart: 37 -> 37, of which waited for: 10 -> 10; matrix products, arithmetic and copies ran while one was open for 4% -> 4% of each run, Pallas kernels for 23% -> 22%
where the time goes in v4:
time: 102 us
  starting transfers between devices  35.6 us (35%)
  waiting for transfers between devices  33.3 us (33%)
  Pallas kernels  22.4 us (22%)
  local copies, waits for them, and re-layouts  6.11 us (6%)
  other arithmetic  3.49 us (3%)
    ppermute x4, waiting for transfers between devices, across(): lax.ppermute(value, 'tm', [(i, (i + step * block_frames) % count) for i i...  24.5 us
    ppermute x12, starting transfers between devices, block_swap(): return lax.ppermute(value, 'tm', [(i, i ^ step) for i in range(count)])  23.5 us
    pallas_call x1, Pallas kernels, lift(): pl.pallas_call(lift_kernel, out_shape=(jax.ShapeDtypeStruct((tokens, feat...  9.82 us
    ppermute x12, waiting for transfers between devices, block_swap(): return lax.ppermute(value, 'tm', [(i, i ^ step) for i in range(count)])  7.76 us
    ppermute x4, starting transfers between devices, across(): lax.ppermute(value, 'tm', [(i, (i + step * block_frames) % count) for i i...  6.33 us
    ppermute x20, starting transfers between devices, core_swap(): return lax.ppermute(value, 'tensor', [(0, 1), (1, 0)])  4.92 us
    pallas_call x2, Pallas kernels, contract(): pl.pallas_call(body, out_shape=(jax.ShapeDtypeStruct((share, channels), w...  4.42 us
    pallas_call x2, Pallas kernels, mix(): pl.pallas_call(mix_grad_kernel if last else mix_conv_kernel, out_shape=ro...  4 us
  transfers between devices with their start and end apart: 37, of which 10 were waited for; matrix products, arithmetic and copies ran while one was open for 4% of the time, Pallas kernels for 22%

profile of v4, /device:TPU:0, one launch (start us, length us, event | category | flops | bytes accessed | tf_op | source)
XLA Modules:
  0.0 101.8 jit_solution(18269120215736684720)
XLA Ops:
  0.6 0.5 collective-permute-start
  1.1 0.1 collective-permute-start.6
  1.2 0.1 pad_add_fusion.index_ref
  1.3 1.4 %copy-done = bf16[128,6144]{1,0:T(8,128)(2,1)S(1)} copy-done((bf16[128,6144]{1,0:T(8,128)(2,1)S(1)}, bf16[128,6144]{1,0:T(8,128)(2,1)}, u32[]{:S(2)}) %copy-start) | copy-done | bytes 1572888
  2.7 0.8 split.1
  3.5 3.0 %collective-permute-start.1 = (bf16[2,2,128,384]{3,2,1,0:T(8,128)(2,1)S(1)}, bf16[2,2,128,384]{3,2,1,0:T(8,128)(2,1)S(1)}, u32[]{:S(2)}, u32[]{:S(2)}) collective-permute-start(bf16[2,2,128,384]{3,2,1,0:T(8,128)(2,1)S(1)} %get-tuple-element.73), channel_id=1, source_target_pairs={{0,2},{2,0},{4,6},{6,4},{8,10},{10,8},{12,14},{14,12},{1,3},{3,1},... | collective-permute-start | bytes 1179656 | tf_op jit(solution)/shard_map/ppermute | solution.py:372
  6.5 1.6 %collective-permute-start.2 = (bf16[2,2,128,384]{3,2,1,0:T(8,128)(2,1)S(1)}, bf16[2,2,128,384]{3,2,1,0:T(8,128)(2,1)S(1)}, u32[]{:S(2)}, u32[]{:S(2)}) collective-permute-start(bf16[2,2,128,384]{3,2,1,0:T(8,128)(2,1)S(1)} %get-tuple-element.74), channel_id=1, source_target_pairs={{0,4},{2,6},{4,0},{6,2},{8,12},{10,14},{12,8},{14,10},{1,5},{3,7},... | collective-permute-start | bytes 1179656 | tf_op jit(solution)/shard_map/ppermute | solution.py:372
  8.1 0.7 broadcast_in_dim.13.start_ref
  8.8 1.7 %copy-done.2 = bf16[3072,384]{1,0:T(8,128)(2,1)S(1)} copy-done((bf16[3072,384]{1,0:T(8,128)(2,1)S(1)}, bf16[3072,384]{1,0:T(8,128)(2,1)}, u32[]{:S(2)}) %copy-start.2) | copy-done | bytes 2359320
  10.4 1.1 %squeeze.43.start_ref = f32[128,384]{1,0:T(8,128)S(1)} custom-call(s32[2]{0:T(128)S(1)} %pad_add_fusion.index_ref, bf16[128,6144]{1,0:T(8,128)(2,1)S(1)} %copy-done.1, bf16[3072,384]{1,0:T(8,128)(2,1)S(1)} %copy-done.2, f32[1,384]{1,0:T(1,128)S(1)} %broadcast_in_dim.13.start_ref), custom_call_target="tpu_custom_call" | custom-call | tf_op jit(solution)/shard_map/squeeze/pallas_call | solution.py:223
  11.6 2.2 %squeeze.44.refs_0_ = bf16[128,384]{1,0:T(8,128)(2,1)S(1)} custom-call(s32[2]{0:T(128)S(1)} %pad_add_fusion.index_ref, bf16[128,6144]{1,0:T(8,128)(2,1)S(1)} %copy-done.1, bf16[3072,384]{1,0:T(8,128)(2,1)} %collective-permute-done.weight_ref, f32[128,384]{1,0:T(8,128)S(1)} %squeeze.43.start_ref), custom_call_target="tpu_custom_call" | custom-call | tf_op jit(solution)/shard_map/squeeze/pallas_call | solution.py:223
  13.8 2.0 %collective-permute-done.1.refs_1_ = bf16[2,2,128,384]{3,2,1,0:T(8,128)(2,1)S(1)} collective-permute-done((bf16[2,2,128,384]{3,2,1,0:T(8,128)(2,1)S(1)}, bf16[2,2,128,384]{3,2,1,0:T(8,128)(2,1)S(1)}, u32[]{:S(2)}, u32[]{:S(2)}) %collective-permute-start.1) | collective-permute-done | bytes 393248 | tf_op jit(solution)/shard_map/ppermute | solution.py:372
  15.8 1.5 %collective-permute-done.2.refs_2_ = bf16[2,2,128,384]{3,2,1,0:T(8,128)(2,1)S(1)} collective-permute-done((bf16[2,2,128,384]{3,2,1,0:T(8,128)(2,1)S(1)}, bf16[2,2,128,384]{3,2,1,0:T(8,128)(2,1)S(1)}, u32[]{:S(2)}, u32[]{:S(2)}) %collective-permute-start.2) | collective-permute-done | bytes 393248 | tf_op jit(solution)/shard_map/ppermute | solution.py:372
  17.3 0.4 collective-permute-start.3
  17.7 2.7 %collective-permute-start.4 = (bf16[128,384]{1,0:T(8,128)(2,1)S(1)}, bf16[128,384]{1,0:T(8,128)(2,1)S(1)}, u32[]{:S(2)}, u32[]{:S(2)}) collective-permute-start(bf16[128,384]{1,0:T(8,128)(2,1)S(1)} %squeeze.44.refs_0_), channel_id=1, source_target_pairs={{0,6},{2,4},{4,2},{6,0},{8,14},{10,12},{12,10},{14,8},{1,7},{3,5},... | collective-permute-start | bytes 294920 | tf_op jit(solution)/shard_map/ppermute | solution.py:372
  20.3 0.8 collective-permute-start.5
  21.2 0.7 pad_maximum_fusion.vectors_ref
  21.9 0.4 collective-permute-done.3.refs_1_
  22.2 1.0 %collective-permute-done.4.refs_3_ = bf16[128,384]{1,0:T(8,128)(2,1)S(1)} collective-permute-done((bf16[128,384]{1,0:T(8,128)(2,1)S(1)}, bf16[128,384]{1,0:T(8,128)(2,1)S(1)}, u32[]{:S(2)}, u32[]{:S(2)}) %collective-permute-start.4) | collective-permute-done | bytes 98336 | tf_op jit(solution)/shard_map/ppermute | solution.py:372
  23.3 5.6 %collective-permute-start.7 = (bf16[2,2,128,384]{3,2,1,0:T(8,128)(2,1)S(1)}, bf16[2,2,128,384]{3,2,1,0:T(8,128)(2,1)S(1)}, u32[]{:S(2)}, u32[]{:S(2)}) collective-permute-start(bf16[2,2,128,384]{3,2,1,0:T(8,128)(2,1)S(1)} %get-tuple-element.82), channel_id=1, source_target_pairs={{0,6},{2,4},{4,2},{6,0},{8,14},{10,12},{12,10},{14,8},{1,7},{3,5},... | collective-permute-start | bytes 1179656 | tf_op jit(solution)/shard_map/ppermute | solution.py:372
  28.9 0.1 pad_add_fusion.2.index_ref
  29.0 0.1 collective-permute-start.24
  29.1 0.7 add_convert_fusion.conv_ref
  29.8 9.8 %lift.1 = (bf16[128,6144]{1,0:T(8,128)(2,1)}, bf16[2,2,128,384]{3,2,1,0:T(8,128)(2,1)}, bf16[2,2,128,384]{3,2,1,0:T(8,128)(2,1)}, bf16[2,2,128,384]{3,2,1,0:T(8,...) custom-call(s32[2]{0:T(128)} %copy-done.6, bf16[128,6144]{1,0:T(8,128)(2,1)} %frames_hbm.1, ...), custom_call_target="tpu_custom_call" | custom-call | tf_op jit(solution)/shard_map/lift/pallas_call | solution.py:155
  39.7 0.1 collective-permute-start.10
  39.8 0.1 pad_add_fusion.1.targets_ref
  39.8 3.5 %collective-permute-start.8 = (bf16[128,384]{1,0:T(8,128)(2,1)}, bf16[128,384]{1,0:T(8,128)(2,1)S(1)}, u32[]{:S(2)}, u32[]{:S(2)}) collective-permute-start(bf16[128,384]{1,0:T(8,128)(2,1)} %get-tuple-element.90.refs_0_.refs_12_), channel_id=1, source_target_pairs={{0,2},{2,0},{4,6},{6,4},{8,10},{10,8},{12,14},{14,12},{1,3},{3,1},... | collective-permute-start | bytes 294920 | tf_op jit(solution)/shard_map/ppermute | solution.py:372
  43.3 2.2 %collective-permute-done.10.refs_3_.refs_15_ = bf16[128,384]{1,0:T(8,128)(2,1)S(1)} collective-permute-done((bf16[128,384]{1,0:T(8,128)(2,1)}, bf16[128,384]{1,0:T(8,128)(2,1)S(1)}, u32[]{:S(2)}, u32[]{:S(2)}) %collective-permute-start.10) | collective-permute-done | bytes 98336 | tf_op jit(solution)/shard_map/ppermute | solution.py:372
  45.5 1.5 %collective-permute-start.25 = (bf16[128,384]{1,0:T(8,128)(2,1)S(1)}, bf16[128,384]{1,0:T(8,128)(2,1)S(1)}, u32[]{:S(2)}, u32[]{:S(2)}) collective-permute-start(bf16[128,384]{1,0:T(8,128)(2,1)S(1)} %select_select_fusion), channel_id=1, source_target_pairs={{0,8},{2,10},{4,12},{6,14},{8,0},{10,2},{12,4},{14,6},{1,9},{3,11}... | collective-permute-start | bytes 294920 | tf_op jit(solution)/shard_map/ppermute | solution.py:391
  47.1 2.0 %collective-permute-start.18 = (bf16[2,2,128,384]{3,2,1,0:T(8,128)(2,1)}, bf16[2,2,128,384]{3,2,1,0:T(8,128)(2,1)S(1)}, u32[]{:S(2)}, u32[]{:S(2)}) collective-permute-start(bf16[2,2,128,384]{3,2,1,0:T(8,128)(2,1)} %get-tuple-element.89), channel_id=1, source_target_pairs={{0,4},{2,6},{4,0},{6,2},{8,12},{10,14},{12,8},{14,10},{1,5},{3,7},... | collective-permute-start | bytes 1179656 | tf_op jit(solution)/shard_map/ppermute | solution.py:372
  49.1 1.6 %collective-permute-start.17 = (bf16[2,2,128,384]{3,2,1,0:T(8,128)(2,1)}, bf16[2,2,128,384]{3,2,1,0:T(8,128)(2,1)S(1)}, u32[]{:S(2)}, u32[]{:S(2)}) collective-permute-start(bf16[2,2,128,384]{3,2,1,0:T(8,128)(2,1)} %get-tuple-element.88), channel_id=1, source_target_pairs={{0,2},{2,0},{4,6},{6,4},{8,10},{10,8},{12,14},{14,12},{1,3},{3,1},... | collective-permute-start | bytes 1179656 | tf_op jit(solution)/shard_map/ppermute | solution.py:372
  50.7 1.8 %collective-permute-start.11 = (bf16[128,384]{1,0:T(8,128)(2,1)S(1)}, bf16[128,384]{1,0:T(8,128)(2,1)S(1)}, u32[]{:S(2)}, u32[]{:S(2)}) collective-permute-start(bf16[128,384]{1,0:T(8,128)(2,1)S(1)} %select_select_fusion.1), channel_id=1, source_target_pairs={{0,8},{2,10},{4,12},{6,14},{8,0},{10,2},{12,4},{14,6},{1,9},{3,11}... | collective-permute-start | bytes 294920 | tf_op jit(solution)/shard_map/ppermute | solution.py:391
  52.5 0.9 slice_bitcast_fusion.3
  53.5 0.1 collective-permute-start.13
  53.6 0.5 collective-permute-start.14
  54.1 5.6 %collective-permute-done.11.refs_4_.refs_5_ = bf16[128,384]{1,0:T(8,128)(2,1)S(1)} collective-permute-done((bf16[128,384]{1,0:T(8,128)(2,1)S(1)}, bf16[128,384]{1,0:T(8,128)(2,1)S(1)}, u32[]{:S(2)}, u32[]{:S(2)}) %collective-permute-start.11) | collective-permute-done | bytes 98336 | tf_op jit(solution)/shard_map/ppermute | solution.py:391
  59.7 3.1 %collective-permute-start.31 = (bf16[2,2,128,384]{3,2,1,0:T(8,128)(2,1)S(1)}, bf16[2,2,128,384]{3,2,1,0:T(8,128)(2,1)S(1)}, u32[]{:S(2)}, u32[]{:S(2)}) collective-permute-start(bf16[2,2,128,384]{3,2,1,0:T(8,128)(2,1)S(1)} %copy-done.9), channel_id=1, source_target_pairs={{0,6},{2,4},{4,2},{6,0},{8,14},{10,12},{12,10},{14,8},{1,7},{3,5},... | collective-permute-start | bytes 1179656 | tf_op jit(solution)/shard_map/ppermute | solution.py:372
  62.9 0.5 collective-permute-start.15
  63.5 1.0 collective-permute-done.15.refs_9_.refs_19_
  64.4 0.2 collective-permute-start.26
  64.7 0.3 collective-permute-start.20
  65.0 0.2 collective-permute-start.21
  65.2 0.3 collective-permute-start.22
  65.5 1.1 %mix_grad.1.rows_ref.grad_ref = bf16[2,4,128,384]{3,2,1,0:T(8,128)(2,1)S(1)} custom-call(s32[3]{0:T(128)S(1)} %pad_add_fusion.2.index_ref, f32[3,384]{1,0:T(4,128)S(1)} %copy-done.5, bf16[128,384]{1,0:T(8,128)(2,1)S(1)} %copy-done.3, bf16[128,384]{1,0:T(8,128)(2,1)S(1)} %collective-permute-done.8.refs_1_.refs_13_, ...), custom_call_target="tpu_custom_call" | custom-call | tf_op jit(solution)/shard_map/mix_grad/pallas_call | solution.py:288
  66.6 0.3 collective-permute-start.27
  66.9 0.3 collective-permute-start.28
  67.2 0.2 collective-permute-start.29
  67.4 2.5 %contract_down.1 = (f32[384,384]{1,0:T(8,128)S(1)}, f32[1,384]{1,0:T(1,128)}, bf16[384,384]{1,0:T(8,128)(2,1)S(1)}) custom-call(s32[2]{0:T(128)S(1)} %pad_add_fusion.1.targets_ref, bf16[2,4,128,384]{3,2,1,0:T(8,128)(2,1)S(1)} %mix_grad.1.rows_ref.grad_ref, bf16[2,2,128,384]{3,2,1,0:T(8,128)(2,1)S(1)} %get-tuple-element.103.refs_0_, ...), custom_call_target="tpu_custom_call" | custom-call | tf_op jit(solution)/shard_map/contract_down/pallas_call | solution.py:337
  69.9 0.3 collective-permute-start.30
  70.2 0.7 collective-permute-done.31.refs_3_
  70.8 2.8 %collective-permute-start.23 = (bf16[384,384]{1,0:T(8,128)(2,1)S(1)}, bf16[384,384]{1,0:T(8,128)(2,1)S(1)}, u32[]{:S(2)}, u32[]{:S(2)}) collective-permute-start(bf16[384,384]{1,0:T(8,128)(2,1)S(1)} %get-tuple-element.108), channel_id=1, source_target_pairs={{0,8},{2,10},{4,12},{6,14},{8,0},{10,2},{12,4},{14,6},{1,9},{3,11}... | collective-permute-start | bytes 884744 | tf_op jit(solution)/shard_map/ppermute | solution.py:391
  73.6 0.1 collective-permute-start.32
  73.7 0.5 collective-permute-start.33
  74.2 0.1 collective-permute-start.34
  74.3 0.4 collective-permute-start.35
  74.7 2.9 %mix_conv.1 = (bf16[2,4,128,384]{3,2,1,0:T(8,128)(2,1)S(1)}, f32[8,384]{1,0:T(8,128)S(1)}) custom-call(s32[3]{0:T(128)S(1)} %pad_add_fusion.2.index_ref, f32[3,384]{1,0:T(4,128)S(1)} %copy-done.5, bf16[2,4,128,384]{3,2,1,0:T(8,128)(2,1)S(1)} %mix_grad.1.rows_ref.grad_ref, bf16[128,384]{1,0:T(8,128)(2,1)S(1)} %squeeze.44.refs_0_, ...), custom_call_target="tpu_custom_call" | custom-call | tf_op jit(solution)/shard_map/mix_conv/pallas_call | solution.py:288
  77.7 2.0 %contract_up.1 = (f32[384,384]{1,0:T(8,128)S(1)}, f32[1,384]{1,0:T(1,128)S(1)}, bf16[400,384]{1,0:T(8,128)(2,1)S(1)}) custom-call(s32[2]{0:T(128)S(1)} %pad_add_fusion.1.targets_ref, bf16[2,4,128,384]{3,2,1,0:T(8,128)(2,1)S(1)} %get-tuple-element.116.rows_ref, f32[8,384]{1,0:T(8,128)S(1)} %get-tuple-element.117.small_ref, ...), custom_call_target="tpu_custom_call" | custom-call | tf_op jit(solution)/shard_map/contract_up/pallas_call | solution.py:337
  79.7 0.2 collective-permute-start.36
  80.0 13.7 %collective-permute-done.23 = bf16[384,384]{1,0:T(8,128)(2,1)S(1)} collective-permute-done((bf16[384,384]{1,0:T(8,128)(2,1)S(1)}, bf16[384,384]{1,0:T(8,128)(2,1)S(1)}, u32[]{:S(2)}, u32[]{:S(2)}) %collective-permute-start.23) | collective-permute-done | bytes 294944 | tf_op jit(solution)/shard_map/ppermute | solution.py:391
  93.7 0.9 convert_add_fusion
  94.5 5.2 %collective-permute-done.36 = bf16[400,384]{1,0:T(8,128)(2,1)S(1)} collective-permute-done((bf16[400,384]{1,0:T(8,128)(2,1)S(1)}, bf16[400,384]{1,0:T(8,128)(2,1)S(1)}, u32[]{:S(2)}, u32[]{:S(2)}) %collective-permute-start.36) | collective-permute-done | bytes 307232 | tf_op jit(solution)/shard_map/ppermute | solution.py:391
  99.7 0.6 slice.83
  100.3 0.6 slice_reduce_fusion
  100.9 0.9 slice_add_fusion
  (62 shorter events, 0.5 us)
Async XLA Ops:
  0.6 10.9 %collective-permute-start = (bf16[3072,384]{1,0:T(8,128)(2,1)}, bf16[3072,384]{1,0:T(8,128)(2,1)}, u32[]{:S(2)}, u32[]{:S(2)}) collective-permute-start(bf16[3072,384]{1,0:T(8,128)(2,1)} %weight_ref.1), channel_id=1, source_target_pairs={{0,1},{1,0},{2,3},{3,2},{4,5},{5,4},{6,7},{7,6},{8,9},{9,8},{10,11... | collective-permute-start | bytes 7077896 | tf_op jit(solution)/shard_map/ppermute | solution.py:369
  1.1 28.7 %collective-permute-start.6 = (bf16[3072,384]{1,0:T(8,128)(2,1)}, bf16[3072,384]{1,0:T(8,128)(2,1)}, u32[]{:S(2)}, u32[]{:S(2)}) collective-permute-start(bf16[3072,384]{1,0:T(8,128)(2,1)} %own_hbm.1), channel_id=1, source_target_pairs={{0,1},{1,0},{2,3},{3,2},{4,5},{5,4},{6,7},{7,6},{8,9},{9,8},{10,11... | collective-permute-start | bytes 7077896 | tf_op jit(solution)/shard_map/ppermute | solution.py:369
  1.3 1.4 %copy-start = (bf16[128,6144]{1,0:T(8,128)(2,1)S(1)}, bf16[128,6144]{1,0:T(8,128)(2,1)}, u32[]{:S(2)}) copy-start(bf16[128,6144]{1,0:T(8,128)(2,1)} %frames_hbm.1) | copy-start | bytes 4718596
  2.7 8.9 %copy-start.6 = (s32[2]{0:T(128)}, s32[2]{0:T(128)S(1)}, u32[]{:S(2)}) copy-start(s32[2]{0:T(128)S(1)} %pad_add_fusion.index_ref) | copy-start | bytes 28
  2.7 6.0 %copy-start.1 = (bf16[128,6144]{1,0:T(8,128)(2,1)S(1)}, bf16[128,6144]{1,0:T(8,128)(2,1)}, u32[]{:S(2)}) copy-start(bf16[128,6144]{1,0:T(8,128)(2,1)} %frames_hbm.1) | copy-start | bytes 4718596
  3.5 12.4 %collective-permute-start.1 = (bf16[2,2,128,384]{3,2,1,0:T(8,128)(2,1)S(1)}, bf16[2,2,128,384]{3,2,1,0:T(8,128)(2,1)S(1)}, u32[]{:S(2)}, u32[]{:S(2)}) collective-permute-start(bf16[2,2,128,384]{3,2,1,0:T(8,128)(2,1)S(1)} %get-tuple-element.73), channel_id=1, source_target_pairs={{0,2},{2,0},{4,6},{6,4},{8,10},{10,8},{12,14},{14,12},{1,3},{3,1},... | collective-permute-start | bytes 1179656 | tf_op jit(solution)/shard_map/ppermute | solution.py:372
  6.5 10.8 %collective-permute-start.2 = (bf16[2,2,128,384]{3,2,1,0:T(8,128)(2,1)S(1)}, bf16[2,2,128,384]{3,2,1,0:T(8,128)(2,1)S(1)}, u32[]{:S(2)}, u32[]{:S(2)}) collective-permute-start(bf16[2,2,128,384]{3,2,1,0:T(8,128)(2,1)S(1)} %get-tuple-element.74), channel_id=1, source_target_pairs={{0,4},{2,6},{4,0},{6,2},{8,12},{10,14},{12,8},{14,10},{1,5},{3,7},... | collective-permute-start | bytes 1179656 | tf_op jit(solution)/shard_map/ppermute | solution.py:372
  8.8 1.7 %copy-start.2 = (bf16[3072,384]{1,0:T(8,128)(2,1)S(1)}, bf16[3072,384]{1,0:T(8,128)(2,1)}, u32[]{:S(2)}) copy-start(bf16[3072,384]{1,0:T(8,128)(2,1)} %weight_ref.1) | copy-start | bytes 7077892
  11.5 9.7 %copy-start.7 = (f32[6144]{0:T(1024)S(1)}, f32[6144]{0:T(1024)}, u32[]{:S(2)}) copy-start(f32[6144]{0:T(1024)} %param.17) | copy-start | bytes 73732
  11.5 9.7 %copy-start.8 = (f32[6144]{0:T(1024)S(1)}, f32[6144]{0:T(1024)}, u32[]{:S(2)}) copy-start(f32[6144]{0:T(1024)} %param.16) | copy-start | bytes 73732
  11.6 17.4 %copy-start.5 = (f32[3,384]{1,0:T(4,128)S(1)}, f32[3,384]{1,0:T(4,128)}, u32[]{:S(2)}) copy-start(f32[3,384]{1,0:T(4,128)} %taps_ref.3) | copy-start | bytes 13828
  17.3 4.9 %collective-permute-start.3 = (bf16[128,384]{1,0:T(8,128)(2,1)S(1)}, bf16[128,384]{1,0:T(8,128)(2,1)S(1)}, u32[]{:S(2)}, u32[]{:S(2)}) collective-permute-start(bf16[128,384]{1,0:T(8,128)(2,1)S(1)} %squeeze.44.refs_0_), channel_id=1, source_target_pairs={{0,2},{2,0},{4,6},{6,4},{8,10},{10,8},{12,14},{14,12},{1,3},{3,1},... | collective-permute-start | bytes 294920 | tf_op jit(solution)/shard_map/ppermute | solution.py:372
  17.7 5.6 %collective-permute-start.4 = (bf16[128,384]{1,0:T(8,128)(2,1)S(1)}, bf16[128,384]{1,0:T(8,128)(2,1)S(1)}, u32[]{:S(2)}, u32[]{:S(2)}) collective-permute-start(bf16[128,384]{1,0:T(8,128)(2,1)S(1)} %squeeze.44.refs_0_), channel_id=1, source_target_pairs={{0,6},{2,4},{4,2},{6,0},{8,14},{10,12},{12,10},{14,8},{1,7},{3,5},... | collective-permute-start | bytes 294920 | tf_op jit(solution)/shard_map/ppermute | solution.py:372
  20.3 2.9 %collective-permute-start.5 = (bf16[128,384]{1,0:T(8,128)(2,1)S(1)}, bf16[128,384]{1,0:T(8,128)(2,1)S(1)}, u32[]{:S(2)}, u32[]{:S(2)}) collective-permute-start(bf16[128,384]{1,0:T(8,128)(2,1)S(1)} %squeeze.44.refs_0_), channel_id=1, source_target_pairs={{6,8},{8,6},{7,9},{9,7},{22,24},{24,22},{23,25},{25,23}} | collective-permute-start | bytes 294920 | tf_op jit(solution)/shard_map/ppermute | solution.py:386
  23.3 16.4 %collective-permute-start.7 = (bf16[2,2,128,384]{3,2,1,0:T(8,128)(2,1)S(1)}, bf16[2,2,128,384]{3,2,1,0:T(8,128)(2,1)S(1)}, u32[]{:S(2)}, u32[]{:S(2)}) collective-permute-start(bf16[2,2,128,384]{3,2,1,0:T(8,128)(2,1)S(1)} %get-tuple-element.82), channel_id=1, source_target_pairs={{0,6},{2,4},{4,2},{6,0},{8,14},{10,12},{12,10},{14,8},{1,7},{3,5},... | collective-permute-start | bytes 1179656 | tf_op jit(solution)/shard_map/ppermute | solution.py:372
  29.0 14.3 %collective-permute-start.24 = (bf16[128,384]{1,0:T(8,128)(2,1)S(1)}, bf16[128,384]{1,0:T(8,128)(2,1)S(1)}, u32[]{:S(2)}, u32[]{:S(2)}) collective-permute-start(bf16[128,384]{1,0:T(8,128)(2,1)S(1)} %squeeze.44.refs_0_), channel_id=1, source_target_pairs={{0,4},{2,6},{4,0},{6,2},{8,12},{10,14},{12,8},{14,10},{1,5},{3,7},... | collective-permute-start | bytes 294920 | tf_op jit(solution)/shard_map/ppermute | solution.py:372
  39.7 20.1 %copy-start.9 = (bf16[2,2,128,384]{3,2,1,0:T(8,128)(2,1)S(1)}, bf16[2,2,128,384]{3,2,1,0:T(8,128)(2,1)}, u32[]{:S(2)}) copy-start(bf16[2,2,128,384]{3,2,1,0:T(8,128)(2,1)} %get-tuple-element.119) | copy-start | bytes 1179652
  39.7 25.8 %copy-start.3 = (bf16[128,384]{1,0:T(8,128)(2,1)S(1)}, bf16[128,384]{1,0:T(8,128)(2,1)}, u32[]{:S(2)}) copy-start(bf16[128,384]{1,0:T(8,128)(2,1)} %get-tuple-element.90.refs_0_.refs_12_) | copy-start | bytes 294916
  39.7 5.8 %collective-permute-start.10 = (bf16[128,384]{1,0:T(8,128)(2,1)}, bf16[128,384]{1,0:T(8,128)(2,1)S(1)}, u32[]{:S(2)}, u32[]{:S(2)}) collective-permute-start(bf16[128,384]{1,0:T(8,128)(2,1)} %get-tuple-element.90.refs_0_.refs_12_), channel_id=1, source_target_pairs={{0,6},{2,4},{4,2},{6,0},{8,14},{10,12},{12,10},{14,8},{1,7},{3,5},... | collective-permute-start | bytes 294920 | tf_op jit(solution)/shard_map/ppermute | solution.py:372
  39.8 7.2 %collective-permute-start.8 = (bf16[128,384]{1,0:T(8,128)(2,1)}, bf16[128,384]{1,0:T(8,128)(2,1)S(1)}, u32[]{:S(2)}, u32[]{:S(2)}) collective-permute-start(bf16[128,384]{1,0:T(8,128)(2,1)} %get-tuple-element.90.refs_0_.refs_12_), channel_id=1, source_target_pairs={{0,2},{2,0},{4,6},{6,4},{8,10},{10,8},{12,14},{14,12},{1,3},{3,1},... | collective-permute-start | bytes 294920 | tf_op jit(solution)/shard_map/ppermute | solution.py:372
  43.3 7.3 %collective-permute-start.9 = (bf16[128,384]{1,0:T(8,128)(2,1)}, bf16[128,384]{1,0:T(8,128)(2,1)S(1)}, u32[]{:S(2)}, u32[]{:S(2)}) collective-permute-start(bf16[128,384]{1,0:T(8,128)(2,1)} %get-tuple-element.90.refs_0_.refs_12_), channel_id=1, source_target_pairs={{0,4},{2,6},{4,0},{6,2},{8,12},{10,14},{12,8},{14,10},{1,5},{3,7},... | collective-permute-start | bytes 294920 | tf_op jit(solution)/shard_map/ppermute | solution.py:372
  43.3 10.2 %collective-permute-start.12 = (bf16[128,384]{1,0:T(8,128)(2,1)}, bf16[128,384]{1,0:T(8,128)(2,1)S(1)}, u32[]{:S(2)}, u32[]{:S(2)}) collective-permute-start(bf16[128,384]{1,0:T(8,128)(2,1)} %get-tuple-element.90.refs_0_.refs_12_), channel_id=1, source_target_pairs={{0,1},{1,0},{2,3},{3,2},{4,5},{5,4},{6,7},{7,6},{8,9},{9,8},{10,11... | collective-permute-start | bytes 294920 | tf_op jit(solution)/shard_map/ppermute | solution.py:369
  45.5 8.0 %collective-permute-start.25 = (bf16[128,384]{1,0:T(8,128)(2,1)S(1)}, bf16[128,384]{1,0:T(8,128)(2,1)S(1)}, u32[]{:S(2)}, u32[]{:S(2)}) collective-permute-start(bf16[128,384]{1,0:T(8,128)(2,1)S(1)} %select_select_fusion), channel_id=1, source_target_pairs={{0,8},{2,10},{4,12},{6,14},{8,0},{10,2},{12,4},{14,6},{1,9},{3,11}... | collective-permute-start | bytes 294920 | tf_op jit(solution)/shard_map/ppermute | solution.py:391
  47.1 18.1 %collective-permute-start.18 = (bf16[2,2,128,384]{3,2,1,0:T(8,128)(2,1)}, bf16[2,2,128,384]{3,2,1,0:T(8,128)(2,1)S(1)}, u32[]{:S(2)}, u32[]{:S(2)}) collective-permute-start(bf16[2,2,128,384]{3,2,1,0:T(8,128)(2,1)} %get-tuple-element.89), channel_id=1, source_target_pairs={{0,4},{2,6},{4,0},{6,2},{8,12},{10,14},{12,8},{14,10},{1,5},{3,7},... | collective-permute-start | bytes 1179656 | tf_op jit(solution)/shard_map/ppermute | solution.py:372
  49.1 14.3 %collective-permute-start.17 = (bf16[2,2,128,384]{3,2,1,0:T(8,128)(2,1)}, bf16[2,2,128,384]{3,2,1,0:T(8,128)(2,1)S(1)}, u32[]{:S(2)}, u32[]{:S(2)}) collective-permute-start(bf16[2,2,128,384]{3,2,1,0:T(8,128)(2,1)} %get-tuple-element.88), channel_id=1, source_target_pairs={{0,2},{2,0},{4,6},{6,4},{8,10},{10,8},{12,14},{14,12},{1,3},{3,1},... | collective-permute-start | bytes 1179656 | tf_op jit(solution)/shard_map/ppermute | solution.py:372
  50.7 9.1 %collective-permute-start.11 = (bf16[128,384]{1,0:T(8,128)(2,1)S(1)}, bf16[128,384]{1,0:T(8,128)(2,1)S(1)}, u32[]{:S(2)}, u32[]{:S(2)}) collective-permute-start(bf16[128,384]{1,0:T(8,128)(2,1)S(1)} %select_select_fusion.1), channel_id=1, source_target_pairs={{0,8},{2,10},{4,12},{6,14},{8,0},{10,2},{12,4},{14,6},{1,9},{3,11}... | collective-permute-start | bytes 294920 | tf_op jit(solution)/shard_map/ppermute | solution.py:391
  53.5 9.4 %collective-permute-start.13 = (bf16[128,384]{1,0:T(8,128)(2,1)S(1)}, bf16[128,384]{1,0:T(8,128)(2,1)S(1)}, u32[]{:S(2)}, u32[]{:S(2)}) collective-permute-start(bf16[128,384]{1,0:T(8,128)(2,1)S(1)} %collective-permute-done.8.refs_1_.refs_13_), channel_id=1, source_target_pairs={{0,1},{1,0},{2,3},{3,2},{4,5},{5,4},{6,7},{7,6},{8,9},{9,8},{10,11... | collective-permute-start | bytes 294920 | tf_op jit(solution)/shard_map/ppermute | solution.py:369
  53.6 9.3 %collective-permute-start.14 = (bf16[128,384]{1,0:T(8,128)(2,1)S(1)}, bf16[128,384]{1,0:T(8,128)(2,1)S(1)}, u32[]{:S(2)}, u32[]{:S(2)}) collective-permute-start(bf16[128,384]{1,0:T(8,128)(2,1)S(1)} %collective-permute-done.9.refs_2_.refs_14_), channel_id=1, source_target_pairs={{0,1},{1,0},{2,3},{3,2},{4,5},{5,4},{6,7},{7,6},{8,9},{9,8},{10,11... | collective-permute-start | bytes 294920 | tf_op jit(solution)/shard_map/ppermute | solution.py:369
  59.7 11.1 %collective-permute-start.31 = (bf16[2,2,128,384]{3,2,1,0:T(8,128)(2,1)S(1)}, bf16[2,2,128,384]{3,2,1,0:T(8,128)(2,1)S(1)}, u32[]{:S(2)}, u32[]{:S(2)}) collective-permute-start(bf16[2,2,128,384]{3,2,1,0:T(8,128)(2,1)S(1)} %copy-done.9), channel_id=1, source_target_pairs={{0,6},{2,4},{4,2},{6,0},{8,14},{10,12},{12,10},{14,8},{1,7},{3,5},... | collective-permute-start | bytes 1179656 | tf_op jit(solution)/shard_map/ppermute | solution.py:372
  62.9 2.1 %collective-permute-start.19 = (bf16[2,128,384]{2,1,0:T(8,128)(2,1)S(1)}, bf16[2,128,384]{2,1,0:T(8,128)(2,1)S(1)}, u32[]{:S(2)}, u32[]{:S(2)}) collective-permute-start(bf16[2,128,384]{2,1,0:T(8,128)(2,1)S(1)} %slice_bitcast_fusion.7), channel_id=1, source_target_pairs={{0,1},{1,0},{2,3},{3,2},{4,5},{5,4},{6,7},{7,6},{8,9},{9,8},{10,11... | collective-permute-start | bytes 589832 | tf_op jit(solution)/shard_map/ppermute | solution.py:369
  62.9 1.6 %collective-permute-start.15 = (bf16[128,384]{1,0:T(8,128)(2,1)S(1)}, bf16[128,384]{1,0:T(8,128)(2,1)S(1)}, u32[]{:S(2)}, u32[]{:S(2)}) collective-permute-start(bf16[128,384]{1,0:T(8,128)(2,1)S(1)} %collective-permute-done.10.refs_3_.refs_15_), channel_id=1, source_target_pairs={{0,1},{1,0},{2,3},{3,2},{4,5},{5,4},{6,7},{7,6},{8,9},{9,8},{10,11... | collective-permute-start | bytes 294920 | tf_op jit(solution)/shard_map/ppermute | solution.py:369
  63.4 1.3 %collective-permute-start.16 = (bf16[128,384]{1,0:T(8,128)(2,1)S(1)}, bf16[128,384]{1,0:T(8,128)(2,1)S(1)}, u32[]{:S(2)}, u32[]{:S(2)}) collective-permute-start(bf16[128,384]{1,0:T(8,128)(2,1)S(1)} %collective-permute-done.11.refs_4_.refs_5_), channel_id=1, source_target_pairs={{0,1},{1,0},{2,3},{3,2},{4,5},{5,4},{6,7},{7,6},{8,9},{9,8},{10,11... | collective-permute-start | bytes 294920 | tf_op jit(solution)/shard_map/ppermute | solution.py:369
  64.4 5.4 %collective-permute-start.26 = (bf16[128,384]{1,0:T(8,128)(2,1)S(1)}, bf16[128,384]{1,0:T(8,128)(2,1)S(1)}, u32[]{:S(2)}, u32[]{:S(2)}) collective-permute-start(bf16[128,384]{1,0:T(8,128)(2,1)S(1)} %squeeze.44.refs_0_), channel_id=1, source_target_pairs={{0,1},{1,0},{2,3},{3,2},{4,5},{5,4},{6,7},{7,6},{8,9},{9,8},{10,11... | collective-permute-start | bytes 294920 | tf_op jit(solution)/shard_map/ppermute | solution.py:369
  64.7 1.9 %collective-permute-start.20 = (bf16[2,128,384]{2,1,0:T(8,128)(2,1)S(1)}, bf16[2,128,384]{2,1,0:T(8,128)(2,1)S(1)}, u32[]{:S(2)}, u32[]{:S(2)}) collective-permute-start(bf16[2,128,384]{2,1,0:T(8,128)(2,1)S(1)} %slice_bitcast_fusion.6), channel_id=1, source_target_pairs={{0,1},{1,0},{2,3},{3,2},{4,5},{5,4},{6,7},{7,6},{8,9},{9,8},{10,11... | collective-permute-start | bytes 589832 | tf_op jit(solution)/shard_map/ppermute | solution.py:369
  65.0 1.9 %collective-permute-start.21 = (bf16[2,128,384]{2,1,0:T(8,128)(2,1)S(1)}, bf16[2,128,384]{2,1,0:T(8,128)(2,1)S(1)}, u32[]{:S(2)}, u32[]{:S(2)}) collective-permute-start(bf16[2,128,384]{2,1,0:T(8,128)(2,1)S(1)} %slice_bitcast_fusion.5), channel_id=1, source_target_pairs={{0,1},{1,0},{2,3},{3,2},{4,5},{5,4},{6,7},{7,6},{8,9},{9,8},{10,11... | collective-permute-start | bytes 589832 | tf_op jit(solution)/shard_map/ppermute | solution.py:369
  65.2 2.0 %collective-permute-start.22 = (bf16[2,128,384]{2,1,0:T(8,128)(2,1)S(1)}, bf16[2,128,384]{2,1,0:T(8,128)(2,1)S(1)}, u32[]{:S(2)}, u32[]{:S(2)}) collective-permute-start(bf16[2,128,384]{2,1,0:T(8,128)(2,1)S(1)} %slice_bitcast_fusion.4), channel_id=1, source_target_pairs={{0,1},{1,0},{2,3},{3,2},{4,5},{5,4},{6,7},{7,6},{8,9},{9,8},{10,11... | collective-permute-start | bytes 589832 | tf_op jit(solution)/shard_map/ppermute | solution.py:369
  66.6 7.0 %collective-permute-start.27 = (bf16[128,384]{1,0:T(8,128)(2,1)S(1)}, bf16[128,384]{1,0:T(8,128)(2,1)S(1)}, u32[]{:S(2)}, u32[]{:S(2)}) collective-permute-start(bf16[128,384]{1,0:T(8,128)(2,1)S(1)} %collective-permute-done.3.refs_1_), channel_id=1, source_target_pairs={{0,1},{1,0},{2,3},{3,2},{4,5},{5,4},{6,7},{7,6},{8,9},{9,8},{10,11... | collective-permute-start | bytes 294920 | tf_op jit(solution)/shard_map/ppermute | solution.py:369
  66.9 6.8 %collective-permute-start.28 = (bf16[128,384]{1,0:T(8,128)(2,1)S(1)}, bf16[128,384]{1,0:T(8,128)(2,1)S(1)}, u32[]{:S(2)}, u32[]{:S(2)}) collective-permute-start(bf16[128,384]{1,0:T(8,128)(2,1)S(1)} %collective-permute-done.24.refs_2_), channel_id=1, source_target_pairs={{0,1},{1,0},{2,3},{3,2},{4,5},{5,4},{6,7},{7,6},{8,9},{9,8},{10,11... | collective-permute-start | bytes 294920 | tf_op jit(solution)/shard_map/ppermute | solution.py:369
  67.2 7.0 %collective-permute-start.29 = (bf16[128,384]{1,0:T(8,128)(2,1)S(1)}, bf16[128,384]{1,0:T(8,128)(2,1)S(1)}, u32[]{:S(2)}, u32[]{:S(2)}) collective-permute-start(bf16[128,384]{1,0:T(8,128)(2,1)S(1)} %collective-permute-done.4.refs_3_), channel_id=1, source_target_pairs={{0,1},{1,0},{2,3},{3,2},{4,5},{5,4},{6,7},{7,6},{8,9},{9,8},{10,11... | collective-permute-start | bytes 294920 | tf_op jit(solution)/shard_map/ppermute | solution.py:369
  69.9 7.8 %copy-start.4 = (bf16[2,2,128,384]{3,2,1,0:T(8,128)(2,1)S(1)}, bf16[2,2,128,384]{3,2,1,0:T(8,128)(2,1)}, u32[]{:S(2)}) copy-start(bf16[2,2,128,384]{3,2,1,0:T(8,128)(2,1)} %get-tuple-element.118.refs_0_) | copy-start | bytes 1179652
  69.9 4.4 %collective-permute-start.30 = (bf16[128,384]{1,0:T(8,128)(2,1)S(1)}, bf16[128,384]{1,0:T(8,128)(2,1)S(1)}, u32[]{:S(2)}, u32[]{:S(2)}) collective-permute-start(bf16[128,384]{1,0:T(8,128)(2,1)S(1)} %collective-permute-done.25.refs_4_.refs_5_), channel_id=1, source_target_pairs={{0,1},{1,0},{2,3},{3,2},{4,5},{5,4},{6,7},{7,6},{8,9},{9,8},{10,11... | collective-permute-start | bytes 294920 | tf_op jit(solution)/shard_map/ppermute | solution.py:369
  70.8 22.8 %collective-permute-start.23 = (bf16[384,384]{1,0:T(8,128)(2,1)S(1)}, bf16[384,384]{1,0:T(8,128)(2,1)S(1)}, u32[]{:S(2)}, u32[]{:S(2)}) collective-permute-start(bf16[384,384]{1,0:T(8,128)(2,1)S(1)} %get-tuple-element.108), channel_id=1, source_target_pairs={{0,8},{2,10},{4,12},{6,14},{8,0},{10,2},{12,4},{14,6},{1,9},{3,11}... | collective-permute-start | bytes 884744 | tf_op jit(solution)/shard_map/ppermute | solution.py:391
  73.6 4.0 %collective-permute-start.32 = (bf16[2,128,384]{2,1,0:T(8,128)(2,1)S(1)}, bf16[2,128,384]{2,1,0:T(8,128)(2,1)S(1)}, u32[]{:S(2)}, u32[]{:S(2)}) collective-permute-start(bf16[2,128,384]{2,1,0:T(8,128)(2,1)S(1)} %slice_bitcast_fusion.3), channel_id=1, source_target_pairs={{0,1},{1,0},{2,3},{3,2},{4,5},{5,4},{6,7},{7,6},{8,9},{9,8},{10,11... | collective-permute-start | bytes 589832 | tf_op jit(solution)/shard_map/ppermute | solution.py:369
  73.7 3.9 %collective-permute-start.33 = (bf16[2,128,384]{2,1,0:T(8,128)(2,1)S(1)}, bf16[2,128,384]{2,1,0:T(8,128)(2,1)S(1)}, u32[]{:S(2)}, u32[]{:S(2)}) collective-permute-start(bf16[2,128,384]{2,1,0:T(8,128)(2,1)S(1)} %slice_bitcast_fusion.2), channel_id=1, source_target_pairs={{0,1},{1,0},{2,3},{3,2},{4,5},{5,4},{6,7},{7,6},{8,9},{9,8},{10,11... | collective-permute-start | bytes 589832 | tf_op jit(solution)/shard_map/ppermute | solution.py:369
  74.2 3.5 %collective-permute-start.34 = (bf16[2,128,384]{2,1,0:T(8,128)(2,1)S(1)}, bf16[2,128,384]{2,1,0:T(8,128)(2,1)S(1)}, u32[]{:S(2)}, u32[]{:S(2)}) collective-permute-start(bf16[2,128,384]{2,1,0:T(8,128)(2,1)S(1)} %slice_bitcast_fusion.1), channel_id=1, source_target_pairs={{0,1},{1,0},{2,3},{3,2},{4,5},{5,4},{6,7},{7,6},{8,9},{9,8},{10,11... | collective-permute-start | bytes 589832 | tf_op jit(solution)/shard_map/ppermute | solution.py:369
  74.3 3.4 %collective-permute-start.35 = (bf16[2,128,384]{2,1,0:T(8,128)(2,1)S(1)}, bf16[2,128,384]{2,1,0:T(8,128)(2,1)S(1)}, u32[]{:S(2)}, u32[]{:S(2)}) collective-permute-start(bf16[2,128,384]{2,1,0:T(8,128)(2,1)S(1)} %slice_bitcast_fusion), channel_id=1, source_target_pairs={{0,1},{1,0},{2,3},{3,2},{4,5},{5,4},{6,7},{7,6},{8,9},{9,8},{10,11... | collective-permute-start | bytes 589832 | tf_op jit(solution)/shard_map/ppermute | solution.py:369
  79.7 20.0 %collective-permute-start.36 = (bf16[400,384]{1,0:T(8,128)(2,1)S(1)}, bf16[400,384]{1,0:T(8,128)(2,1)S(1)}, u32[]{:S(2)}, u32[]{:S(2)}) collective-permute-start(bf16[400,384]{1,0:T(8,128)(2,1)S(1)} %get-tuple-element.120), channel_id=1, source_target_pairs={{0,8},{2,10},{4,12},{6,14},{8,0},{10,2},{12,4},{14,6},{1,9},{3,11}... | collective-permute-start | bytes 921608 | tf_op jit(solution)/shard_map/ppermute | solution.py:391

commit v5 on v4

--- a/solution.py
+++ b/solution.py
@@ -12,7 +12,7 @@
 block_frames = 4
 members = cores * block_frames
 lanes = 128
-chunk = 1536
+chunk = 3072
 narrow, wide = jnp.bfloat16, jnp.float32
 
 

time: 102 us -> 102 us (level)
  no operation moved by 1% of the time
where the time goes in v5:
time: 102 us
  starting transfers between devices  35.6 us (35%)
  waiting for transfers between devices  33.2 us (33%)
  Pallas kernels  22.3 us (22%)
  local copies, waits for them, and re-layouts  6.11 us (6%)
  other arithmetic  3.49 us (3%)
    ppermute x4, waiting for transfers between devices, across(): lax.ppermute(value, 'tm', [(i, (i + step * block_frames) % count) for i i...  24.4 us
    ppermute x12, starting transfers between devices, block_swap(): return lax.ppermute(value, 'tm', [(i, i ^ step) for i in range(count)])  23.5 us
    pallas_call x1, Pallas kernels, lift(): pl.pallas_call(lift_kernel, out_shape=(jax.ShapeDtypeStruct((tokens, feat...  9.82 us
    ppermute x12, waiting for transfers between devices, block_swap(): return lax.ppermute(value, 'tm', [(i, i ^ step) for i in range(count)])  7.77 us
    ppermute x4, starting transfers between devices, across(): lax.ppermute(value, 'tm', [(i, (i + step * block_frames) % count) for i i...  6.32 us
    ppermute x20, starting transfers between devices, core_swap(): return lax.ppermute(value, 'tensor', [(0, 1), (1, 0)])  4.92 us
    pallas_call x2, Pallas kernels, contract(): pl.pallas_call(body, out_shape=(jax.ShapeDtypeStruct((share, channels), w...  4.42 us
    pallas_call x2, Pallas kernels, mix(): pl.pallas_call(mix_grad_kernel if last else mix_conv_kernel, out_shape=ro...  4 us
  transfers between devices with their start and end apart: 37, of which 10 were waited for; matrix products, arithmetic and copies ran while one was open for 4% of the time, Pallas kernels for 22%

profile of v5, /device:TPU:0, one launch (start us, length us, event | category | flops | bytes accessed | tf_op | source)
XLA Modules:
  0.0 101.8 jit_solution(8428890347658313097)
XLA Ops:
  0.6 0.5 collective-permute-start
  1.1 0.1 collective-permute-start.6
  1.2 0.1 pad_add_fusion.index_ref
  1.3 1.4 %copy-done = bf16[128,6144]{1,0:T(8,128)(2,1)S(1)} copy-done((bf16[128,6144]{1,0:T(8,128)(2,1)S(1)}, bf16[128,6144]{1,0:T(8,128)(2,1)}, u32[]{:S(2)}) %copy-start) | copy-done | bytes 1572888
  2.7 0.8 split.1
  3.5 3.0 %collective-permute-start.1 = (bf16[2,2,128,384]{3,2,1,0:T(8,128)(2,1)S(1)}, bf16[2,2,128,384]{3,2,1,0:T(8,128)(2,1)S(1)}, u32[]{:S(2)}, u32[]{:S(2)}) collective-permute-start(bf16[2,2,128,384]{3,2,1,0:T(8,128)(2,1)S(1)} %get-tuple-element.73), channel_id=1, source_target_pairs={{0,2},{2,0},{4,6},{6,4},{8,10},{10,8},{12,14},{14,12},{1,3},{3,1},... | collective-permute-start | bytes 1179656 | tf_op jit(solution)/shard_map/ppermute | solution.py:372
  6.5 1.6 %collective-permute-start.2 = (bf16[2,2,128,384]{3,2,1,0:T(8,128)(2,1)S(1)}, bf16[2,2,128,384]{3,2,1,0:T(8,128)(2,1)S(1)}, u32[]{:S(2)}, u32[]{:S(2)}) collective-permute-start(bf16[2,2,128,384]{3,2,1,0:T(8,128)(2,1)S(1)} %get-tuple-element.74), channel_id=1, source_target_pairs={{0,4},{2,6},{4,0},{6,2},{8,12},{10,14},{12,8},{14,10},{1,5},{3,7},... | collective-permute-start | bytes 1179656 | tf_op jit(solution)/shard_map/ppermute | solution.py:372
  8.1 0.7 broadcast_in_dim.13.start_ref
  8.8 1.7 %copy-done.2 = bf16[3072,384]{1,0:T(8,128)(2,1)S(1)} copy-done((bf16[3072,384]{1,0:T(8,128)(2,1)S(1)}, bf16[3072,384]{1,0:T(8,128)(2,1)}, u32[]{:S(2)}) %copy-start.2) | copy-done | bytes 2359320
  10.4 1.1 %squeeze.43.start_ref = f32[128,384]{1,0:T(8,128)S(1)} custom-call(s32[2]{0:T(128)S(1)} %pad_add_fusion.index_ref, bf16[128,6144]{1,0:T(8,128)(2,1)S(1)} %copy-done.1, bf16[3072,384]{1,0:T(8,128)(2,1)S(1)} %copy-done.2, f32[1,384]{1,0:T(1,128)S(1)} %broadcast_in_dim.13.start_ref), custom_call_target="tpu_custom_call" | custom-call | tf_op jit(solution)/shard_map/squeeze/pallas_call | solution.py:223
  11.6 2.2 %squeeze.44.refs_0_ = bf16[128,384]{1,0:T(8,128)(2,1)S(1)} custom-call(s32[2]{0:T(128)S(1)} %pad_add_fusion.index_ref, bf16[128,6144]{1,0:T(8,128)(2,1)S(1)} %copy-done.1, bf16[3072,384]{1,0:T(8,128)(2,1)} %collective-permute-done.weight_ref, f32[128,384]{1,0:T(8,128)S(1)} %squeeze.43.start_ref), custom_call_target="tpu_custom_call" | custom-call | tf_op jit(solution)/shard_map/squeeze/pallas_call | solution.py:223
  13.8 2.0 %collective-permute-done.1.refs_1_ = bf16[2,2,128,384]{3,2,1,0:T(8,128)(2,1)S(1)} collective-permute-done((bf16[2,2,128,384]{3,2,1,0:T(8,128)(2,1)S(1)}, bf16[2,2,128,384]{3,2,1,0:T(8,128)(2,1)S(1)}, u32[]{:S(2)}, u32[]{:S(2)}) %collective-permute-start.1) | collective-permute-done | bytes 393248 | tf_op jit(solution)/shard_map/ppermute | solution.py:372
  15.8 1.5 %collective-permute-done.2.refs_2_ = bf16[2,2,128,384]{3,2,1,0:T(8,128)(2,1)S(1)} collective-permute-done((bf16[2,2,128,384]{3,2,1,0:T(8,128)(2,1)S(1)}, bf16[2,2,128,384]{3,2,1,0:T(8,128)(2,1)S(1)}, u32[]{:S(2)}, u32[]{:S(2)}) %collective-permute-start.2) | collective-permute-done | bytes 393248 | tf_op jit(solution)/shard_map/ppermute | solution.py:372
  17.3 0.4 collective-permute-start.3
  17.7 2.7 %collective-permute-start.4 = (bf16[128,384]{1,0:T(8,128)(2,1)S(1)}, bf16[128,384]{1,0:T(8,128)(2,1)S(1)}, u32[]{:S(2)}, u32[]{:S(2)}) collective-permute-start(bf16[128,384]{1,0:T(8,128)(2,1)S(1)} %squeeze.44.refs_0_), channel_id=1, source_target_pairs={{0,6},{2,4},{4,2},{6,0},{8,14},{10,12},{12,10},{14,8},{1,7},{3,5},... | collective-permute-start | bytes 294920 | tf_op jit(solution)/shard_map/ppermute | solution.py:372
  20.3 0.8 collective-permute-start.5
  21.2 0.7 pad_maximum_fusion.vectors_ref
  21.9 0.4 collective-permute-done.3.refs_1_
  22.2 1.0 %collective-permute-done.4.refs_3_ = bf16[128,384]{1,0:T(8,128)(2,1)S(1)} collective-permute-done((bf16[128,384]{1,0:T(8,128)(2,1)S(1)}, bf16[128,384]{1,0:T(8,128)(2,1)S(1)}, u32[]{:S(2)}, u32[]{:S(2)}) %collective-permute-start.4) | collective-permute-done | bytes 98336 | tf_op jit(solution)/shard_map/ppermute | solution.py:372
  23.3 5.6 %collective-permute-start.7 = (bf16[2,2,128,384]{3,2,1,0:T(8,128)(2,1)S(1)}, bf16[2,2,128,384]{3,2,1,0:T(8,128)(2,1)S(1)}, u32[]{:S(2)}, u32[]{:S(2)}) collective-permute-start(bf16[2,2,128,384]{3,2,1,0:T(8,128)(2,1)S(1)} %get-tuple-element.82), channel_id=1, source_target_pairs={{0,6},{2,4},{4,2},{6,0},{8,14},{10,12},{12,10},{14,8},{1,7},{3,5},... | collective-permute-start | bytes 1179656 | tf_op jit(solution)/shard_map/ppermute | solution.py:372
  28.9 0.1 pad_add_fusion.2.index_ref
  29.0 0.1 collective-permute-start.24
  29.1 0.7 add_convert_fusion.conv_ref
  29.8 9.8 %lift.1 = (bf16[128,6144]{1,0:T(8,128)(2,1)}, bf16[2,2,128,384]{3,2,1,0:T(8,128)(2,1)}, bf16[2,2,128,384]{3,2,1,0:T(8,128)(2,1)}, bf16[2,2,128,384]{3,2,1,0:T(8,...) custom-call(s32[2]{0:T(128)} %copy-done.6, bf16[128,6144]{1,0:T(8,128)(2,1)} %frames_hbm.1, ...), custom_call_target="tpu_custom_call" | custom-call | tf_op jit(solution)/shard_map/lift/pallas_call | solution.py:155
  39.7 0.1 collective-permute-start.10
  39.8 0.1 pad_add_fusion.1.targets_ref
  39.8 3.5 %collective-permute-start.8 = (bf16[128,384]{1,0:T(8,128)(2,1)}, bf16[128,384]{1,0:T(8,128)(2,1)S(1)}, u32[]{:S(2)}, u32[]{:S(2)}) collective-permute-start(bf16[128,384]{1,0:T(8,128)(2,1)} %get-tuple-element.90.refs_0_.refs_12_), channel_id=1, source_target_pairs={{0,2},{2,0},{4,6},{6,4},{8,10},{10,8},{12,14},{14,12},{1,3},{3,1},... | collective-permute-start | bytes 294920 | tf_op jit(solution)/shard_map/ppermute | solution.py:372
  43.3 2.2 %collective-permute-done.10.refs_3_.refs_15_ = bf16[128,384]{1,0:T(8,128)(2,1)S(1)} collective-permute-done((bf16[128,384]{1,0:T(8,128)(2,1)}, bf16[128,384]{1,0:T(8,128)(2,1)S(1)}, u32[]{:S(2)}, u32[]{:S(2)}) %collective-permute-start.10) | collective-permute-done | bytes 98336 | tf_op jit(solution)/shard_map/ppermute | solution.py:372
  45.5 1.5 %collective-permute-start.25 = (bf16[128,384]{1,0:T(8,128)(2,1)S(1)}, bf16[128,384]{1,0:T(8,128)(2,1)S(1)}, u32[]{:S(2)}, u32[]{:S(2)}) collective-permute-start(bf16[128,384]{1,0:T(8,128)(2,1)S(1)} %select_select_fusion), channel_id=1, source_target_pairs={{0,8},{2,10},{4,12},{6,14},{8,0},{10,2},{12,4},{14,6},{1,9},{3,11}... | collective-permute-start | bytes 294920 | tf_op jit(solution)/shard_map/ppermute | solution.py:391
  47.0 2.0 %collective-permute-start.18 = (bf16[2,2,128,384]{3,2,1,0:T(8,128)(2,1)}, bf16[2,2,128,384]{3,2,1,0:T(8,128)(2,1)S(1)}, u32[]{:S(2)}, u32[]{:S(2)}) collective-permute-start(bf16[2,2,128,384]{3,2,1,0:T(8,128)(2,1)} %get-tuple-element.89), channel_id=1, source_target_pairs={{0,4},{2,6},{4,0},{6,2},{8,12},{10,14},{12,8},{14,10},{1,5},{3,7},... | collective-permute-start | bytes 1179656 | tf_op jit(solution)/shard_map/ppermute | solution.py:372
  49.0 1.6 %collective-permute-start.17 = (bf16[2,2,128,384]{3,2,1,0:T(8,128)(2,1)}, bf16[2,2,128,384]{3,2,1,0:T(8,128)(2,1)S(1)}, u32[]{:S(2)}, u32[]{:S(2)}) collective-permute-start(bf16[2,2,128,384]{3,2,1,0:T(8,128)(2,1)} %get-tuple-element.88), channel_id=1, source_target_pairs={{0,2},{2,0},{4,6},{6,4},{8,10},{10,8},{12,14},{14,12},{1,3},{3,1},... | collective-permute-start | bytes 1179656 | tf_op jit(solution)/shard_map/ppermute | solution.py:372
  50.6 1.8 %collective-permute-start.11 = (bf16[128,384]{1,0:T(8,128)(2,1)S(1)}, bf16[128,384]{1,0:T(8,128)(2,1)S(1)}, u32[]{:S(2)}, u32[]{:S(2)}) collective-permute-start(bf16[128,384]{1,0:T(8,128)(2,1)S(1)} %select_select_fusion.1), channel_id=1, source_target_pairs={{0,8},{2,10},{4,12},{6,14},{8,0},{10,2},{12,4},{14,6},{1,9},{3,11}... | collective-permute-start | bytes 294920 | tf_op jit(solution)/shard_map/ppermute | solution.py:391
  52.4 0.9 slice_bitcast_fusion.3
  53.5 0.1 collective-permute-start.13
  53.6 0.5 collective-permute-start.14
  54.1 5.6 %collective-permute-done.11.refs_4_.refs_5_ = bf16[128,384]{1,0:T(8,128)(2,1)S(1)} collective-permute-done((bf16[128,384]{1,0:T(8,128)(2,1)S(1)}, bf16[128,384]{1,0:T(8,128)(2,1)S(1)}, u32[]{:S(2)}, u32[]{:S(2)}) %collective-permute-start.11) | collective-permute-done | bytes 98336 | tf_op jit(solution)/shard_map/ppermute | solution.py:391
  59.7 3.2 %collective-permute-start.31 = (bf16[2,2,128,384]{3,2,1,0:T(8,128)(2,1)S(1)}, bf16[2,2,128,384]{3,2,1,0:T(8,128)(2,1)S(1)}, u32[]{:S(2)}, u32[]{:S(2)}) collective-permute-start(bf16[2,2,128,384]{3,2,1,0:T(8,128)(2,1)S(1)} %copy-done.9), channel_id=1, source_target_pairs={{0,6},{2,4},{4,2},{6,0},{8,14},{10,12},{12,10},{14,8},{1,7},{3,5},... | collective-permute-start | bytes 1179656 | tf_op jit(solution)/shard_map/ppermute | solution.py:372
  62.9 0.5 collective-permute-start.15
  63.5 1.0 collective-permute-done.15.refs_9_.refs_19_
  64.4 0.2 collective-permute-start.26
  64.7 0.3 collective-permute-start.20
  64.9 0.2 collective-permute-start.21
  65.2 0.3 collective-permute-start.22
  65.5 1.1 %mix_grad.1.rows_ref.grad_ref = bf16[2,4,128,384]{3,2,1,0:T(8,128)(2,1)S(1)} custom-call(s32[3]{0:T(128)S(1)} %pad_add_fusion.2.index_ref, f32[3,384]{1,0:T(4,128)S(1)} %copy-done.5, bf16[128,384]{1,0:T(8,128)(2,1)S(1)} %copy-done.3, bf16[128,384]{1,0:T(8,128)(2,1)S(1)} %collective-permute-done.8.refs_1_.refs_13_, ...), custom_call_target="tpu_custom_call" | custom-call | tf_op jit(solution)/shard_map/mix_grad/pallas_call | solution.py:288
  66.6 0.3 collective-permute-start.27
  66.9 0.3 collective-permute-start.28
  67.2 0.2 collective-permute-start.29
  67.4 2.5 %contract_down.1 = (f32[384,384]{1,0:T(8,128)S(1)}, f32[1,384]{1,0:T(1,128)}, bf16[384,384]{1,0:T(8,128)(2,1)S(1)}) custom-call(s32[2]{0:T(128)S(1)} %pad_add_fusion.1.targets_ref, bf16[2,4,128,384]{3,2,1,0:T(8,128)(2,1)S(1)} %mix_grad.1.rows_ref.grad_ref, bf16[2,2,128,384]{3,2,1,0:T(8,128)(2,1)S(1)} %get-tuple-element.103.refs_0_, ...), custom_call_target="tpu_custom_call" | custom-call | tf_op jit(solution)/shard_map/contract_down/pallas_call | solution.py:337
  69.9 0.3 collective-permute-start.30
  70.1 0.7 collective-permute-done.31.refs_3_
  70.8 2.7 %collective-permute-start.23 = (bf16[384,384]{1,0:T(8,128)(2,1)S(1)}, bf16[384,384]{1,0:T(8,128)(2,1)S(1)}, u32[]{:S(2)}, u32[]{:S(2)}) collective-permute-start(bf16[384,384]{1,0:T(8,128)(2,1)S(1)} %get-tuple-element.108), channel_id=1, source_target_pairs={{0,8},{2,10},{4,12},{6,14},{8,0},{10,2},{12,4},{14,6},{1,9},{3,11}... | collective-permute-start | bytes 884744 | tf_op jit(solution)/shard_map/ppermute | solution.py:391
  73.6 0.1 collective-permute-start.32
  73.7 0.5 collective-permute-start.33
  74.2 0.1 collective-permute-start.34
  74.3 0.4 collective-permute-start.35
  74.7 2.9 %mix_conv.1 = (bf16[2,4,128,384]{3,2,1,0:T(8,128)(2,1)S(1)}, f32[8,384]{1,0:T(8,128)S(1)}) custom-call(s32[3]{0:T(128)S(1)} %pad_add_fusion.2.index_ref, f32[3,384]{1,0:T(4,128)S(1)} %copy-done.5, bf16[2,4,128,384]{3,2,1,0:T(8,128)(2,1)S(1)} %mix_grad.1.rows_ref.grad_ref, bf16[128,384]{1,0:T(8,128)(2,1)S(1)} %squeeze.44.refs_0_, ...), custom_call_target="tpu_custom_call" | custom-call | tf_op jit(solution)/shard_map/mix_conv/pallas_call | solution.py:288
  77.7 2.0 %contract_up.1 = (f32[384,384]{1,0:T(8,128)S(1)}, f32[1,384]{1,0:T(1,128)S(1)}, bf16[400,384]{1,0:T(8,128)(2,1)S(1)}) custom-call(s32[2]{0:T(128)S(1)} %pad_add_fusion.1.targets_ref, bf16[2,4,128,384]{3,2,1,0:T(8,128)(2,1)S(1)} %get-tuple-element.116.rows_ref, f32[8,384]{1,0:T(8,128)S(1)} %get-tuple-element.117.small_ref, ...), custom_call_target="tpu_custom_call" | custom-call | tf_op jit(solution)/shard_map/contract_up/pallas_call | solution.py:337
  79.6 0.2 collective-permute-start.36
  79.9 13.7 %collective-permute-done.23 = bf16[384,384]{1,0:T(8,128)(2,1)S(1)} collective-permute-done((bf16[384,384]{1,0:T(8,128)(2,1)S(1)}, bf16[384,384]{1,0:T(8,128)(2,1)S(1)}, u32[]{:S(2)}, u32[]{:S(2)}) %collective-permute-start.23) | collective-permute-done | bytes 294944 | tf_op jit(solution)/shard_map/ppermute | solution.py:391
  93.6 0.9 convert_add_fusion
  94.5 5.2 %collective-permute-done.36 = bf16[400,384]{1,0:T(8,128)(2,1)S(1)} collective-permute-done((bf16[400,384]{1,0:T(8,128)(2,1)S(1)}, bf16[400,384]{1,0:T(8,128)(2,1)S(1)}, u32[]{:S(2)}, u32[]{:S(2)}) %collective-permute-start.36) | collective-permute-done | bytes 307232 | tf_op jit(solution)/shard_map/ppermute | solution.py:391
  99.7 0.6 slice.83
  100.3 0.6 slice_reduce_fusion
  100.9 0.9 slice_add_fusion
  (62 shorter events, 0.5 us)
Async XLA Ops:
  0.6 10.9 %collective-permute-start = (bf16[3072,384]{1,0:T(8,128)(2,1)}, bf16[3072,384]{1,0:T(8,128)(2,1)}, u32[]{:S(2)}, u32[]{:S(2)}) collective-permute-start(bf16[3072,384]{1,0:T(8,128)(2,1)} %weight_ref.1), channel_id=1, source_target_pairs={{0,1},{1,0},{2,3},{3,2},{4,5},{5,4},{6,7},{7,6},{8,9},{9,8},{10,11... | collective-permute-start | bytes 7077896 | tf_op jit(solution)/shard_map/ppermute | solution.py:369
  1.1 28.7 %collective-permute-start.6 = (bf16[3072,384]{1,0:T(8,128)(2,1)}, bf16[3072,384]{1,0:T(8,128)(2,1)}, u32[]{:S(2)}, u32[]{:S(2)}) collective-permute-start(bf16[3072,384]{1,0:T(8,128)(2,1)} %own_hbm.1), channel_id=1, source_target_pairs={{0,1},{1,0},{2,3},{3,2},{4,5},{5,4},{6,7},{7,6},{8,9},{9,8},{10,11... | collective-permute-start | bytes 7077896 | tf_op jit(solution)/shard_map/ppermute | solution.py:369
  1.3 1.4 %copy-start = (bf16[128,6144]{1,0:T(8,128)(2,1)S(1)}, bf16[128,6144]{1,0:T(8,128)(2,1)}, u32[]{:S(2)}) copy-start(bf16[128,6144]{1,0:T(8,128)(2,1)} %frames_hbm.1) | copy-start | bytes 4718596
  2.7 8.9 %copy-start.6 = (s32[2]{0:T(128)}, s32[2]{0:T(128)S(1)}, u32[]{:S(2)}) copy-start(s32[2]{0:T(128)S(1)} %pad_add_fusion.index_ref) | copy-start | bytes 28
  2.7 6.0 %copy-start.1 = (bf16[128,6144]{1,0:T(8,128)(2,1)S(1)}, bf16[128,6144]{1,0:T(8,128)(2,1)}, u32[]{:S(2)}) copy-start(bf16[128,6144]{1,0:T(8,128)(2,1)} %frames_hbm.1) | copy-start | bytes 4718596
  3.5 12.4 %collective-permute-start.1 = (bf16[2,2,128,384]{3,2,1,0:T(8,128)(2,1)S(1)}, bf16[2,2,128,384]{3,2,1,0:T(8,128)(2,1)S(1)}, u32[]{:S(2)}, u32[]{:S(2)}) collective-permute-start(bf16[2,2,128,384]{3,2,1,0:T(8,128)(2,1)S(1)} %get-tuple-element.73), channel_id=1, source_target_pairs={{0,2},{2,0},{4,6},{6,4},{8,10},{10,8},{12,14},{14,12},{1,3},{3,1},... | collective-permute-start | bytes 1179656 | tf_op jit(solution)/shard_map/ppermute | solution.py:372
  6.5 10.8 %collective-permute-start.2 = (bf16[2,2,128,384]{3,2,1,0:T(8,128)(2,1)S(1)}, bf16[2,2,128,384]{3,2,1,0:T(8,128)(2,1)S(1)}, u32[]{:S(2)}, u32[]{:S(2)}) collective-permute-start(bf16[2,2,128,384]{3,2,1,0:T(8,128)(2,1)S(1)} %get-tuple-element.74), channel_id=1, source_target_pairs={{0,4},{2,6},{4,0},{6,2},{8,12},{10,14},{12,8},{14,10},{1,5},{3,7},... | collective-permute-start | bytes 1179656 | tf_op jit(solution)/shard_map/ppermute | solution.py:372
  8.8 1.7 %copy-start.2 = (bf16[3072,384]{1,0:T(8,128)(2,1)S(1)}, bf16[3072,384]{1,0:T(8,128)(2,1)}, u32[]{:S(2)}) copy-start(bf16[3072,384]{1,0:T(8,128)(2,1)} %weight_ref.1) | copy-start | bytes 7077892
  11.5 9.7 %copy-start.7 = (f32[6144]{0:T(1024)S(1)}, f32[6144]{0:T(1024)}, u32[]{:S(2)}) copy-start(f32[6144]{0:T(1024)} %param.17) | copy-start | bytes 73732
  11.5 9.7 %copy-start.8 = (f32[6144]{0:T(1024)S(1)}, f32[6144]{0:T(1024)}, u32[]{:S(2)}) copy-start(f32[6144]{0:T(1024)} %param.16) | copy-start | bytes 73732
  11.6 17.4 %copy-start.5 = (f32[3,384]{1,0:T(4,128)S(1)}, f32[3,384]{1,0:T(4,128)}, u32[]{:S(2)}) copy-start(f32[3,384]{1,0:T(4,128)} %taps_ref.3) | copy-start | bytes 13828
  17.3 4.9 %collective-permute-start.3 = (bf16[128,384]{1,0:T(8,128)(2,1)S(1)}, bf16[128,384]{1,0:T(8,128)(2,1)S(1)}, u32[]{:S(2)}, u32[]{:S(2)}) collective-permute-start(bf16[128,384]{1,0:T(8,128)(2,1)S(1)} %squeeze.44.refs_0_), channel_id=1, source_target_pairs={{0,2},{2,0},{4,6},{6,4},{8,10},{10,8},{12,14},{14,12},{1,3},{3,1},... | collective-permute-start | bytes 294920 | tf_op jit(solution)/shard_map/ppermute | solution.py:372
  17.7 5.6 %collective-permute-start.4 = (bf16[128,384]{1,0:T(8,128)(2,1)S(1)}, bf16[128,384]{1,0:T(8,128)(2,1)S(1)}, u32[]{:S(2)}, u32[]{:S(2)}) collective-permute-start(bf16[128,384]{1,0:T(8,128)(2,1)S(1)} %squeeze.44.refs_0_), channel_id=1, source_target_pairs={{0,6},{2,4},{4,2},{6,0},{8,14},{10,12},{12,10},{14,8},{1,7},{3,5},... | collective-permute-start | bytes 294920 | tf_op jit(solution)/shard_map/ppermute | solution.py:372
  20.3 2.9 %collective-permute-start.5 = (bf16[128,384]{1,0:T(8,128)(2,1)S(1)}, bf16[128,384]{1,0:T(8,128)(2,1)S(1)}, u32[]{:S(2)}, u32[]{:S(2)}) collective-permute-start(bf16[128,384]{1,0:T(8,128)(2,1)S(1)} %squeeze.44.refs_0_), channel_id=1, source_target_pairs={{6,8},{8,6},{7,9},{9,7},{22,24},{24,22},{23,25},{25,23}} | collective-permute-start | bytes 294920 | tf_op jit(solution)/shard_map/ppermute | solution.py:386
  23.3 16.4 %collective-permute-start.7 = (bf16[2,2,128,384]{3,2,1,0:T(8,128)(2,1)S(1)}, bf16[2,2,128,384]{3,2,1,0:T(8,128)(2,1)S(1)}, u32[]{:S(2)}, u32[]{:S(2)}) collective-permute-start(bf16[2,2,128,384]{3,2,1,0:T(8,128)(2,1)S(1)} %get-tuple-element.82), channel_id=1, source_target_pairs={{0,6},{2,4},{4,2},{6,0},{8,14},{10,12},{12,10},{14,8},{1,7},{3,5},... | collective-permute-start | bytes 1179656 | tf_op jit(solution)/shard_map/ppermute | solution.py:372
  29.0 14.3 %collective-permute-start.24 = (bf16[128,384]{1,0:T(8,128)(2,1)S(1)}, bf16[128,384]{1,0:T(8,128)(2,1)S(1)}, u32[]{:S(2)}, u32[]{:S(2)}) collective-permute-start(bf16[128,384]{1,0:T(8,128)(2,1)S(1)} %squeeze.44.refs_0_), channel_id=1, source_target_pairs={{0,4},{2,6},{4,0},{6,2},{8,12},{10,14},{12,8},{14,10},{1,5},{3,7},... | collective-permute-start | bytes 294920 | tf_op jit(solution)/shard_map/ppermute | solution.py:372
  39.6 20.0 %copy-start.9 = (bf16[2,2,128,384]{3,2,1,0:T(8,128)(2,1)S(1)}, bf16[2,2,128,384]{3,2,1,0:T(8,128)(2,1)}, u32[]{:S(2)}) copy-start(bf16[2,2,128,384]{3,2,1,0:T(8,128)(2,1)} %get-tuple-element.119) | copy-start | bytes 1179652
  39.7 25.8 %copy-start.3 = (bf16[128,384]{1,0:T(8,128)(2,1)S(1)}, bf16[128,384]{1,0:T(8,128)(2,1)}, u32[]{:S(2)}) copy-start(bf16[128,384]{1,0:T(8,128)(2,1)} %get-tuple-element.90.refs_0_.refs_12_) | copy-start | bytes 294916
  39.7 5.8 %collective-permute-start.10 = (bf16[128,384]{1,0:T(8,128)(2,1)}, bf16[128,384]{1,0:T(8,128)(2,1)S(1)}, u32[]{:S(2)}, u32[]{:S(2)}) collective-permute-start(bf16[128,384]{1,0:T(8,128)(2,1)} %get-tuple-element.90.refs_0_.refs_12_), channel_id=1, source_target_pairs={{0,6},{2,4},{4,2},{6,0},{8,14},{10,12},{12,10},{14,8},{1,7},{3,5},... | collective-permute-start | bytes 294920 | tf_op jit(solution)/shard_map/ppermute | solution.py:372
  39.8 7.2 %collective-permute-start.8 = (bf16[128,384]{1,0:T(8,128)(2,1)}, bf16[128,384]{1,0:T(8,128)(2,1)S(1)}, u32[]{:S(2)}, u32[]{:S(2)}) collective-permute-start(bf16[128,384]{1,0:T(8,128)(2,1)} %get-tuple-element.90.refs_0_.refs_12_), channel_id=1, source_target_pairs={{0,2},{2,0},{4,6},{6,4},{8,10},{10,8},{12,14},{14,12},{1,3},{3,1},... | collective-permute-start | bytes 294920 | tf_op jit(solution)/shard_map/ppermute | solution.py:372
  43.3 7.3 %collective-permute-start.9 = (bf16[128,384]{1,0:T(8,128)(2,1)}, bf16[128,384]{1,0:T(8,128)(2,1)S(1)}, u32[]{:S(2)}, u32[]{:S(2)}) collective-permute-start(bf16[128,384]{1,0:T(8,128)(2,1)} %get-tuple-element.90.refs_0_.refs_12_), channel_id=1, source_target_pairs={{0,4},{2,6},{4,0},{6,2},{8,12},{10,14},{12,8},{14,10},{1,5},{3,7},... | collective-permute-start | bytes 294920 | tf_op jit(solution)/shard_map/ppermute | solution.py:372
  43.3 10.2 %collective-permute-start.12 = (bf16[128,384]{1,0:T(8,128)(2,1)}, bf16[128,384]{1,0:T(8,128)(2,1)S(1)}, u32[]{:S(2)}, u32[]{:S(2)}) collective-permute-start(bf16[128,384]{1,0:T(8,128)(2,1)} %get-tuple-element.90.refs_0_.refs_12_), channel_id=1, source_target_pairs={{0,1},{1,0},{2,3},{3,2},{4,5},{5,4},{6,7},{7,6},{8,9},{9,8},{10,11... | collective-permute-start | bytes 294920 | tf_op jit(solution)/shard_map/ppermute | solution.py:369
  45.5 8.0 %collective-permute-start.25 = (bf16[128,384]{1,0:T(8,128)(2,1)S(1)}, bf16[128,384]{1,0:T(8,128)(2,1)S(1)}, u32[]{:S(2)}, u32[]{:S(2)}) collective-permute-start(bf16[128,384]{1,0:T(8,128)(2,1)S(1)} %select_select_fusion), channel_id=1, source_target_pairs={{0,8},{2,10},{4,12},{6,14},{8,0},{10,2},{12,4},{14,6},{1,9},{3,11}... | collective-permute-start | bytes 294920 | tf_op jit(solution)/shard_map/ppermute | solution.py:391
  47.0 18.1 %collective-permute-start.18 = (bf16[2,2,128,384]{3,2,1,0:T(8,128)(2,1)}, bf16[2,2,128,384]{3,2,1,0:T(8,128)(2,1)S(1)}, u32[]{:S(2)}, u32[]{:S(2)}) collective-permute-start(bf16[2,2,128,384]{3,2,1,0:T(8,128)(2,1)} %get-tuple-element.89), channel_id=1, source_target_pairs={{0,4},{2,6},{4,0},{6,2},{8,12},{10,14},{12,8},{14,10},{1,5},{3,7},... | collective-permute-start | bytes 1179656 | tf_op jit(solution)/shard_map/ppermute | solution.py:372
  49.0 14.3 %collective-permute-start.17 = (bf16[2,2,128,384]{3,2,1,0:T(8,128)(2,1)}, bf16[2,2,128,384]{3,2,1,0:T(8,128)(2,1)S(1)}, u32[]{:S(2)}, u32[]{:S(2)}) collective-permute-start(bf16[2,2,128,384]{3,2,1,0:T(8,128)(2,1)} %get-tuple-element.88), channel_id=1, source_target_pairs={{0,2},{2,0},{4,6},{6,4},{8,10},{10,8},{12,14},{14,12},{1,3},{3,1},... | collective-permute-start | bytes 1179656 | tf_op jit(solution)/shard_map/ppermute | solution.py:372
  50.6 9.1 %collective-permute-start.11 = (bf16[128,384]{1,0:T(8,128)(2,1)S(1)}, bf16[128,384]{1,0:T(8,128)(2,1)S(1)}, u32[]{:S(2)}, u32[]{:S(2)}) collective-permute-start(bf16[128,384]{1,0:T(8,128)(2,1)S(1)} %select_select_fusion.1), channel_id=1, source_target_pairs={{0,8},{2,10},{4,12},{6,14},{8,0},{10,2},{12,4},{14,6},{1,9},{3,11}... | collective-permute-start | bytes 294920 | tf_op jit(solution)/shard_map/ppermute | solution.py:391
  53.5 9.3 %collective-permute-start.13 = (bf16[128,384]{1,0:T(8,128)(2,1)S(1)}, bf16[128,384]{1,0:T(8,128)(2,1)S(1)}, u32[]{:S(2)}, u32[]{:S(2)}) collective-permute-start(bf16[128,384]{1,0:T(8,128)(2,1)S(1)} %collective-permute-done.8.refs_1_.refs_13_), channel_id=1, source_target_pairs={{0,1},{1,0},{2,3},{3,2},{4,5},{5,4},{6,7},{7,6},{8,9},{9,8},{10,11... | collective-permute-start | bytes 294920 | tf_op jit(solution)/shard_map/ppermute | solution.py:369
  53.6 9.3 %collective-permute-start.14 = (bf16[128,384]{1,0:T(8,128)(2,1)S(1)}, bf16[128,384]{1,0:T(8,128)(2,1)S(1)}, u32[]{:S(2)}, u32[]{:S(2)}) collective-permute-start(bf16[128,384]{1,0:T(8,128)(2,1)S(1)} %collective-permute-done.9.refs_2_.refs_14_), channel_id=1, source_target_pairs={{0,1},{1,0},{2,3},{3,2},{4,5},{5,4},{6,7},{7,6},{8,9},{9,8},{10,11... | collective-permute-start | bytes 294920 | tf_op jit(solution)/shard_map/ppermute | solution.py:369
  59.7 11.1 %collective-permute-start.31 = (bf16[2,2,128,384]{3,2,1,0:T(8,128)(2,1)S(1)}, bf16[2,2,128,384]{3,2,1,0:T(8,128)(2,1)S(1)}, u32[]{:S(2)}, u32[]{:S(2)}) collective-permute-start(bf16[2,2,128,384]{3,2,1,0:T(8,128)(2,1)S(1)} %copy-done.9), channel_id=1, source_target_pairs={{0,6},{2,4},{4,2},{6,0},{8,14},{10,12},{12,10},{14,8},{1,7},{3,5},... | collective-permute-start | bytes 1179656 | tf_op jit(solution)/shard_map/ppermute | solution.py:372
  62.8 2.1 %collective-permute-start.19 = (bf16[2,128,384]{2,1,0:T(8,128)(2,1)S(1)}, bf16[2,128,384]{2,1,0:T(8,128)(2,1)S(1)}, u32[]{:S(2)}, u32[]{:S(2)}) collective-permute-start(bf16[2,128,384]{2,1,0:T(8,128)(2,1)S(1)} %slice_bitcast_fusion.7), channel_id=1, source_target_pairs={{0,1},{1,0},{2,3},{3,2},{4,5},{5,4},{6,7},{7,6},{8,9},{9,8},{10,11... | collective-permute-start | bytes 589832 | tf_op jit(solution)/shard_map/ppermute | solution.py:369
  62.9 1.6 %collective-permute-start.15 = (bf16[128,384]{1,0:T(8,128)(2,1)S(1)}, bf16[128,384]{1,0:T(8,128)(2,1)S(1)}, u32[]{:S(2)}, u32[]{:S(2)}) collective-permute-start(bf16[128,384]{1,0:T(8,128)(2,1)S(1)} %collective-permute-done.10.refs_3_.refs_15_), channel_id=1, source_target_pairs={{0,1},{1,0},{2,3},{3,2},{4,5},{5,4},{6,7},{7,6},{8,9},{9,8},{10,11... | collective-permute-start | bytes 294920 | tf_op jit(solution)/shard_map/ppermute | solution.py:369
  63.4 1.3 %collective-permute-start.16 = (bf16[128,384]{1,0:T(8,128)(2,1)S(1)}, bf16[128,384]{1,0:T(8,128)(2,1)S(1)}, u32[]{:S(2)}, u32[]{:S(2)}) collective-permute-start(bf16[128,384]{1,0:T(8,128)(2,1)S(1)} %collective-permute-done.11.refs_4_.refs_5_), channel_id=1, source_target_pairs={{0,1},{1,0},{2,3},{3,2},{4,5},{5,4},{6,7},{7,6},{8,9},{9,8},{10,11... | collective-permute-start | bytes 294920 | tf_op jit(solution)/shard_map/ppermute | solution.py:369
  64.4 5.4 %collective-permute-start.26 = (bf16[128,384]{1,0:T(8,128)(2,1)S(1)}, bf16[128,384]{1,0:T(8,128)(2,1)S(1)}, u32[]{:S(2)}, u32[]{:S(2)}) collective-permute-start(bf16[128,384]{1,0:T(8,128)(2,1)S(1)} %squeeze.44.refs_0_), channel_id=1, source_target_pairs={{0,1},{1,0},{2,3},{3,2},{4,5},{5,4},{6,7},{7,6},{8,9},{9,8},{10,11... | collective-permute-start | bytes 294920 | tf_op jit(solution)/shard_map/ppermute | solution.py:369
  64.7 1.9 %collective-permute-start.20 = (bf16[2,128,384]{2,1,0:T(8,128)(2,1)S(1)}, bf16[2,128,384]{2,1,0:T(8,128)(2,1)S(1)}, u32[]{:S(2)}, u32[]{:S(2)}) collective-permute-start(bf16[2,128,384]{2,1,0:T(8,128)(2,1)S(1)} %slice_bitcast_fusion.6), channel_id=1, source_target_pairs={{0,1},{1,0},{2,3},{3,2},{4,5},{5,4},{6,7},{7,6},{8,9},{9,8},{10,11... | collective-permute-start | bytes 589832 | tf_op jit(solution)/shard_map/ppermute | solution.py:369
  64.9 1.9 %collective-permute-start.21 = (bf16[2,128,384]{2,1,0:T(8,128)(2,1)S(1)}, bf16[2,128,384]{2,1,0:T(8,128)(2,1)S(1)}, u32[]{:S(2)}, u32[]{:S(2)}) collective-permute-start(bf16[2,128,384]{2,1,0:T(8,128)(2,1)S(1)} %slice_bitcast_fusion.5), channel_id=1, source_target_pairs={{0,1},{1,0},{2,3},{3,2},{4,5},{5,4},{6,7},{7,6},{8,9},{9,8},{10,11... | collective-permute-start | bytes 589832 | tf_op jit(solution)/shard_map/ppermute | solution.py:369
  65.2 2.0 %collective-permute-start.22 = (bf16[2,128,384]{2,1,0:T(8,128)(2,1)S(1)}, bf16[2,128,384]{2,1,0:T(8,128)(2,1)S(1)}, u32[]{:S(2)}, u32[]{:S(2)}) collective-permute-start(bf16[2,128,384]{2,1,0:T(8,128)(2,1)S(1)} %slice_bitcast_fusion.4), channel_id=1, source_target_pairs={{0,1},{1,0},{2,3},{3,2},{4,5},{5,4},{6,7},{7,6},{8,9},{9,8},{10,11... | collective-permute-start | bytes 589832 | tf_op jit(solution)/shard_map/ppermute | solution.py:369
  66.6 7.0 %collective-permute-start.27 = (bf16[128,384]{1,0:T(8,128)(2,1)S(1)}, bf16[128,384]{1,0:T(8,128)(2,1)S(1)}, u32[]{:S(2)}, u32[]{:S(2)}) collective-permute-start(bf16[128,384]{1,0:T(8,128)(2,1)S(1)} %collective-permute-done.3.refs_1_), channel_id=1, source_target_pairs={{0,1},{1,0},{2,3},{3,2},{4,5},{5,4},{6,7},{7,6},{8,9},{9,8},{10,11... | collective-permute-start | bytes 294920 | tf_op jit(solution)/shard_map/ppermute | solution.py:369
  66.9 6.8 %collective-permute-start.28 = (bf16[128,384]{1,0:T(8,128)(2,1)S(1)}, bf16[128,384]{1,0:T(8,128)(2,1)S(1)}, u32[]{:S(2)}, u32[]{:S(2)}) collective-permute-start(bf16[128,384]{1,0:T(8,128)(2,1)S(1)} %collective-permute-done.24.refs_2_), channel_id=1, source_target_pairs={{0,1},{1,0},{2,3},{3,2},{4,5},{5,4},{6,7},{7,6},{8,9},{9,8},{10,11... | collective-permute-start | bytes 294920 | tf_op jit(solution)/shard_map/ppermute | solution.py:369
  67.2 7.0 %collective-permute-start.29 = (bf16[128,384]{1,0:T(8,128)(2,1)S(1)}, bf16[128,384]{1,0:T(8,128)(2,1)S(1)}, u32[]{:S(2)}, u32[]{:S(2)}) collective-permute-start(bf16[128,384]{1,0:T(8,128)(2,1)S(1)} %collective-permute-done.4.refs_3_), channel_id=1, source_target_pairs={{0,1},{1,0},{2,3},{3,2},{4,5},{5,4},{6,7},{7,6},{8,9},{9,8},{10,11... | collective-permute-start | bytes 294920 | tf_op jit(solution)/shard_map/ppermute | solution.py:369
  69.9 7.8 %copy-start.4 = (bf16[2,2,128,384]{3,2,1,0:T(8,128)(2,1)S(1)}, bf16[2,2,128,384]{3,2,1,0:T(8,128)(2,1)}, u32[]{:S(2)}) copy-start(bf16[2,2,128,384]{3,2,1,0:T(8,128)(2,1)} %get-tuple-element.118.refs_0_) | copy-start | bytes 1179652
  69.9 4.4 %collective-permute-start.30 = (bf16[128,384]{1,0:T(8,128)(2,1)S(1)}, bf16[128,384]{1,0:T(8,128)(2,1)S(1)}, u32[]{:S(2)}, u32[]{:S(2)}) collective-permute-start(bf16[128,384]{1,0:T(8,128)(2,1)S(1)} %collective-permute-done.25.refs_4_.refs_5_), channel_id=1, source_target_pairs={{0,1},{1,0},{2,3},{3,2},{4,5},{5,4},{6,7},{7,6},{8,9},{9,8},{10,11... | collective-permute-start | bytes 294920 | tf_op jit(solution)/shard_map/ppermute | solution.py:369
  70.8 22.8 %collective-permute-start.23 = (bf16[384,384]{1,0:T(8,128)(2,1)S(1)}, bf16[384,384]{1,0:T(8,128)(2,1)S(1)}, u32[]{:S(2)}, u32[]{:S(2)}) collective-permute-start(bf16[384,384]{1,0:T(8,128)(2,1)S(1)} %get-tuple-element.108), channel_id=1, source_target_pairs={{0,8},{2,10},{4,12},{6,14},{8,0},{10,2},{12,4},{14,6},{1,9},{3,11}... | collective-permute-start | bytes 884744 | tf_op jit(solution)/shard_map/ppermute | solution.py:391
  73.6 4.0 %collective-permute-start.32 = (bf16[2,128,384]{2,1,0:T(8,128)(2,1)S(1)}, bf16[2,128,384]{2,1,0:T(8,128)(2,1)S(1)}, u32[]{:S(2)}, u32[]{:S(2)}) collective-permute-start(bf16[2,128,384]{2,1,0:T(8,128)(2,1)S(1)} %slice_bitcast_fusion.3), channel_id=1, source_target_pairs={{0,1},{1,0},{2,3},{3,2},{4,5},{5,4},{6,7},{7,6},{8,9},{9,8},{10,11... | collective-permute-start | bytes 589832 | tf_op jit(solution)/shard_map/ppermute | solution.py:369
  73.7 3.9 %collective-permute-start.33 = (bf16[2,128,384]{2,1,0:T(8,128)(2,1)S(1)}, bf16[2,128,384]{2,1,0:T(8,128)(2,1)S(1)}, u32[]{:S(2)}, u32[]{:S(2)}) collective-permute-start(bf16[2,128,384]{2,1,0:T(8,128)(2,1)S(1)} %slice_bitcast_fusion.2), channel_id=1, source_target_pairs={{0,1},{1,0},{2,3},{3,2},{4,5},{5,4},{6,7},{7,6},{8,9},{9,8},{10,11... | collective-permute-start | bytes 589832 | tf_op jit(solution)/shard_map/ppermute | solution.py:369
  74.2 3.5 %collective-permute-start.34 = (bf16[2,128,384]{2,1,0:T(8,128)(2,1)S(1)}, bf16[2,128,384]{2,1,0:T(8,128)(2,1)S(1)}, u32[]{:S(2)}, u32[]{:S(2)}) collective-permute-start(bf16[2,128,384]{2,1,0:T(8,128)(2,1)S(1)} %slice_bitcast_fusion.1), channel_id=1, source_target_pairs={{0,1},{1,0},{2,3},{3,2},{4,5},{5,4},{6,7},{7,6},{8,9},{9,8},{10,11... | collective-permute-start | bytes 589832 | tf_op jit(solution)/shard_map/ppermute | solution.py:369
  74.3 3.4 %collective-permute-start.35 = (bf16[2,128,384]{2,1,0:T(8,128)(2,1)S(1)}, bf16[2,128,384]{2,1,0:T(8,128)(2,1)S(1)}, u32[]{:S(2)}, u32[]{:S(2)}) collective-permute-start(bf16[2,128,384]{2,1,0:T(8,128)(2,1)S(1)} %slice_bitcast_fusion), channel_id=1, source_target_pairs={{0,1},{1,0},{2,3},{3,2},{4,5},{5,4},{6,7},{7,6},{8,9},{9,8},{10,11... | collective-permute-start | bytes 589832 | tf_op jit(solution)/shard_map/ppermute | solution.py:369
  79.6 20.0 %collective-permute-start.36 = (bf16[400,384]{1,0:T(8,128)(2,1)S(1)}, bf16[400,384]{1,0:T(8,128)(2,1)S(1)}, u32[]{:S(2)}, u32[]{:S(2)}) collective-permute-start(bf16[400,384]{1,0:T(8,128)(2,1)S(1)} %get-tuple-element.120), channel_id=1, source_target_pairs={{0,8},{2,10},{4,12},{6,14},{8,0},{10,2},{12,4},{14,6},{1,9},{3,11}... | collective-permute-start | bytes 921608 | tf_op jit(solution)/shard_map/ppermute | solution.py:391
